TPU v7x, 32 devices: a whole 2x2x4 slice. The times are simulated.
32 devices in a mesh: fsdp: 2 (over y), ctx: 4 (over x, core), tp: 4 (over z).
Axes of the slice: x: 2, y: 2, z: 4, core: 2. Of those that a mesh axis runs over, the one named last changes fastest.
Arguments:
- tokens: bfloat16 [2, 2048, 2048], P('fsdp', 'ctx'), may hold values from -6 to 6
- q_weight: bfloat16 [2048, 2048], P(('fsdp', 'ctx'), 'tp'), may hold values from -0.125 to 0.125
- k_weight: bfloat16 [2048, 2048], P(('fsdp', 'ctx'), 'tp'), may hold values from -0.125 to 0.125
- v_weight: bfloat16 [2048, 2048], P(('fsdp', 'ctx'), 'tp'), may hold values from -0.125 to 0.125
- o_weight: bfloat16 [2048, 2048], P(('fsdp', 'ctx'), 'tp'), may hold values from -0.125 to 0.125
- gate_weight: bfloat16 [2048, 8192], P(('fsdp', 'ctx'), 'tp'), may hold values from -0.125 to 0.125
- up_weight: bfloat16 [2048, 8192], P(('fsdp', 'ctx'), 'tp'), may hold values from -0.125 to 0.125
- down_weight: bfloat16 [2048, 8192], P(('fsdp', 'ctx'), 'tp'), may hold values from -0.0625 to 0.0625
- norm_gains: bfloat16 [2048, 4], P(('fsdp', 'ctx')), may hold values from 0.5 to 2
- cotangent: bfloat16 [2, 2048, 2048], P('fsdp', 'ctx'), may hold values from -6 to 6
Outputs:
- block_out: bfloat16 [2, 2048, 2048], P('fsdp', 'ctx')
- token_grad: float32 [2, 2048, 2048], P('fsdp', 'ctx')
- q_grad: float32 [2048, 2048], P(('fsdp', 'ctx'), 'tp')
- k_grad: float32 [2048, 2048], P(('fsdp', 'ctx'), 'tp')
- v_grad: float32 [2048, 2048], P(('fsdp', 'ctx'), 'tp')
- o_grad: float32 [2048, 2048], P(('fsdp', 'ctx'), 'tp')
- gate_grad: float32 [2048, 8192], P(('fsdp', 'ctx'), 'tp')
- up_grad: float32 [2048, 8192], P(('fsdp', 'ctx'), 'tp')
- down_grad: float32 [2048, 8192], P(('fsdp', 'ctx'), 'tp')
- gain_grad: float32 [2048, 4], P(('fsdp', 'ctx'))
All inputs are finite; a program needn't handle non-finite values.
Results may differ from a plain program's by a relative error of at most 0.017.
Values may be sent and summed in bfloat16 or wider, within the bound.
No kernel may reach another device: no remote copies, remote signals or barrier semaphores. Data moves between devices by JAX's collectives and lax.ppermute only.
A program may use at most 192 MiB of HBM per device.

v0:
```python
import math

import jax
import jax.numpy as jnp
from jax import lax
from jax.sharding import PartitionSpec as P

HEAD_DIM = 128


norm_eps = 1e-06
rope_base = 500000.0


def rms_scale(values_in):
    return lax.rsqrt(jnp.mean(values_in * values_in, axis=-1, keepdims=True) + norm_eps)


def rope_tables(length, offset):
    half_dim = HEAD_DIM // 2
    frequency = rope_base ** (-(jnp.arange(half_dim, dtype=jnp.float32) * 2.0) / HEAD_DIM)
    angles = (offset + jnp.arange(length, dtype=jnp.int32)).astype(jnp.float32)[
        :, None
    ] * frequency[None, :]
    return (jnp.cos(angles), jnp.sin(angles))


def rotate(values_in, cosine_table, sine_table):
    half_dim = values_in.shape[-1] // 2
    first_half = values_in[..., :half_dim]
    second_half = values_in[..., half_dim:]
    cosine = cosine_table[:, None, :]
    sine_part = sine_table[:, None, :]
    return jnp.concatenate(
        [
            first_half * cosine - second_half * sine_part,
            second_half * cosine + first_half * sine_part,
        ],
        axis=-1,
    )


def unrotate(grad_in, cosine_table, sine_table):
    half_dim = grad_in.shape[-1] // 2
    first_half = grad_in[..., :half_dim]
    second_half = grad_in[..., half_dim:]
    cosine = cosine_table[:, None, :]
    sine_part = sine_table[:, None, :]
    return jnp.concatenate(
        [
            first_half * cosine + second_half * sine_part,
            second_half * cosine - first_half * sine_part,
        ],
        axis=-1,
    )


def contract_rows(left, right):
    return lax.dot_general(
        left, right, (((0,), (0,)), ((), ())), preferred_element_type=jnp.float32
    )


def contract_cols(left, right):
    return lax.dot_general(
        left, right, (((1,), (1,)), ((), ())), preferred_element_type=jnp.float32
    )


def norm_backward(grad_in, values_in, scale_rows, gain_vec, dot_rows, model_width):
    cubed = scale_rows * scale_rows * scale_rows
    return scale_rows * (grad_in * gain_vec) - values_in * (cubed / model_width) * dot_rows


def per_device(
    tokens,
    q_weight,
    k_weight,
    v_weight,
    o_weight,
    gate_weight,
    up_weight,
    down_weight,
    norm_gains,
    cotangent,
):
    seq_count, seq_span, model_width = tokens.shape
    row_count = seq_count * seq_span
    tensor = lax.axis_size("tp")
    local_width = model_width // tensor
    heads_here = local_width // HEAD_DIM
    feature_start = lax.axis_index("tp") * local_width
    position = lax.axis_index("ctx") * seq_span
    score_scale = 1.0 / math.sqrt(HEAD_DIM)
    gathered = (
        lax.all_gather(q_weight, ("fsdp", "ctx"), axis=0, tiled=True),
        lax.all_gather(k_weight, ("fsdp", "ctx"), axis=0, tiled=True),
        lax.all_gather(v_weight, ("fsdp", "ctx"), axis=0, tiled=True),
        lax.all_gather(o_weight, ("fsdp", "ctx"), axis=0, tiled=True),
        lax.all_gather(gate_weight, ("fsdp", "ctx"), axis=0, tiled=True),
        lax.all_gather(up_weight, ("fsdp", "ctx"), axis=0, tiled=True),
        lax.all_gather(down_weight, ("fsdp", "ctx"), axis=0, tiled=True),
        lax.all_gather(norm_gains, ("fsdp", "ctx"), axis=0, tiled=True),
    )
    w_query, w_key, w_value, w_out, w_gate, w_up, w_down, gain_all = gathered
    gain_table = gain_all.astype(jnp.float32)
    gain_q = lax.dynamic_slice_in_dim(gain_table[:, 0], feature_start, local_width)
    gain_k = lax.dynamic_slice_in_dim(gain_table[:, 1], feature_start, local_width)
    gain_attn = gain_table[:, 2]
    gain_ffn = gain_table[:, 3]
    inputs = tokens.reshape(row_count, model_width)
    q_proj = jnp.dot(inputs, w_query, preferred_element_type=jnp.float32)
    k_proj = jnp.dot(inputs, w_key, preferred_element_type=jnp.float32)
    v_proj = jnp.dot(inputs, w_value, preferred_element_type=jnp.float32)
    q_squares, k_squares = lax.psum(
        (jnp.sum(q_proj * q_proj, axis=1), jnp.sum(k_proj * k_proj, axis=1)), "tp"
    )
    q_rs = lax.rsqrt(q_squares / model_width + norm_eps)[:, None]
    k_rs = lax.rsqrt(k_squares / model_width + norm_eps)[:, None]
    cosine_table, sine_table = rope_tables(seq_span, position)
    q_shape = (seq_count, seq_span, heads_here, HEAD_DIM)
    q_rot = rotate((q_proj * q_rs * gain_q).reshape(q_shape), cosine_table, sine_table).astype(
        jnp.bfloat16
    )
    k_rot = rotate((k_proj * k_rs * gain_k).reshape(q_shape), cosine_table, sine_table).astype(
        jnp.bfloat16
    )
    v_low = v_proj.astype(jnp.bfloat16).reshape(q_shape)
    k_all, v_all = (
        lax.all_gather(k_rot, "ctx", axis=1, tiled=True),
        lax.all_gather(v_low, "ctx", axis=1, tiled=True),
    )
    length = k_all.shape[1]
    allowed = (
        jnp.arange(length, dtype=jnp.int32)[None, :]
        <= (position + jnp.arange(seq_span, dtype=jnp.int32))[:, None]
    )

    def masked_scores(q_seq, k_seq):
        scores = (
            jnp.einsum("qhd,khd->hqk", q_seq, k_seq, preferred_element_type=jnp.float32)
            * score_scale
        )
        return jnp.where(allowed[None], scores, -1e30)

    def forward_seq(packed):
        q_seq, k_seq, v_seq = packed
        scores = masked_scores(q_seq, k_seq)
        row_max = jnp.max(scores, axis=-1, keepdims=True)
        weights = jnp.exp(scores - row_max)
        row_total = jnp.sum(weights, axis=-1, keepdims=True)
        probs_low = (weights / row_total).astype(jnp.bfloat16)
        attended = jnp.einsum("hqk,khd->qhd", probs_low, v_seq, preferred_element_type=jnp.float32)
        return (attended, row_max + jnp.log(row_total))

    attended, log_total = lax.map(forward_seq, (q_rot, k_all, v_all))
    att_low = attended.reshape(row_count, local_width).astype(jnp.bfloat16)
    branch_a = lax.psum(contract_cols(att_low, w_out), "tp")
    a_rs = rms_scale(branch_a)
    middle = inputs.astype(jnp.float32) + branch_a * a_rs * gain_attn
    middle_low = middle.astype(jnp.bfloat16)
    gate_proj = jnp.dot(middle_low, w_gate, preferred_element_type=jnp.float32)
    up_proj = jnp.dot(middle_low, w_up, preferred_element_type=jnp.float32)
    activated = (jax.nn.silu(gate_proj) * up_proj).astype(jnp.bfloat16)
    branch_f = lax.psum(contract_cols(activated, w_down), "tp")
    f_rs = rms_scale(branch_f)
    block_out = (
        (middle + branch_f * f_rs * gain_ffn)
        .astype(jnp.bfloat16)
        .reshape(seq_count, seq_span, model_width)
    )
    grad_out = cotangent.reshape(row_count, model_width).astype(jnp.float32)
    ffn_gain_part = jnp.sum(grad_out * branch_f * f_rs, axis=0)
    ffn_dot = jnp.sum(grad_out * gain_ffn * branch_f, axis=1, keepdims=True)
    d_branch_f = norm_backward(grad_out, branch_f, f_rs, gain_ffn, ffn_dot, model_width).astype(
        jnp.bfloat16
    )
    down_part = contract_rows(d_branch_f, activated)
    d_act = jnp.dot(d_branch_f, w_down, preferred_element_type=jnp.float32)
    sigmoid_gate = jax.nn.sigmoid(gate_proj)
    d_gate = (d_act * up_proj * sigmoid_gate * (1.0 + gate_proj * (1.0 - sigmoid_gate))).astype(
        jnp.bfloat16
    )
    d_up = (d_act * gate_proj * sigmoid_gate).astype(jnp.bfloat16)
    gate_part = contract_rows(middle_low, d_gate)
    up_part = contract_rows(middle_low, d_up)
    d_middle = grad_out + lax.psum(contract_cols(d_gate, w_gate) + contract_cols(d_up, w_up), "tp")
    attn_gain_part = jnp.sum(d_middle * branch_a * a_rs, axis=0)
    attn_dot = jnp.sum(d_middle * gain_attn * branch_a, axis=1, keepdims=True)
    d_branch_a = norm_backward(d_middle, branch_a, a_rs, gain_attn, attn_dot, model_width).astype(
        jnp.bfloat16
    )
    out_part = contract_rows(d_branch_a, att_low)
    d_att = (
        jnp.dot(d_branch_a, w_out, preferred_element_type=jnp.float32)
        .astype(jnp.bfloat16)
        .reshape(q_shape)
    )

    def backward_seq(packed):
        q_seq, k_seq, v_seq, total_seq, grad_seq = packed
        probs = jnp.exp(masked_scores(q_seq, k_seq) - total_seq)
        d_probs = jnp.einsum("qhd,khd->hqk", grad_seq, v_seq, preferred_element_type=jnp.float32)
        d_values = jnp.einsum(
            "hqk,qhd->khd", probs.astype(jnp.bfloat16), grad_seq, preferred_element_type=jnp.float32
        )
        row_delta = jnp.sum(d_probs * probs, axis=-1, keepdims=True)
        d_scores = (probs * (d_probs - row_delta)).astype(jnp.bfloat16)
        d_query = (
            jnp.einsum("hqk,khd->qhd", d_scores, k_seq, preferred_element_type=jnp.float32)
            * score_scale
        )
        d_keys = (
            jnp.einsum("hqk,qhd->khd", d_scores, q_seq, preferred_element_type=jnp.float32)
            * score_scale
        )
        return (d_query, d_keys, d_values)

    d_q_rot, d_k_full, d_v_full = lax.map(backward_seq, (q_rot, k_all, v_all, log_total, d_att))
    d_k_rot, d_v_own = (
        lax.psum_scatter(d_k_full, "ctx", scatter_dimension=1, tiled=True),
        lax.psum_scatter(d_v_full, "ctx", scatter_dimension=1, tiled=True),
    )
    d_value = d_v_own.reshape(row_count, local_width).astype(jnp.bfloat16)
    d_q_norm = unrotate(d_q_rot, cosine_table, sine_table).reshape(row_count, local_width)
    d_k_norm = unrotate(d_k_rot, cosine_table, sine_table).reshape(row_count, local_width)
    query_gain_part = jnp.sum(d_q_norm * q_proj * q_rs, axis=0)
    key_gain_part = jnp.sum(d_k_norm * k_proj * k_rs, axis=0)
    pre_gains = lax.dynamic_update_slice(
        jnp.zeros((model_width, 2), jnp.float32),
        jnp.stack([query_gain_part, key_gain_part], axis=1),
        (feature_start, 0),
    )
    is_first = lax.axis_index("tp") == 0
    post_gains = jnp.where(is_first, jnp.stack([attn_gain_part, ffn_gain_part], axis=1), 0.0)
    gain_part = jnp.concatenate([pre_gains, post_gains], axis=1)
    query_dot, key_dot, gain_sum = lax.psum(
        (
            jnp.sum(d_q_norm * gain_q * q_proj, axis=1),
            jnp.sum(d_k_norm * gain_k * k_proj, axis=1),
            gain_part,
        ),
        "tp",
    )
    d_query = norm_backward(d_q_norm, q_proj, q_rs, gain_q, query_dot[:, None], model_width).astype(
        jnp.bfloat16
    )
    d_key = norm_backward(d_k_norm, k_proj, k_rs, gain_k, key_dot[:, None], model_width).astype(
        jnp.bfloat16
    )
    query_part = contract_rows(inputs, d_query)
    key_part = contract_rows(inputs, d_key)
    value_part = contract_rows(inputs, d_value)
    input_part = (
        contract_cols(d_query, w_query)
        + contract_cols(d_key, w_key)
        + contract_cols(d_value, w_value)
    )
    token_grad = (d_middle + lax.psum(input_part, "tp")).reshape(seq_count, seq_span, model_width)
    owned_grads = (
        lax.psum_scatter(query_part, ("fsdp", "ctx"), scatter_dimension=0, tiled=True),
        lax.psum_scatter(key_part, ("fsdp", "ctx"), scatter_dimension=0, tiled=True),
        lax.psum_scatter(value_part, ("fsdp", "ctx"), scatter_dimension=0, tiled=True),
        lax.psum_scatter(out_part, ("fsdp", "ctx"), scatter_dimension=0, tiled=True),
        lax.psum_scatter(gate_part, ("fsdp", "ctx"), scatter_dimension=0, tiled=True),
        lax.psum_scatter(up_part, ("fsdp", "ctx"), scatter_dimension=0, tiled=True),
        lax.psum_scatter(down_part, ("fsdp", "ctx"), scatter_dimension=0, tiled=True),
        lax.psum_scatter(gain_sum, ("fsdp", "ctx"), scatter_dimension=0, tiled=True),
    )
    return (
        block_out,
        token_grad,
        owned_grads[0],
        owned_grads[1],
        owned_grads[2],
        owned_grads[3],
        owned_grads[4],
        owned_grads[5],
        owned_grads[6],
        owned_grads[7],
    )


def solution(mesh):
    return jax.shard_map(
        per_device,
        mesh=mesh,
        in_specs=(
            P("fsdp", "ctx", None),
            P(("fsdp", "ctx"), "tp"),
            P(("fsdp", "ctx"), "tp"),
            P(("fsdp", "ctx"), "tp"),
            P(("fsdp", "ctx"), "tp"),
            P(("fsdp", "ctx"), "tp"),
            P(("fsdp", "ctx"), "tp"),
            P(("fsdp", "ctx"), "tp"),
            P(("fsdp", "ctx"), None),
            P("fsdp", "ctx", None),
        ),
        out_specs=(
            P("fsdp", "ctx", None),
            P("fsdp", "ctx", None),
            P(("fsdp", "ctx"), "tp"),
            P(("fsdp", "ctx"), "tp"),
            P(("fsdp", "ctx"), "tp"),
            P(("fsdp", "ctx"), "tp"),
            P(("fsdp", "ctx"), "tp"),
            P(("fsdp", "ctx"), "tp"),
            P(("fsdp", "ctx"), "tp"),
            P(("fsdp", "ctx"), None),
        ),
        check_vma=False,
    )
```

profile of v0, /device:TPU:0, one launch (start us, length us, event | category | flops | bytes accessed | tf_op | source)
XLA Modules:
  0.0 1794.4 jit_solution(4205277640615246279)
XLA Ops:
  9.5 10.5 all_gather.33
  21.9 18.5 %all-gather.14.cloned.1.call-done = bf16[2048,512]{1,0:T(8,128)(2,1)} async-done(((bf16[256,512]{1,0:T(8,128)(2,1)}), bf16[2048,512]{1,0:T(8,128)(2,1)}) %all-gather.14.cloned.1.call-update) | async-done | bytes 2097168 | tf_op jit(solution)/shard_map/all_gather | solution.py:96
  40.4 4.5 multiply_reduce_fusion.8
  44.9 25.2 %all-gather.16.cloned.1.call-done = bf16[2048,512]{1,0:T(8,128)(2,1)} async-done(((bf16[256,512]{1,0:T(8,128)(2,1)}), bf16[2048,512]{1,0:T(8,128)(2,1)}) %all-gather.16.cloned.1.call-update) | async-done | bytes 2097168 | tf_op jit(solution)/shard_map/all_gather | solution.py:97
  70.1 2.9 multiply_reduce_fusion.7
  73.0 11.7 all-reduce.1
  87.7 2.4 copy.59
  90.1 2.4 copy.58
  93.7 2.4 copy.60
  96.1 2.4 copy.61
  98.5 3.5 fusion.49
  103.1 3.7 fusion.39
  108.3 16.1 all-gather.18.cloned.1.call-done
  124.4 11.9 fusion.65
  136.3 8.2 fusion
  144.5 4.5 all-gather.12.cloned.1.call-done
  149.0 8.1 fusion.42
  157.1 21.4 %all-gather.20.cloned.1.call-done = bf16[2048,512]{1,0:T(8,128)(2,1)} async-done(((bf16[256,512]{1,0:T(8,128)(2,1)}), bf16[2048,512]{1,0:T(8,128)(2,1)}) %all-gather.20.cloned.1.call-update) | async-done | bytes 2097168 | tf_op jit(solution)/shard_map/all_gather | solution.py:99
  178.5 4.9 fusion.66
  185.8 152.8 %all-reduce.7.cloned.1.call-done = f32[512,2048]{1,0:T(8,128)} async-done(((f32[512,2048]{1,0:T(8,128)}), f32[512,2048]{1,0:T(8,128)}) %all-reduce.7.cloned.1.call-update) | async-done | bytes 4194320 | tf_op jit(solution)/shard_map/psum | solution.py:158
  338.6 2.7 multiply_reduce_fusion.4
  344.1 49.6 %all-gather.22.cloned.1.call-done = bf16[2048,2048]{1,0:T(8,128)(2,1)} async-done(((bf16[256,2048]{1,0:T(8,128)(2,1)}), bf16[2048,2048]{1,0:T(8,128)(2,1)}) %all-gather.22.cloned.1.call-update) | async-done | bytes 8388624 | tf_op jit(solution)/shard_map/all_gather | solution.py:100
  393.7 10.5 fusion.67
  404.3 45.7 %all-gather.24.cloned.1.call-done = bf16[2048,2048]{1,0:T(8,128)(2,1)} async-done(((bf16[256,2048]{1,0:T(8,128)(2,1)}), bf16[2048,2048]{1,0:T(8,128)(2,1)}) %all-gather.24.cloned.1.call-update) | async-done | bytes 8388624 | tf_op jit(solution)/shard_map/all_gather | solution.py:101
  449.9 12.5 multiply_convert_fusion.3
  462.4 43.5 %all-gather.26.cloned.1.call-done = bf16[2048,2048]{1,0:T(8,128)(2,1)} async-done(((bf16[256,2048]{1,0:T(8,128)(2,1)}), bf16[2048,2048]{1,0:T(8,128)(2,1)}) %all-gather.26.cloned.1.call-update) | async-done | bytes 8388624 | tf_op jit(solution)/shard_map/all_gather | solution.py:102
  505.9 10.6 fusion.68
  517.0 154.7 %all-reduce.9.cloned.1.call-done = f32[512,2048]{1,0:T(8,128)} async-done(((f32[512,2048]{1,0:T(8,128)}), f32[512,2048]{1,0:T(8,128)}) %all-reduce.9.cloned.1.call-update) | async-done | bytes 4194320 | tf_op jit(solution)/shard_map/psum | solution.py:165
  671.7 2.7 multiply_reduce_fusion.3
  675.1 3.1 fusion.12
  678.3 11.1 multiply_convert_fusion.1
  689.4 6.1 fusion.69
  695.5 10.1 convolution_add_fusion
  705.9 153.9 %all-reduce.11.cloned.1.call-done = f32[512,2048]{1,0:T(8,128)} async-done(((f32[512,2048]{1,0:T(8,128)}), f32[512,2048]{1,0:T(8,128)}) %all-reduce.11.cloned.1.call-update) | async-done | bytes 4194320 | tf_op jit(solution)/shard_map/psum | solution.py:187
  859.7 5.5 multiply_reduce_fusion.1
  866.9 5.3 subtract_convert_fusion
  876.2 9.6 multiply_reduce_fusion
  885.9 10.3 multiply_convert_fusion
  896.2 8.6 multiply_bitcast_fusion
  905.1 11.5 fusion.13
  918.2 5.7 fusion.36
  924.0 24.4 %reduce-scatter.13.cloned.1.call-done = f32[1,512,4,128]{3,1,2,0:T(8,128)} async-done(((f32[1,2048,4,128]{3,1,2,0:T(8,128)}), f32[1,512,4,128]{3,1,2,0:T(8,128)}) %reduce-scatter.13.cloned.1.call-update) | async-done | bytes 1048592 | tf_op jit(solution)/shard_map/reduce_scatter | solution.py:221
  948.4 3.6 multiply_add_fusion.1
  953.7 2.6 pad_maximum_fusion.1
  961.7 33.6 %reduce-scatter.15.cloned.1.call-done = f32[1,512,4,128]{1,3,2,0:T(8,128)} async-done(((f32[1,2048,4,128]{1,3,2,0:T(8,128)}), f32[1,512,4,128]{1,3,2,0:T(8,128)}) %reduce-scatter.15.cloned.1.call-update) | async-done | bytes 1048592 | tf_op jit(solution)/shard_map/reduce_scatter | solution.py:222
  997.3 37.5 %reduce-scatter.31.cloned.1.call-done = f32[256,4]{1,0:T(8,128)} async-done(((f32[2048,4]{1,0:T(8,128)}), f32[256,4]{1,0:T(8,128)}) %reduce-scatter.31.cloned.1.call-update) | async-done | bytes 4112
  1035.8 12.4 all-reduce
  1053.7 3.4 add_add_fusion
  1058.7 3.2 convolution_bitcast_fusion
  1062.0 3.2 convolution_bitcast_fusion.2
  1065.3 3.3 convolution_bitcast_fusion.1
  1070.2 3.4 fusion.72
  1075.2 9.8 fusion.73
  1085.1 9.8 fusion.74
  1096.5 13.6 fusion.58
  1110.2 99.3 %all-reduce.13.cloned.1.call-done = f32[512,2048]{1,0:T(8,128)} async-done(((f32[512,2048]{1,0:T(8,128)}), f32[512,2048]{1,0:T(8,128)}) %all-reduce.13.cloned.1.call-update) | async-done | bytes 4194320 | tf_op jit(solution)/shard_map/psum | solution.py:259
  1209.5 7.0 add_bitcast_fusion
  1216.5 46.3 %reduce-scatter.21.cloned.1.call-done = f32[256,512]{0,1:T(8,128)} async-done(((f32[2048,512]{0,1:T(8,128)}), f32[256,512]{0,1:T(8,128)}) %reduce-scatter.21.cloned.1.call-update) | async-done | bytes 524304 | tf_op jit(solution)/shard_map/reduce_scatter | solution.py:263
  1264.8 52.3 %reduce-scatter.17.cloned.1.call-done = f32[256,512]{0,1:T(8,128)} async-done(((f32[2048,512]{0,1:T(8,128)}), f32[256,512]{0,1:T(8,128)}) %reduce-scatter.17.cloned.1.call-update) | async-done | bytes 524304 | tf_op jit(solution)/shard_map/reduce_scatter | solution.py:261
  1319.1 52.4 %reduce-scatter.19.cloned.1.call-done = f32[256,512]{0,1:T(8,128)} async-done(((f32[2048,512]{0,1:T(8,128)}), f32[256,512]{0,1:T(8,128)}) %reduce-scatter.19.cloned.1.call-update) | async-done | bytes 524304 | tf_op jit(solution)/shard_map/reduce_scatter | solution.py:262
  1373.6 52.9 %reduce-scatter.23.cloned.1.call-done = f32[256,512]{1,0:T(8,128)} async-done(((f32[2048,512]{1,0:T(8,128)}), f32[256,512]{1,0:T(8,128)}) %reduce-scatter.23.cloned.1.call-update) | async-done | bytes 524304 | tf_op jit(solution)/shard_map/reduce_scatter | solution.py:264
  1426.6 120.4 %reduce-scatter.25.cloned.1.call-done = f32[256,2048]{1,0:T(8,128)} async-done(((f32[2048,2048]{1,0:T(8,128)}), f32[256,2048]{1,0:T(8,128)}) %reduce-scatter.25.cloned.1.call-update) | async-done | bytes 2097168 | tf_op jit(solution)/shard_map/reduce_scatter | solution.py:265
  1546.9 120.4 %reduce-scatter.27.cloned.1.call-done = f32[256,2048]{1,0:T(8,128)} async-done(((f32[2048,2048]{1,0:T(8,128)}), f32[256,2048]{1,0:T(8,128)}) %reduce-scatter.27.cloned.1.call-update) | async-done | bytes 2097168 | tf_op jit(solution)/shard_map/reduce_scatter | solution.py:266
  1667.3 120.4 %reduce-scatter.29.cloned.1.call-done = f32[256,2048]{1,0:T(8,128)} async-done(((f32[2048,2048]{1,0:T(8,128)}), f32[256,2048]{1,0:T(8,128)}) %reduce-scatter.29.cloned.1.call-update) | async-done | bytes 2097168 | tf_op jit(solution)/shard_map/reduce_scatter | solution.py:267
  (189 shorter events, 52.9 us)
Async XLA Ops:
  7.2 33.2 %all-gather.14.cloned.1.call-start = ((), (), s32[]{:S(2)}) async-start(), calls=%async_computation.12 | async-start | bytes 2359296 | tf_op jit(solution)/shard_map/all_gather | solution.py:96
  7.9 62.2 %all-gather.16.cloned.1.call-start = ((), (), s32[]{:S(2)}) async-start(), calls=%async_computation.13 | async-start | bytes 2359296 | tf_op jit(solution)/shard_map/all_gather | solution.py:97
  8.7 94.5 %all-gather.10.cloned.1.call-start = ((), (), s32[]{:S(2)}) async-start(), calls=%async_computation.10 | async-start | bytes 2359296 | tf_op jit(solution)/shard_map/all_gather | solution.py:98
  9.4 115.0 %all-gather.18.cloned.1.call-start = ((), (), s32[]{:S(2)}) async-start(), calls=%async_computation.14 | async-start | bytes 2621440 | tf_op jit(solution)/shard_map/all_gather | solution.py:130
  20.1 65.3 %copy-start.35 = (f32[512,1]{0,1:T(1,128)}, f32[512,1]{0,1:T(1,128)S(1)}, u32[]{:S(2)}) copy-start(f32[512,1]{0,1:T(1,128)S(1)} %constant_dynamic-slice_fusion.1) | copy-start | bytes 6148
  20.1 72.4 %copy-start.33 = (f32[512,1]{0,1:T(1,128)}, f32[512,1]{0,1:T(1,128)S(1)}, u32[]{:S(2)}) copy-start(f32[512,1]{0,1:T(1,128)S(1)} %constant_dynamic-slice_fusion) | copy-start | bytes 6148
  21.9 76.6 %copy-start.26 = (f32[512,64]{1,0:T(8,128)}, f32[512,64]{1,0:T(8,128)S(1)}, u32[]{:S(2)}) copy-start(f32[512,64]{1,0:T(8,128)S(1)} %get-tuple-element.118) | copy-start | bytes 393220
  21.9 48.2 %copy-start.2 = (bf16[1,512,2048]{2,1,0:T(8,128)(2,1)S(1)}, bf16[1,512,2048]{2,1,0:T(8,128)(2,1)}, u32[]{:S(2)}) copy-start(bf16[1,512,2048]{2,1,0:T(8,128)(2,1)} %param.10) | copy-start | bytes 6291460
  73.0 19.6 %copy-start.11 = (f32[512,512]{0,1:T(8,128)}, f32[512,512]{0,1:T(8,128)S(1)}, u32[]{:S(2)}) copy-start(f32[512,512]{0,1:T(8,128)S(1)} %get-tuple-element.129) | copy-start | bytes 3145732
  85.3 2.4 copy-start.39
  85.3 7.3 copy-start.37
  92.7 5.8 copy-start.23
  103.0 45.9 %all-gather.12.cloned.1.call-start = ((), (), s32[]{:S(2)}) async-start(), calls=%async_computation.11 | async-start | bytes 2621440 | tf_op jit(solution)/shard_map/all_gather | solution.py:131
  106.8 71.7 %all-gather.20.cloned.1.call-start = ((), (), s32[]{:S(2)}) async-start(), calls=%async_computation.15 | async-start | bytes 2359296 | tf_op jit(solution)/shard_map/all_gather | solution.py:99
  107.4 231.2 %all-reduce.7.cloned.1.call-start = ((), (), s32[]{:S(2)}) async-start(), calls=%async_computation.16 | async-start | bytes 8388608 | tf_op jit(solution)/shard_map/psum | solution.py:158
  157.1 26.4 %copy-start.24 = (bf16[4,128,512]{2,1,0:T(8,128)(2,1)}, bf16[4,128,512]{2,1,0:T(8,128)(2,1)S(1)}, u32[]{:S(2)}) copy-start(bf16[4,128,512]{2,1,0:T(8,128)(2,1)S(1)} %fusion.42) | copy-start | bytes 1572868
  183.5 210.3 %all-gather.22.cloned.1.call-start = ((), (), s32[]{:S(2)}) async-start(), calls=%async_computation.17 | async-start | bytes 9437184 | tf_op jit(solution)/shard_map/all_gather | solution.py:100
  184.2 265.7 %all-gather.24.cloned.1.call-start = ((), (), s32[]{:S(2)}) async-start(), calls=%async_computation.18 | async-start | bytes 9437184 | tf_op jit(solution)/shard_map/all_gather | solution.py:101
  184.9 321.0 %all-gather.26.cloned.1.call-start = ((), (), s32[]{:S(2)}) async-start(), calls=%async_computation.19 | async-start | bytes 9437184 | tf_op jit(solution)/shard_map/all_gather | solution.py:102
  185.5 486.1 %all-reduce.9.cloned.1.call-start = ((), (), s32[]{:S(2)}) async-start(), calls=%async_computation.20 | async-start | bytes 8388608 | tf_op jit(solution)/shard_map/psum | solution.py:165
  338.6 3.4 copy-start
  516.5 343.2 %all-reduce.11.cloned.1.call-start = ((), (), s32[]{:S(2)}) async-start(), calls=%async_computation.21 | async-start | bytes 8388608 | tf_op jit(solution)/shard_map/psum | solution.py:187
  671.7 3.4 copy-start.5
  674.3 3.9 copy-start.6
  675.1 14.2 slice-start.4
  678.3 11.1 slice-start.5
  689.3 6.2 copy-start.44
  689.3 6.2 copy-start.43
  705.6 242.8 %reduce-scatter.13.cloned.1.call-start = ((), (), s32[]{:S(2)}) async-start(), calls=%async_computation.22 | async-start | bytes 5242880 | tf_op jit(solution)/shard_map/reduce_scatter | solution.py:221
  859.7 5.6 copy-start.1
  859.7 6.5 copy-start.4
  859.7 7.1 copy-start.7
  866.8 5.3 copy-start.31
  866.9 6.6 slice-start
  866.9 6.6 slice-start.1
  866.9 8.0 slice-start.2
  872.1 4.1 slice-start.3
  885.9 10.3 copy-start.18
  885.9 10.3 copy-start.19
  904.8 90.5 %reduce-scatter.15.cloned.1.call-start = ((), (), s32[]{:S(2)}) async-start(), calls=%async_computation.23 | async-start | bytes 5242880 | tf_op jit(solution)/shard_map/reduce_scatter | solution.py:222
  916.6 118.2 %reduce-scatter.31.cloned.1.call-start = ((), (), s32[]{:S(2)}) async-start(), calls=%async_computation.32 | async-start | bytes 1179648
  918.2 30.2 %copy-start.27 = (f32[512,64]{1,0:T(8,128)S(1)}, f32[512,64]{1,0:T(8,128)}, u32[]{:S(2)}) copy-start(f32[512,64]{1,0:T(8,128)} %copy-done.26) | copy-start | bytes 393220
  952.4 5.6 copy-start.13
  952.4 5.6 copy-start.36
  952.4 5.6 copy-start.40
  953.7 6.1 copy-start.12
  953.7 6.1 copy-start.34
  953.7 6.1 copy-start.38
  958.0 90.2 %copy-start.42 = (f32[512]{0:T(512)S(1)}, f32[512]{0:T(512)}, u32[]{:S(2)}) copy-start(f32[512]{0:T(512)} %get-tuple-element.122) | copy-start | bytes 6148
  959.9 90.0 %copy-start.41 = (f32[512]{0:T(512)S(1)}, f32[512]{0:T(512)}, u32[]{:S(2)}) copy-start(f32[512]{0:T(512)} %get-tuple-element.139) | copy-start | bytes 6148
  961.6 247.9 %all-reduce.13.cloned.1.call-start = ((), (), s32[]{:S(2)}) async-start(), calls=%async_computation.24 | async-start | bytes 8388608 | tf_op jit(solution)/shard_map/psum | solution.py:259
  1048.2 1.9 copy-start.28
  1050.1 1.8 copy-start.29
  1051.9 1.8 copy-start.32
  1057.1 4.9 copy-start.17
  1057.1 205.7 %reduce-scatter.21.cloned.1.call-start = ((), (), s32[]{:S(2)}) async-start(), calls=%async_computation.27 | async-start | bytes 4718592 | tf_op jit(solution)/shard_map/reduce_scatter | solution.py:263
  1061.9 3.4 copy-start.15
  1061.9 255.2 %reduce-scatter.17.cloned.1.call-start = ((), (), s32[]{:S(2)}) async-start(), calls=%async_computation.25 | async-start | bytes 4718592 | tf_op jit(solution)/shard_map/reduce_scatter | solution.py:261
  1065.3 3.4 copy-start.25
  1065.3 306.3 %reduce-scatter.19.cloned.1.call-start = ((), (), s32[]{:S(2)}) async-start(), calls=%async_computation.26 | async-start | bytes 4718592 | tf_op jit(solution)/shard_map/reduce_scatter | solution.py:262
  1068.6 357.9 %reduce-scatter.23.cloned.1.call-start = ((), (), s32[]{:S(2)}) async-start(), calls=%async_computation.28 | async-start | bytes 4718592 | tf_op jit(solution)/shard_map/reduce_scatter | solution.py:264
  1073.6 473.3 %reduce-scatter.25.cloned.1.call-start = ((), (), s32[]{:S(2)}) async-start(), calls=%async_computation.29 | async-start | bytes 18874368 | tf_op jit(solution)/shard_map/reduce_scatter | solution.py:265
  1085.0 582.2 %reduce-scatter.27.cloned.1.call-start = ((), (), s32[]{:S(2)}) async-start(), calls=%async_computation.30 | async-start | bytes 18874368 | tf_op jit(solution)/shard_map/reduce_scatter | solution.py:266
  1095.0 692.7 %reduce-scatter.29.cloned.1.call-start = ((), (), s32[]{:S(2)}) async-start(), calls=%async_computation.31 | async-start | bytes 18874368 | tf_op jit(solution)/shard_map/reduce_scatter | solution.py:267
  (10 other events, 15.3 us)
Sparse Core Ops, SparseCore 0:
  9.9 30.4 all-gather.13
  42.3 27.7 all-gather.15
  72.0 27.7 all-gather.9
  103.2 21.1 all-gather.17
  126.4 22.5 all-gather.11
  150.7 27.7 all-gather.19
  183.6 154.9 all-reduce.6
  340.5 53.2 all-gather.21
  395.6 54.2 all-gather.23
  451.7 54.2 all-gather.25
  516.6 154.9 all-reduce.8
  705.7 153.9 all-reduce.10
  904.9 43.4 reduce-scatter.12
  950.8 44.4 reduce-scatter.14
  998.9 35.9 reduce-scatter.30
  1057.2 152.2 all-reduce.12
  1212.7 50.0 reduce-scatter.20
  1266.0 51.0 reduce-scatter.16
  1320.5 51.0 reduce-scatter.18
  1375.4 51.1 reduce-scatter.22
  1430.7 116.1 reduce-scatter.24
  1551.1 116.1 reduce-scatter.26
  1671.4 116.1 reduce-scatter.28
where the time goes:
time: 1800 us; the launch traced here: 1790 us
  waiting for transfers between devices  1450 us (81%)
  matrix products  186 us (10%)
  other arithmetic  68.6 us (4%)
  local copies, waits for them, and re-layouts  36.8 us (2%)
  blocking collectives  34.6 us (2%)
    psum x1, waiting for transfers between devices, per_device(): branch_f = lax.psum(contract_cols(activated, w_down), 'tp')  155 us
    psum x1, waiting for transfers between devices, per_device(): lax.psum(contract_cols(d_gate, w_gate) + contract_cols(d_up, w_up), 'tp')  154 us
    psum x1, waiting for transfers between devices, per_device(): branch_a = lax.psum(contract_cols(att_low, w_out), 'tp')  153 us
    reduce_scatter x1, waiting for transfers between devices, per_device(): lax.psum_scatter(down_part, ('fsdp', 'ctx'), scatter_dimension=0, tiled=T...  120 us
    reduce_scatter x1, waiting for transfers between devices, per_device(): lax.psum_scatter(gate_part, ('fsdp', 'ctx'), scatter_dimension=0, tiled=T...  120 us
    reduce_scatter x1, waiting for transfers between devices, per_device(): lax.psum_scatter(up_part, ('fsdp', 'ctx'), scatter_dimension=0, tiled=True)  120 us
    psum x1, waiting for transfers between devices, per_device(): lax.psum(input_part, 'tp')  99.3 us
    reduce_scatter x1, waiting for transfers between devices, per_device(): lax.psum_scatter(out_part, ('fsdp', 'ctx'), scatter_dimension=0, tiled=True)  52.9 us
  transfers between devices with their start and end apart: 23, of which 22 were waited for; matrix products, arithmetic and copies ran while one was open for 10% of the time, Pallas kernels for 0%

commit v1 on v0

v1 whole, which is shorter than its diff:
```python
import functools
import math

import jax
import jax.numpy as jnp
from jax import lax
from jax.experimental import pallas as pl
from jax.experimental.pallas import tpu as pltpu
from jax.sharding import PartitionSpec as P

HEAD_DIM = 128
LOG2E = 1.4426950408889634
ATTN_BLOCK = 512

norm_eps = 1e-06
rope_base = 500000.0
weight_axes = ("fsdp", "ctx")


def rms_scale(values_in):
    return lax.rsqrt(jnp.mean(values_in * values_in, axis=-1, keepdims=True) + norm_eps)


def rope_tables(length, offset):
    half_dim = HEAD_DIM // 2
    frequency = rope_base ** (-(jnp.arange(half_dim, dtype=jnp.float32) * 2.0) / HEAD_DIM)
    angles = (offset + jnp.arange(length, dtype=jnp.int32)).astype(jnp.float32)[
        :, None
    ] * frequency[None, :]
    return (jnp.cos(angles), jnp.sin(angles))


def rotate(values_in, cosine_table, sine_table):
    half_dim = values_in.shape[-1] // 2
    first_half = values_in[..., :half_dim]
    second_half = values_in[..., half_dim:]
    cosine = cosine_table[:, None, :]
    sine_part = sine_table[:, None, :]
    return jnp.concatenate(
        [
            first_half * cosine - second_half * sine_part,
            second_half * cosine + first_half * sine_part,
        ],
        axis=-1,
    )


def unrotate(grad_in, cosine_table, sine_table):
    return rotate(grad_in, cosine_table, -sine_table)


def dot_f32(left, right, left_dim, right_dim):
    return lax.dot_general(
        left,
        right,
        (((left_dim,), (right_dim,)), ((), ())),
        preferred_element_type=jnp.float32,
    )


def contract_rows(left, right):
    return dot_f32(left, right, 0, 0)


def contract_cols(left, right):
    return dot_f32(left, right, 1, 1)


def norm_backward(grad_in, values_in, scale_rows, gain_vec, dot_rows, model_width):
    cubed = scale_rows * scale_rows * scale_rows
    return scale_rows * (grad_in * gain_vec) - values_in * (cubed / model_width) * dot_rows


def causal(values_in, fill):
    keys = lax.broadcasted_iota(jnp.int32, values_in.shape, 0)
    queries = lax.broadcasted_iota(jnp.int32, values_in.shape, 1)
    return jnp.where(keys <= queries, values_in, fill)


def attn_fwd_kernel(q_ref, k_ref, v_ref, out_ref, lse_ref, max_s, sum_s, acc_s, *, block, scale):
    i = pl.program_id(1)
    q = q_ref[0]
    max_s[...] = jnp.full(max_s.shape, -1e30, jnp.float32)
    sum_s[...] = jnp.zeros_like(sum_s)
    acc_s[...] = jnp.zeros_like(acc_s)

    def step(j, diagonal):
        rows = pl.ds(pl.multiple_of(j * block, block), block)
        scores = dot_f32(k_ref[0, rows, :], q, 1, 1) * (scale * LOG2E)
        if diagonal:
            scores = causal(scores, -1e30)
        old_max = max_s[...]
        new_max = jnp.maximum(old_max, jnp.max(scores, axis=0, keepdims=True))
        decay = jnp.exp2(old_max - new_max)
        weights = jnp.exp2(scores - new_max)
        sum_s[...] = sum_s[...] * decay + jnp.sum(weights, axis=0, keepdims=True)
        max_s[...] = new_max
        acc_s[...] = acc_s[...] * decay + dot_f32(
            v_ref[0, rows, :], weights.astype(jnp.bfloat16), 0, 0
        )

    def body(j, carry):
        step(j, False)
        return carry

    lax.fori_loop(0, i, body, 0)
    step(i, True)
    total = sum_s[...]
    out_ref[0] = jnp.transpose(acc_s[...] / total).astype(jnp.bfloat16)
    lse_ref[0] = max_s[...] + jnp.log2(total)


def attn_fwd(packed):
    count, length, _ = packed.shape
    block = min(ATTN_BLOCK, length)
    rows = pl.BlockSpec((1, block, HEAD_DIM), lambda b, i: (b, i, 0))
    return pl.pallas_call(
        functools.partial(attn_fwd_kernel, block=block, scale=1.0 / math.sqrt(HEAD_DIM)),
        grid=(count, length // block),
        in_specs=[
            rows,
            pl.BlockSpec((1, length, HEAD_DIM), lambda b, i: (b, 0, 1)),
            pl.BlockSpec((1, length, HEAD_DIM), lambda b, i: (b, 0, 2)),
        ],
        out_specs=[rows, pl.BlockSpec((1, 1, block), lambda b, i: (b, 0, i))],
        out_shape=[
            jax.ShapeDtypeStruct((count, length, HEAD_DIM), jnp.bfloat16),
            jax.ShapeDtypeStruct((count, 1, length), jnp.float32),
        ],
        scratch_shapes=[
            pltpu.VMEM((1, block), jnp.float32),
            pltpu.VMEM((1, block), jnp.float32),
            pltpu.VMEM((HEAD_DIM, block), jnp.float32),
        ],
        cost_estimate=pl.CostEstimate(
            flops=2 * count * length * length * HEAD_DIM,
            bytes_accessed=10 * count * length * HEAD_DIM,
            transcendentals=count * length * length // 2,
        ),
        name="attn_fwd",
    )(packed, packed, packed)


def attn_bwd_kernel(
    q_ref, k_ref, v_ref, att_ref, grad_ref, lse_ref, out_ref, dk_s, dv_s, dq_s, *, block, scale, blocks
):
    i = pl.program_id(1)

    @pl.when(i == 0)
    def _():
        dk_s[...] = jnp.zeros_like(dk_s)
        dv_s[...] = jnp.zeros_like(dv_s)

    q = q_ref[0]
    grad = grad_ref[0]
    lse = lse_ref[0]
    delta = jnp.sum(
        jnp.transpose(grad.astype(jnp.float32) * att_ref[0].astype(jnp.float32)),
        axis=0,
        keepdims=True,
    )
    dq_s[...] = jnp.zeros_like(dq_s)

    def step(j, diagonal):
        rows = pl.ds(pl.multiple_of(j * block, block), block)
        k = k_ref[0, rows, :]
        probs = jnp.exp2(dot_f32(k, q, 1, 1) * (scale * LOG2E) - lse)
        if diagonal:
            probs = causal(probs, 0.0)
        dv_s[rows, :] += dot_f32(probs.astype(jnp.bfloat16), grad, 1, 0)
        d_probs = dot_f32(v_ref[0, rows, :], grad, 1, 1)
        d_scores = (probs * (d_probs - delta)).astype(jnp.bfloat16)
        dk_s[rows, :] += dot_f32(d_scores, q, 1, 0)
        dq_s[...] += dot_f32(k, d_scores, 0, 0)

    def body(j, carry):
        step(j, False)
        return carry

    lax.fori_loop(0, i, body, 0)
    step(i, True)
    here = pl.ds(pl.multiple_of(i * block, block), block)
    out_ref[0, here, 0:HEAD_DIM] = (jnp.transpose(dq_s[...]) * scale).astype(jnp.bfloat16)

    @pl.when(i == blocks - 1)
    def _():
        out_ref[0, :, HEAD_DIM : 2 * HEAD_DIM] = (dk_s[...] * scale).astype(jnp.bfloat16)
        out_ref[0, :, 2 * HEAD_DIM : 3 * HEAD_DIM] = dv_s[...].astype(jnp.bfloat16)


def attn_bwd(packed, attended, grad, lse):
    count, length, _ = packed.shape
    block = min(ATTN_BLOCK, length)
    rows = pl.BlockSpec((1, block, HEAD_DIM), lambda b, i: (b, i, 0))
    return pl.pallas_call(
        functools.partial(
            attn_bwd_kernel,
            block=block,
            scale=1.0 / math.sqrt(HEAD_DIM),
            blocks=length // block,
        ),
        grid=(count, length // block),
        in_specs=[
            rows,
            pl.BlockSpec((1, length, HEAD_DIM), lambda b, i: (b, 0, 1)),
            pl.BlockSpec((1, length, HEAD_DIM), lambda b, i: (b, 0, 2)),
            rows,
            rows,
            pl.BlockSpec((1, 1, block), lambda b, i: (b, 0, i)),
        ],
        out_specs=pl.BlockSpec((1, length, 3 * HEAD_DIM), lambda b, i: (b, 0, 0)),
        out_shape=jax.ShapeDtypeStruct((count, length, 3 * HEAD_DIM), jnp.bfloat16),
        scratch_shapes=[
            pltpu.VMEM((length, HEAD_DIM), jnp.float32),
            pltpu.VMEM((length, HEAD_DIM), jnp.float32),
            pltpu.VMEM((HEAD_DIM, block), jnp.float32),
        ],
        cost_estimate=pl.CostEstimate(
            flops=5 * count * length * length * HEAD_DIM,
            bytes_accessed=18 * count * length * HEAD_DIM,
            transcendentals=count * length * length // 2,
        ),
        name="attn_bwd",
    )(packed, packed, packed, attended, grad, lse)


def to_heads(values_in, ctx_size):
    seqs, span, heads, width = values_in.shape
    each = heads // ctx_size
    parts = values_in.reshape(seqs, span, ctx_size, each, width).transpose(2, 0, 3, 1, 4)
    parts = lax.all_to_all(parts, "ctx", 0, 0, tiled=True)
    return parts.transpose(1, 2, 0, 3, 4).reshape(seqs * each, ctx_size * span, width)


def to_positions(values_in, seqs, ctx_size):
    count, length, width = values_in.shape
    each, span = count // seqs, length // ctx_size
    parts = values_in.reshape(seqs, each, ctx_size, span, width).transpose(2, 0, 1, 3, 4)
    parts = lax.all_to_all(parts, "ctx", 0, 0, tiled=True)
    return parts.transpose(1, 3, 0, 2, 4).reshape(seqs, span, ctx_size * each, width)


def tensor_sum(values_in):
    return lax.psum(values_in.astype(jnp.bfloat16), "tp").astype(jnp.float32)


def gather_rows(values_in):
    return lax.all_gather(values_in, weight_axes, axis=0, tiled=True)


def scatter_rows(values_in):
    return lax.psum_scatter(
        values_in.astype(jnp.bfloat16), weight_axes, scatter_dimension=0, tiled=True
    ).astype(jnp.float32)


def per_device(
    tokens,
    q_weight,
    k_weight,
    v_weight,
    o_weight,
    gate_weight,
    up_weight,
    down_weight,
    norm_gains,
    cotangent,
):
    seq_count, seq_span, model_width = tokens.shape
    row_count = seq_count * seq_span
    tensor = lax.axis_size("tp")
    ctx_size = lax.axis_size("ctx")
    local_width = model_width // tensor
    hidden = gate_weight.shape[1]
    heads_here = local_width // HEAD_DIM
    feature_start = lax.axis_index("tp") * local_width
    position = lax.axis_index("ctx") * seq_span
    q_shape = (seq_count, seq_span, heads_here, HEAD_DIM)

    w_qkv = gather_rows(jnp.concatenate([q_weight, k_weight, v_weight], axis=1))
    w_out = gather_rows(o_weight)
    w_gate_up = gather_rows(jnp.concatenate([gate_weight, up_weight], axis=1))
    w_down = gather_rows(down_weight)
    gain_table = gather_rows(norm_gains).astype(jnp.float32)
    gain_q = lax.dynamic_slice_in_dim(gain_table[:, 0], feature_start, local_width)
    gain_k = lax.dynamic_slice_in_dim(gain_table[:, 1], feature_start, local_width)
    gain_attn = gain_table[:, 2]
    gain_ffn = gain_table[:, 3]
    inputs = tokens.reshape(row_count, model_width)
    cosine_table, sine_table = rope_tables(seq_span, position)

    qkv_proj = jnp.dot(inputs, w_qkv, preferred_element_type=jnp.float32)
    q_proj = qkv_proj[:, :local_width]
    k_proj = qkv_proj[:, local_width : 2 * local_width]
    v_low = qkv_proj[:, 2 * local_width :].astype(jnp.bfloat16)
    q_squares, k_squares = lax.psum(
        (jnp.sum(q_proj * q_proj, axis=1), jnp.sum(k_proj * k_proj, axis=1)), "tp"
    )
    q_rs = lax.rsqrt(q_squares / model_width + norm_eps)[:, None]
    k_rs = lax.rsqrt(k_squares / model_width + norm_eps)[:, None]
    q_rot = rotate((q_proj * q_rs * gain_q).reshape(q_shape), cosine_table, sine_table)
    k_rot = rotate((k_proj * k_rs * gain_k).reshape(q_shape), cosine_table, sine_table)
    packed = to_heads(
        jnp.concatenate(
            [q_rot.astype(jnp.bfloat16), k_rot.astype(jnp.bfloat16), v_low.reshape(q_shape)], axis=-1
        ),
        ctx_size,
    )
    attended, log_total = attn_fwd(packed)
    att_low = to_positions(attended, seq_count, ctx_size).reshape(row_count, local_width)
    branch_a = tensor_sum(contract_cols(att_low, w_out))
    a_rs = rms_scale(branch_a)
    middle = inputs.astype(jnp.float32) + branch_a * a_rs * gain_attn
    middle_low = middle.astype(jnp.bfloat16)
    gate_up = jnp.dot(middle_low, w_gate_up, preferred_element_type=jnp.float32)
    gate_proj = gate_up[:, :hidden]
    up_proj = gate_up[:, hidden:]
    activated = (jax.nn.silu(gate_proj) * up_proj).astype(jnp.bfloat16)
    branch_f = tensor_sum(contract_cols(activated, w_down))
    f_rs = rms_scale(branch_f)
    block_out = (
        (middle + branch_f * f_rs * gain_ffn)
        .astype(jnp.bfloat16)
        .reshape(seq_count, seq_span, model_width)
    )
    grad_out = cotangent.reshape(row_count, model_width).astype(jnp.float32)
    ffn_gain_part = jnp.sum(grad_out * branch_f * f_rs, axis=0)
    ffn_dot = jnp.sum(grad_out * gain_ffn * branch_f, axis=1, keepdims=True)
    d_branch_f = norm_backward(grad_out, branch_f, f_rs, gain_ffn, ffn_dot, model_width).astype(
        jnp.bfloat16
    )
    down_grad = scatter_rows(contract_rows(d_branch_f, activated))
    d_act = jnp.dot(d_branch_f, w_down, preferred_element_type=jnp.float32)
    sigmoid_gate = jax.nn.sigmoid(gate_proj)
    d_gate = (d_act * up_proj * sigmoid_gate * (1.0 + gate_proj * (1.0 - sigmoid_gate))).astype(
        jnp.bfloat16
    )
    d_up = (d_act * gate_proj * sigmoid_gate).astype(jnp.bfloat16)
    d_gate_up = jnp.concatenate([d_gate, d_up], axis=1)
    d_middle = grad_out + tensor_sum(contract_cols(d_gate_up, w_gate_up))
    gate_up_grad = scatter_rows(contract_rows(middle_low, d_gate_up))
    attn_gain_part = jnp.sum(d_middle * branch_a * a_rs, axis=0)
    attn_dot = jnp.sum(d_middle * gain_attn * branch_a, axis=1, keepdims=True)
    d_branch_a = norm_backward(d_middle, branch_a, a_rs, gain_attn, attn_dot, model_width).astype(
        jnp.bfloat16
    )
    d_att = jnp.dot(d_branch_a, w_out, preferred_element_type=jnp.float32).astype(jnp.bfloat16)
    out_grad = scatter_rows(contract_rows(d_branch_a, att_low))
    d_packed = to_positions(
        attn_bwd(packed, attended, to_heads(d_att.reshape(q_shape), ctx_size), log_total),
        seq_count,
        ctx_size,
    )
    d_q_rot = d_packed[..., :HEAD_DIM].astype(jnp.float32)
    d_k_rot = d_packed[..., HEAD_DIM : 2 * HEAD_DIM].astype(jnp.float32)
    d_value = d_packed[..., 2 * HEAD_DIM :].reshape(row_count, local_width)
    d_q_norm = unrotate(d_q_rot, cosine_table, sine_table).reshape(row_count, local_width)
    d_k_norm = unrotate(d_k_rot, cosine_table, sine_table).reshape(row_count, local_width)
    query_gain_part = jnp.sum(d_q_norm * q_proj * q_rs, axis=0)
    key_gain_part = jnp.sum(d_k_norm * k_proj * k_rs, axis=0)
    pre_gains = lax.dynamic_update_slice(
        jnp.zeros((model_width, 2), jnp.float32),
        jnp.stack([query_gain_part, key_gain_part], axis=1),
        (feature_start, 0),
    )
    is_first = lax.axis_index("tp") == 0
    post_gains = jnp.where(is_first, jnp.stack([attn_gain_part, ffn_gain_part], axis=1), 0.0)
    gain_part = jnp.concatenate([pre_gains, post_gains], axis=1)
    query_dot, key_dot, gain_sum = lax.psum(
        (
            jnp.sum(d_q_norm * gain_q * q_proj, axis=1),
            jnp.sum(d_k_norm * gain_k * k_proj, axis=1),
            gain_part,
        ),
        "tp",
    )
    d_query = norm_backward(d_q_norm, q_proj, q_rs, gain_q, query_dot[:, None], model_width)
    d_key = norm_backward(d_k_norm, k_proj, k_rs, gain_k, key_dot[:, None], model_width)
    d_qkv = jnp.concatenate(
        [d_query.astype(jnp.bfloat16), d_key.astype(jnp.bfloat16), d_value], axis=1
    )
    token_grad = (d_middle + tensor_sum(contract_cols(d_qkv, w_qkv))).reshape(
        seq_count, seq_span, model_width
    )
    qkv_grad = scatter_rows(contract_rows(inputs, d_qkv))
    gain_grad = lax.psum_scatter(gain_sum, weight_axes, scatter_dimension=0, tiled=True)
    return (
        block_out,
        token_grad,
        qkv_grad[:, :local_width],
        qkv_grad[:, local_width : 2 * local_width],
        qkv_grad[:, 2 * local_width :],
        out_grad,
        gate_up_grad[:, :hidden],
        gate_up_grad[:, hidden:],
        down_grad,
        gain_grad,
    )


def solution(mesh):
    weight_spec = P(weight_axes, "tp")
    token_spec = P("fsdp", "ctx", None)
    return jax.shard_map(
        per_device,
        mesh=mesh,
        in_specs=(token_spec,) + (weight_spec,) * 7 + (P(weight_axes, None), token_spec),
        out_specs=(token_spec, token_spec) + (weight_spec,) * 7 + (P(weight_axes, None),),
        check_vma=False,
    )
```

time: 1800 us -> 1110 us (0.62)
  waiting for transfers between devices: 1450 us -> 791 us
  matrix products: 186 us -> 104 us
  blocking collectives: 34.6 us -> 70 us
  Pallas kernels: 0 us -> 20.9 us
    reduce_scatter x9 -> x4, waiting for transfers between devices: 623 us -> 246 us  [scatter_rows(): lax.psum_scatter(values_in.astype(jnp.bfloat16), weight_axes, scatter_dim...]
    psum x4, waiting for transfers between devices: 561 us -> 323 us  [tensor_sum(): return lax.psum(values_in.astype(jnp.bfloat16), 'tp').astype(jnp.float32)]
    dot_general x25 -> x10, matrix products: 174 us -> 92 us  [the longest x8 72.9 us: dot_f32(): lax.dot_general(left, right, (((left_dim,), (right_dim,)), ((), ())), pre...]
    all_gather x9 -> x4, waiting for transfers between devices: 225 us -> 164 us  [gather_rows(): return lax.all_gather(values_in, weight_axes, axis=0, tiled=True)]
    all_to_all x0 -> x2, blocking collectives: none -> 35.4 us  [to_heads(): parts = lax.all_to_all(parts, 'ctx', 0, 0, tiled=True)]
    all_to_all x0 -> x2, waiting for transfers between devices: none -> 28.7 us  [to_positions(): parts = lax.all_to_all(parts, 'ctx', 0, 0, tiled=True)]
    pallas_call x0 -> x2, Pallas kernels: none -> 20.9 us  [the longest x1 11.9 us: attn_bwd(): pl.pallas_call(functools.partial(attn_bwd_kernel, block=block, scale=1.0...]
    unnamed x24 -> x14, waiting for transfers between devices: 42.3 us -> 29.2 us
  transfers between devices with their start and end apart: 23 -> 15, of which waited for: 22 -> 13; matrix products, arithmetic and copies ran while one was open for 10% -> 10% of each run, Pallas kernels for 0% -> 1%
where the time goes in v1:
time: 1110 us; the launch traced here: 1100 us
  waiting for transfers between devices  791 us (71%)
  matrix products  104 us (9%)
  blocking collectives  70 us (6%)
  other arithmetic  53.1 us (5%)
  local copies, waits for them, and re-layouts  40.9 us (4%)
  Pallas kernels  20.9 us (2%)
  between operations  14.4 us (1%)
    psum x4, waiting for transfers between devices, tensor_sum(): return lax.psum(values_in.astype(jnp.bfloat16), 'tp').astype(jnp.float32)  323 us
    reduce_scatter x4, waiting for transfers between devices, scatter_rows(): lax.psum_scatter(values_in.astype(jnp.bfloat16), weight_axes, scatter_dim...  246 us
    all_gather x4, waiting for transfers between devices, gather_rows(): return lax.all_gather(values_in, weight_axes, axis=0, tiled=True)  164 us
    dot_general x8, matrix products, dot_f32(): lax.dot_general(left, right, (((left_dim,), (right_dim,)), ((), ())), pre...  72.9 us
    all_to_all x2, blocking collectives, to_heads(): parts = lax.all_to_all(parts, 'ctx', 0, 0, tiled=True)  35.4 us
    unnamed x14, waiting for transfers between devices  29.2 us
    all_to_all x2, waiting for transfers between devices, to_positions(): parts = lax.all_to_all(parts, 'ctx', 0, 0, tiled=True)  28.7 us
  transfers between devices with their start and end apart: 15, of which 13 were waited for; matrix products, arithmetic and copies ran while one was open for 10% of the time, Pallas kernels for 1%

profile of v1, /device:TPU:0, one launch (start us, length us, event | category | flops | bytes accessed | tf_op | source)
XLA Modules:
  0.0 1103.6 jit_solution(2059391255002606348)
XLA Ops:
  7.2 2.0 pad_maximum_fusion.7
  10.1 10.5 all_gather.16
  20.6 1.8 fusion.29
  22.5 36.1 %all-gather.5.cloned.1.call-done = bf16[2048,1536]{1,0:T(8,128)(2,1)} async-done(((bf16[256,1536]{1,0:T(8,128)(2,1)}), bf16[2048,1536]{1,0:T(8,128)(2,1)}) %all-gather.5.cloned.1.call-update) | async-done | bytes 6291472 | tf_op jit(solution)/shard_map/all_gather | solution.py:248
  58.6 6.2 convolution_bitcast_fusion
  66.9 11.7 %all-reduce.1 = (f32[512]{0:T(512)S(1)}, f32[512]{0:T(512)S(1)}) all-reduce(f32[512]{0:T(512)S(1)} %get-tuple-element.55, f32[512]{0:T(512)S(1)} %get-tuple-element.54), channel_id=1, replica_groups=mesh['fsdp'=2,'ctx'=4,'tp'=4] {'tp'}, use_global_device_ids=true, to_apply=%region_1.0 | all-reduce | flops 1024 | bytes 8192 | tf_op jit(solution)/shard_map/psum | solution.py:296
  78.6 1.8 multiply_multiply_fusion
  81.6 1.4 copy.66
  84.1 1.4 copy.64
  85.4 2.4 copy.63
  87.8 2.0 copy.49
  89.8 3.0 add_convert_fusion
  92.8 3.0 concatenate.46
  95.9 23.2 %all_to_all.20 = bf16[4,1,1,512,384]{4,3,2,1,0:T(8,128)(2,1)} all-to-all(bf16[4,1,1,512,384]{4,3,2,1,0:T(8,128)(2,1)S(1)} %bitcast.106), channel_id=1, replica_groups=mesh['fsdp'=2,'ctx'=4,'tp'=4] {'ctx'}, dimensions={0} | all-to-all | bytes 3145728 | tf_op jit(solution)/shard_map/all_to_all | solution.py:231
  119.1 9.0 attn_fwd.1
  128.2 2.0 copy.50
  130.2 3.5 all-to-all-start.1
  133.8 8.7 all-to-all-done.1
  142.5 4.4 convolution_convert_fusion.6
  147.0 2.9 pad_maximum_fusion.3
  151.1 79.4 %all-reduce.7.cloned.1.call-done = bf16[512,2048]{1,0:T(8,128)(2,1)} async-done(((bf16[512,2048]{1,0:T(8,128)(2,1)}), bf16[512,2048]{1,0:T(8,128)(2,1)}) %all-reduce.7.cloned.1.call-update) | async-done | bytes 2097168 | tf_op jit(solution)/shard_map/psum | solution.py:244
  230.5 2.1 fusion.4
  232.6 89.0 %all-gather.9.cloned.1.call-done = bf16[2048,4096]{1,0:T(8,128)(2,1)} async-done(((bf16[256,4096]{1,0:T(8,128)(2,1)}), bf16[2048,4096]{1,0:T(8,128)(2,1)}) %all-gather.9.cloned.1.call-update) | async-done | bytes 16777232 | tf_op jit(solution)/shard_map/all_gather | solution.py:248
  321.6 12.8 %fusion.39 = f32[512,4096]{1,0:T(8,128)S(1)} fusion(bf16[2048,4096]{1,0:T(8,128)(2,1)} %all-gather.9.cloned.1.call-done, bf16[512,2048]{1,0:T(8,128)(2,1)} %all-reduce.7.cloned.1.call-done, bf16[1,512,2048]{2,1,0:T(8,128)(2,1)S(1)} %copy-done.8, f32[2048]{0:T(1024)S(1)} %bitcast.119, f32[512]{0:T(512)S(1)} %get-tuple-element.105), kind=kOutput, calls=%fused_computation.111 | convolution fusion | flops 8596226048 | bytes 29370368 | tf_op jit(solution)/shard_map/dot_general | solution.py:315
  334.5 3.2 copy-done.6
  339.0 38.7 %all-gather.11.cloned.1.call-done = bf16[2048,2048]{1,0:T(8,128)(2,1)} async-done(((bf16[256,2048]{1,0:T(8,128)(2,1)}), bf16[2048,2048]{1,0:T(8,128)(2,1)}) %all-gather.11.cloned.1.call-update) | async-done | bytes 8388624 | tf_op jit(solution)/shard_map/all_gather | solution.py:248
  377.7 9.1 convolution_convert_fusion.5
  386.8 86.2 %all-reduce.9.cloned.1.call-done = bf16[512,2048]{1,0:T(8,128)(2,1)} async-done(((bf16[512,2048]{1,0:T(8,128)(2,1)}), bf16[512,2048]{1,0:T(8,128)(2,1)}) %all-reduce.9.cloned.1.call-update) | async-done | bytes 2097168 | tf_op jit(solution)/shard_map/psum | solution.py:244
  473.1 2.2 fusion.13
  475.3 3.2 fusion.20
  478.5 10.9 multiply_convert_fusion.1
  489.4 1.4 copy-done.19
  491.4 13.4 %convolution_convert_fusion.7 = bf16[512,2048]{1,0:T(8,128)(2,1)} fusion(bf16[2048,4096]{1,0:T(8,128)(2,1)} %all-gather.9.cloned.1.call-done, bf16[512,2048]{1,0:T(8,128)(2,1)S(1)} %get-tuple-element.62, bf16[512,2048]{1,0:T(8,128)(2,1)S(1)} %get-tuple-element.61), kind=kOutput, calls=%fused_computation.48 | convolution fusion | flops 8599371776 | bytes 23068672 | tf_op jit(solution)/shard_map/dot_general | solution.py:53
  504.8 85.3 %all-reduce.11.cloned.1.call-done = bf16[512,2048]{1,0:T(8,128)(2,1)} async-done(((bf16[512,2048]{1,0:T(8,128)(2,1)}), bf16[512,2048]{1,0:T(8,128)(2,1)}) %all-reduce.11.cloned.1.call-update) | async-done | bytes 2097168 | tf_op jit(solution)/shard_map/psum | solution.py:244
  590.1 4.0 fusion.12
  594.3 5.0 fusion.9
  600.8 12.1 %all_to_all.21 = bf16[4,1,1,512,128]{4,3,2,1,0:T(8,128)(2,1)} all-to-all(bf16[4,1,1,512,128]{4,3,2,1,0:T(8,128)(2,1)S(1)} %bitcast.110), channel_id=1, replica_groups=mesh['fsdp'=2,'ctx'=4,'tp'=4] {'ctx'}, dimensions={0} | all-to-all | bytes 1048576 | tf_op jit(solution)/shard_map/all_to_all | solution.py:231
  613.0 11.9 %attn_bwd.1 = bf16[1,2048,384]{2,1,0:T(8,128)(2,1)} custom-call(bf16[1,2048,384]{2,1,0:T(8,128)(2,1)} %bitcast.103, bf16[1,2048,384]{2,1,0:T(8,128)(2,1)} %bitcast.104, bf16[1,2048,384]{2,1,0:T(8,128)(2,1)} %bitcast.105, bf16[1,2048,128]{2,1,0:T(8,128)(2,1)} %get-tuple-element.12.att_ref, bf16[1,2048,128]{2,1,0:T(8,128)(2,1)} %bitcast.117, ...), custom_call_target="tpu_custom_call" | custom-call | flops 2684354560 | bytes 4718592 | tf_op jit(solution)/shard_map/attn_bwd/pallas_call | solution.py:195
  624.8 4.5 all-to-all-start.3
  629.4 20.0 %all-to-all-done.3 = bf16[4,1,1,512,384]{4,3,2,1,0:T(8,128)(2,1)} async-done(((bf16[4,1,1,512,384]{4,3,2,1,0:T(8,128)(2,1)}), bf16[4,1,1,512,384]{4,3,2,1,0:T(8,128)(2,1)}, u32[]{:S(2)}, u32[]{:S(2)}) %all-to-all-start.3) | async-done | bytes 1572896 | tf_op jit(solution)/shard_map/all_to_all | solution.py:239
  649.4 2.3 slice_convert_fusion.2
  651.8 2.0 multiply_subtract_fusion.1
  655.1 1.6 copy.55
  656.6 2.9 pad_maximum_fusion.6
  659.5 2.5 copy.56
  662.0 2.5 fusion.28
  664.6 1.4 copy.61
  666.0 4.3 convolution_convert_fusion.3
  670.4 2.1 copy.57
  672.5 27.8 %reduce-scatter.16.cloned.1.call-done = f32[256,4]{1,0:T(8,128)} async-done(((f32[2048,4]{1,0:T(8,128)}), f32[256,4]{1,0:T(8,128)}) %reduce-scatter.16.cloned.1.call-update) | async-done | bytes 4112
  701.2 12.4 %all-reduce = (f32[512]{0:T(512)S(1)}, f32[512]{0:T(512)S(1)}, f32[256,4]{0,1:T(4,128)}) all-reduce(f32[512]{0:T(512)S(1)} %get-tuple-element.52, f32[512]{0:T(512)S(1)} %get-tuple-element.47, f32[256,4]{0,1:T(4,128)S(1)} %copy.62), channel_id=1, replica_groups=mesh['fsdp'=2,'ctx'=4,'tp'=4] {'tp'}, use_global_device_ids=true, to_apply=%region_14.15 | all-reduce | flops 2048 | bytes 16384 | tf_op jit(solution)/shard_map/psum | solution.py:369
  713.6 2.5 subtract_convert_fusion.1
  717.1 7.5 convolution_convert_fusion.4
  724.9 10.6 convolution_convert_fusion.1
  736.7 7.9 fusion
  745.2 15.6 %convolution_convert_fusion = bf16[2048,4096]{1,0:T(8,128)(2,1)} fusion(bf16[512,2048]{1,0:T(8,128)(2,1)} %copy-done.20, bf16[512,2048]{1,0:T(8,128)(2,1)} %copy-done.19, bf16[512,2048]{1,0:T(8,128)(2,1)} %all-reduce.7.cloned.1.call-done, bf16[1,512,2048]{2,1,0:T(8,128)(2,1)} %param.10, f32[2048]{0:T(1024)S(1)} %bitcast.122, f32[512]{0:T(512)S(1)} %get-tuple-element.105), kind=kOutput, calls=%fused_computation | convolution fusion | flops 8613003264 | bytes 25176064 | tf_op jit(solution)/shard_map/dot_general | solution.py:53
  760.9 1.8 convert_element_type.154
  762.7 71.5 %all-reduce.13.cloned.1.call-done = bf16[512,2048]{1,0:T(8,128)(2,1)} async-done(((bf16[512,2048]{1,0:T(8,128)(2,1)}), bf16[512,2048]{1,0:T(8,128)(2,1)}) %all-reduce.13.cloned.1.call-update) | async-done | bytes 2097168 | tf_op jit(solution)/shard_map/psum | solution.py:244
  834.2 5.4 add_bitcast_fusion
  839.6 68.6 %reduce-scatter.14.cloned.1.call-done = bf16[256,2048]{1,0:T(8,128)(2,1)} async-done(((bf16[2048,2048]{1,0:T(8,128)(2,1)}), bf16[256,2048]{1,0:T(8,128)(2,1)}) %reduce-scatter.14.cloned.1.call-update) | async-done | bytes 1048592 | tf_op jit(solution)/shard_map/reduce_scatter | solution.py:252
  908.2 2.8 convert_element_type.158
  911.0 62.1 %reduce-scatter.8.cloned.1.call-done = bf16[256,1536]{0,1:T(8,128)(2,1)} async-done(((bf16[2048,1536]{0,1:T(8,128)(2,1)}), bf16[256,1536]{0,1:T(8,128)(2,1)}) %reduce-scatter.8.cloned.1.call-update) | async-done | bytes 786448 | tf_op jit(solution)/shard_map/reduce_scatter | solution.py:252
  977.3 115.6 %reduce-scatter.12.cloned.1.call-done = bf16[256,4096]{1,0:T(8,128)(2,1)} async-done(((bf16[2048,4096]{1,0:T(8,128)(2,1)}), bf16[256,4096]{1,0:T(8,128)(2,1)}) %reduce-scatter.12.cloned.1.call-update) | async-done | bytes 2097168 | tf_op jit(solution)/shard_map/reduce_scatter | solution.py:252
  1092.9 4.1 fusion.44
  (93 shorter events, 20.0 us)
Async XLA Ops:
  7.2 51.4 %all-gather.5.cloned.1.call-start = ((), (), s32[]{:S(2)}) async-start(), calls=%async_computation.9 | async-start | bytes 7077888 | tf_op jit(solution)/shard_map/all_gather | solution.py:248
  9.3 124.5 %all-gather.7.cloned.1.call-start = ((), (), s32[]{:S(2)}) async-start(), calls=%async_computation.10 | async-start | bytes 2359296 | tf_op jit(solution)/shard_map/all_gather | solution.py:248
  64.8 1.8 copy-start.1
  130.2 12.3 %all-to-all-start.1 = ((bf16[4,1,1,512,128]{3,4,2,1,0:T(8,128)(2,1)}), bf16[4,1,1,512,128]{3,4,2,1,0:T(8,128)(2,1)S(1)}, u32[]{:S(2)}, u32[]{:S(2)}) async-start(bf16[4,1,1,512,128]{3,4,2,1,0:T(8,128)(2,1)} %copy.50), calls=%async_computation.1 | async-start | bytes 1048576 | tf_op jit(solution)/shard_map/all_to_all | solution.py:239
  133.7 96.8 %all-reduce.7.cloned.1.call-start = ((), (), s32[]{:S(2)}) async-start(), calls=%async_computation.11 | async-start | bytes 4194304 | tf_op jit(solution)/shard_map/psum | solution.py:244
  142.5 4.5 copy-start.16
  142.5 4.5 copy-start.11
  147.0 174.7 %copy-start.8 = (bf16[1,512,2048]{2,1,0:T(8,128)(2,1)S(1)}, bf16[1,512,2048]{2,1,0:T(8,128)(2,1)}, u32[]{:S(2)}) copy-start(bf16[1,512,2048]{2,1,0:T(8,128)(2,1)} %param.10) | copy-start | bytes 6291460
  147.0 174.7 %all-gather.9.cloned.1.call-start = ((), (), s32[]{:S(2)}) async-start(), calls=%async_computation.12 | async-start | bytes 18874368 | tf_op jit(solution)/shard_map/all_gather | solution.py:248
  149.9 227.7 %all-gather.11.cloned.1.call-start = ((), (), s32[]{:S(2)}) async-start(), calls=%async_computation.13 | async-start | bytes 9437184 | tf_op jit(solution)/shard_map/all_gather | solution.py:248
  150.5 322.5 %all-reduce.9.cloned.1.call-start = ((), (), s32[]{:S(2)}) async-start(), calls=%async_computation.14 | async-start | bytes 4194304 | tf_op jit(solution)/shard_map/psum | solution.py:244
  334.4 3.2 copy-start.6
  339.0 38.7 %copy-start.7 = (bf16[512,2048]{1,0:T(8,128)(2,1)}, bf16[512,2048]{1,0:T(8,128)(2,1)S(1)}, u32[]{:S(2)}) copy-start(bf16[512,2048]{1,0:T(8,128)(2,1)S(1)} %multiply_convert_fusion.2) | copy-start | bytes 6291460
  386.8 88.5 %copy-start = (bf16[1,512,2048]{2,1,0:T(8,128)(2,1)S(1)}, bf16[1,512,2048]{2,1,0:T(8,128)(2,1)}, u32[]{:S(2)}) copy-start(bf16[1,512,2048]{2,1,0:T(8,128)(2,1)} %param.19) | copy-start | bytes 6291460
  386.8 203.4 %all-reduce.11.cloned.1.call-start = ((), (), s32[]{:S(2)}) async-start(), calls=%async_computation.15 | async-start | bytes 4194304 | tf_op jit(solution)/shard_map/psum | solution.py:244
  473.0 5.4 copy-start.2
  489.4 1.4 copy-start.19
  489.4 2.0 copy-start.20
  590.1 4.0 copy-start.3
  590.1 4.0 copy-start.4
  590.1 4.1 copy-start.5
  594.3 5.0 copy-start.18
  599.2 1.3 copy-start.9
  624.8 26.9 %copy-start.10 = (f32[512,64]{1,0:T(8,128)S(1)}, f32[512,64]{1,0:T(8,128)}, u32[]{:S(2)}) copy-start(f32[512,64]{1,0:T(8,128)} %get-tuple-element.97) | copy-start | bytes 393220
  624.8 24.6 %all-to-all-start.3 = ((bf16[4,1,1,512,384]{4,3,2,1,0:T(8,128)(2,1)}), bf16[4,1,1,512,384]{4,3,2,1,0:T(8,128)(2,1)}, u32[]{:S(2)}, u32[]{:S(2)}) async-start(bf16[4,1,1,512,384]{4,3,2,1,0:T(8,128)(2,1)} %bitcast.111), calls=%async_computation.3 | async-start | bytes 3145728 | tf_op jit(solution)/shard_map/all_to_all | solution.py:239
  629.3 70.9 %reduce-scatter.16.cloned.1.call-start = ((), (), s32[]{:S(2)}) async-start(), calls=%async_computation.21 | async-start | bytes 1179648
  666.0 94.9 %reduce-scatter.10.cloned.1.call-start = ((), (), s32[]{:S(2)}) async-start(), calls=%async_computation.18 | async-start | bytes 2359296 | tf_op jit(solution)/shard_map/reduce_scatter | solution.py:252
  670.4 163.8 %all-reduce.13.cloned.1.call-start = ((), (), s32[]{:S(2)}) async-start(), calls=%async_computation.16 | async-start | bytes 4194304 | tf_op jit(solution)/shard_map/psum | solution.py:244
  713.6 3.5 copy-start.17
  716.1 0.8 copy-start.12
  716.1 1.0 copy-start.14
  724.6 183.6 %reduce-scatter.14.cloned.1.call-start = ((), (), s32[]{:S(2)}) async-start(), calls=%async_computation.20 | async-start | bytes 9437184 | tf_op jit(solution)/shard_map/reduce_scatter | solution.py:252
  735.5 1.0 copy-start.13
  735.5 1.2 copy-start.15
  735.5 237.6 %reduce-scatter.8.cloned.1.call-start = ((), (), s32[]{:S(2)}) async-start(), calls=%async_computation.17 | async-start | bytes 7077888 | tf_op jit(solution)/shard_map/reduce_scatter | solution.py:252
  744.6 348.2 %reduce-scatter.12.cloned.1.call-start = ((), (), s32[]{:S(2)}) async-start(), calls=%async_computation.19 | async-start | bytes 18874368 | tf_op jit(solution)/shard_map/reduce_scatter | solution.py:252
Sparse Core Ops, SparseCore 0:
  10.4 48.1 all-gather.4
  60.5 27.7 all-gather.6
  147.1 83.3 all-reduce.6
  232.8 88.7 all-gather.8
  323.4 54.2 all-gather.10
  386.9 86.1 all-reduce.8
  504.9 85.1 all-reduce.10
  666.1 34.0 reduce-scatter.15
  704.1 41.1 reduce-scatter.9
  748.0 86.1 all-reduce.12
  837.7 70.5 reduce-scatter.13
  911.5 61.5 reduce-scatter.7
  976.7 116.1 reduce-scatter.11

commit v2 on v1

--- a/solution.py
+++ b/solution.py
@@ -7,6 +7,7 @@
 from jax.experimental import pallas as pl
 from jax.experimental.pallas import tpu as pltpu
 from jax.sharding import PartitionSpec as P
+
 
 HEAD_DIM = 128
 LOG2E = 1.4426950408889634
@@ -241,7 +242,9 @@
 
 
 def tensor_sum(values_in):
-    return lax.psum(values_in.astype(jnp.bfloat16), "tp").astype(jnp.float32)
+    values_in = values_in.astype(jnp.bfloat16)
+    total = lax.psum(values_in, "tp")
+    return total.astype(jnp.float32)
 
 
 def gather_rows(values_in):
@@ -249,9 +252,8 @@
 
 
 def scatter_rows(values_in):
-    return lax.psum_scatter(
-        values_in.astype(jnp.bfloat16), weight_axes, scatter_dimension=0, tiled=True
-    ).astype(jnp.float32)
+    values_in = values_in.astype(jnp.bfloat16)
+    return lax.psum_scatter(values_in, weight_axes, scatter_dimension=0, tiled=True)
 
 
 def per_device(
@@ -329,7 +331,8 @@
     d_branch_f = norm_backward(grad_out, branch_f, f_rs, gain_ffn, ffn_dot, model_width).astype(
         jnp.bfloat16
     )
-    down_grad = scatter_rows(contract_rows(d_branch_f, activated))
+    down_part = contract_rows(d_branch_f, activated)
+    down_grad = scatter_rows(down_part).astype(jnp.float32)
     d_act = jnp.dot(d_branch_f, w_down, preferred_element_type=jnp.float32)
     sigmoid_gate = jax.nn.sigmoid(gate_proj)
     d_gate = (d_act * up_proj * sigmoid_gate * (1.0 + gate_proj * (1.0 - sigmoid_gate))).astype(
@@ -338,14 +341,16 @@
     d_up = (d_act * gate_proj * sigmoid_gate).astype(jnp.bfloat16)
     d_gate_up = jnp.concatenate([d_gate, d_up], axis=1)
     d_middle = grad_out + tensor_sum(contract_cols(d_gate_up, w_gate_up))
-    gate_up_grad = scatter_rows(contract_rows(middle_low, d_gate_up))
+    gate_up_part = contract_rows(middle_low, d_gate_up)
+    gate_up_grad = scatter_rows(gate_up_part).astype(jnp.float32)
     attn_gain_part = jnp.sum(d_middle * branch_a * a_rs, axis=0)
     attn_dot = jnp.sum(d_middle * gain_attn * branch_a, axis=1, keepdims=True)
     d_branch_a = norm_backward(d_middle, branch_a, a_rs, gain_attn, attn_dot, model_width).astype(
         jnp.bfloat16
     )
     d_att = jnp.dot(d_branch_a, w_out, preferred_element_type=jnp.float32).astype(jnp.bfloat16)
-    out_grad = scatter_rows(contract_rows(d_branch_a, att_low))
+    out_part = contract_rows(d_branch_a, att_low)
+    out_grad = scatter_rows(out_part).astype(jnp.float32)
     d_packed = to_positions(
         attn_bwd(packed, attended, to_heads(d_att.reshape(q_shape), ctx_size), log_total),
         seq_count,
@@ -359,21 +364,24 @@
     query_gain_part = jnp.sum(d_q_norm * q_proj * q_rs, axis=0)
     key_gain_part = jnp.sum(d_k_norm * k_proj * k_rs, axis=0)
     pre_gains = lax.dynamic_update_slice(
-        jnp.zeros((model_width, 2), jnp.float32),
-        jnp.stack([query_gain_part, key_gain_part], axis=1),
-        (feature_start, 0),
+        jnp.zeros((2, model_width), jnp.float32),
+        jnp.stack([query_gain_part, key_gain_part]),
+        (0, feature_start),
     )
     is_first = lax.axis_index("tp") == 0
-    post_gains = jnp.where(is_first, jnp.stack([attn_gain_part, ffn_gain_part], axis=1), 0.0)
-    gain_part = jnp.concatenate([pre_gains, post_gains], axis=1)
+    post_gains = jnp.where(is_first, jnp.stack([attn_gain_part, ffn_gain_part]), 0.0)
     query_dot, key_dot, gain_sum = lax.psum(
         (
             jnp.sum(d_q_norm * gain_q * q_proj, axis=1),
             jnp.sum(d_k_norm * gain_k * k_proj, axis=1),
-            gain_part,
+            jnp.concatenate([pre_gains, post_gains], axis=0),
         ),
         "tp",
     )
+    gain_high = gain_sum.astype(jnp.bfloat16)
+    gain_rest = (gain_sum - gain_high.astype(jnp.float32)).astype(jnp.bfloat16)
+    gain_terms = jnp.concatenate([gain_high, gain_rest], axis=0).T
+    gain_terms = jnp.pad(gain_terms, ((0, 0), (0, HEAD_DIM - gain_terms.shape[1])))
     d_query = norm_backward(d_q_norm, q_proj, q_rs, gain_q, query_dot[:, None], model_width)
     d_key = norm_backward(d_k_norm, k_proj, k_rs, gain_k, key_dot[:, None], model_width)
     d_qkv = jnp.concatenate(
@@ -382,8 +390,13 @@
     token_grad = (d_middle + tensor_sum(contract_cols(d_qkv, w_qkv))).reshape(
         seq_count, seq_span, model_width
     )
-    qkv_grad = scatter_rows(contract_rows(inputs, d_qkv))
-    gain_grad = lax.psum_scatter(gain_sum, weight_axes, scatter_dimension=0, tiled=True)
+    qkv_part = contract_rows(inputs, d_qkv).astype(jnp.bfloat16)
+    last_grad = scatter_rows(jnp.concatenate([qkv_part, gain_terms], axis=1)).astype(jnp.float32)
+    qkv_grad = last_grad[:, : 3 * local_width]
+    gain_grad = (
+        last_grad[:, 3 * local_width : 3 * local_width + 4]
+        + last_grad[:, 3 * local_width + 4 : 3 * local_width + 8]
+    )
     return (
         block_out,
         token_grad,

time: 1110 us -> 1060 us (0.955)
  waiting for transfers between devices: 791 us -> 734 us
    unnamed x14 -> x12, waiting for transfers between devices: 29.2 us -> 1.39 us
    psum x4, waiting for transfers between devices: 323 us -> 296 us  [tensor_sum(): total = lax.psum(values_in, 'tp')]
  transfers between devices with their start and end apart: 15 -> 14, of which waited for: 13 -> 12; matrix products, arithmetic and copies ran while one was open for 10% -> 13% of each run, Pallas kernels for 1% -> 1%
where the time goes in v2:
time: 1060 us; the launch traced here: 1050 us
  waiting for transfers between devices  734 us (69%)
  matrix products  101 us (10%)
  blocking collectives  75.4 us (7%)
  other arithmetic  58.7 us (6%)
  local copies, waits for them, and re-layouts  40.1 us (4%)
  Pallas kernels  21 us (2%)
  between operations  14.8 us (1%)
    psum x4, waiting for transfers between devices, tensor_sum(): total = lax.psum(values_in, 'tp')  296 us
    reduce_scatter x4, waiting for transfers between devices, scatter_rows(): lax.psum_scatter(values_in, weight_axes, scatter_dimension=0, tiled=True)  248 us
    all_gather x4, waiting for transfers between devices, gather_rows(): return lax.all_gather(values_in, weight_axes, axis=0, tiled=True)  164 us
    dot_general x8, matrix products, dot_f32(): lax.dot_general(left, right, (((left_dim,), (right_dim,)), ((), ())), pre...  70.1 us
    all_to_all x2, blocking collectives, to_heads(): parts = lax.all_to_all(parts, 'ctx', 0, 0, tiled=True)  35.6 us
    all_to_all x2, waiting for transfers between devices, to_positions(): parts = lax.all_to_all(parts, 'ctx', 0, 0, tiled=True)  24.4 us
  transfers between devices with their start and end apart: 14, of which 12 were waited for; matrix products, arithmetic and copies ran while one was open for 13% of the time, Pallas kernels for 1%

profile of v2, /device:TPU:0, one launch (start us, length us, event | category | flops | bytes accessed | tf_op | source)
XLA Modules:
  0.0 1053.8 jit_solution(9176302126456644540)
XLA Ops:
  7.2 2.0 pad_maximum_fusion.7
  10.1 10.5 %all_gather.16 = bf16[2048,4]{0,1:T(4,128)(2,1)S(1)} all-gather(bf16[256,4]{0,1:T(4,128)(2,1)} %param.18), channel_id=1, replica_groups=mesh['fsdp'=2,'ctx'=4,'tp'=4] {'fsdp','ctx'}, dimensions={0}, use_global_device_ids=true | all-gather | bytes 18432 | tf_op jit(solution)/shard_map/all_gather | solution.py:251
  20.6 1.8 fusion.31
  22.5 36.1 %all-gather.5.cloned.1.call-done = bf16[2048,1536]{1,0:T(8,128)(2,1)} async-done(((bf16[256,1536]{1,0:T(8,128)(2,1)}), bf16[2048,1536]{1,0:T(8,128)(2,1)}) %all-gather.5.cloned.1.call-update) | async-done | bytes 6291472 | tf_op jit(solution)/shard_map/all_gather | solution.py:251
  58.6 6.2 convolution_bitcast_fusion
  66.0 11.7 %all-reduce.2 = (f32[512]{0:T(512)S(1)}, f32[512]{0:T(512)S(1)}) all-reduce(f32[512]{0:T(512)S(1)} %get-tuple-element.55, f32[512]{0:T(512)S(1)} %get-tuple-element.54), channel_id=1, replica_groups=mesh['fsdp'=2,'ctx'=4,'tp'=4] {'tp'}, use_global_device_ids=true, to_apply=%region_1.0 | all-reduce | flops 1024 | bytes 8192 | tf_op jit(solution)/shard_map/psum | solution.py:298
  80.0 1.4 copy.63
  81.3 1.4 copy.64
  82.7 2.2 fusion.48
  85.0 1.4 copy.62
  86.3 2.4 copy.61
  88.7 2.0 copy.49
  90.7 3.0 add_convert_fusion
  93.7 3.0 concatenate.52
  96.8 23.3 %all_to_all.20 = bf16[4,1,1,512,384]{4,3,2,1,0:T(8,128)(2,1)} all-to-all(bf16[4,1,1,512,384]{4,3,2,1,0:T(8,128)(2,1)S(1)} %bitcast.107), channel_id=1, replica_groups=mesh['fsdp'=2,'ctx'=4,'tp'=4] {'ctx'}, dimensions={0} | all-to-all | bytes 3145728 | tf_op jit(solution)/shard_map/all_to_all | solution.py:232
  120.1 9.0 attn_fwd.1
  129.1 2.0 copy.50
  131.1 3.5 all-to-all-start.1
  134.7 8.7 all-to-all-done.1
  143.4 4.4 convolution_convert_fusion.6
  147.9 2.9 pad_maximum_fusion.3
  151.6 79.5 %all-reduce.8.cloned.1.call-done = bf16[512,2048]{1,0:T(8,128)(2,1)} async-done(((bf16[512,2048]{1,0:T(8,128)(2,1)}), bf16[512,2048]{1,0:T(8,128)(2,1)}) %all-reduce.8.cloned.1.call-update) | async-done | bytes 2097168 | tf_op jit(solution)/shard_map/psum | solution.py:246
  231.2 2.1 fusion.6
  233.3 89.0 %all-gather.9.cloned.1.call-done = bf16[2048,4096]{1,0:T(8,128)(2,1)} async-done(((bf16[256,4096]{1,0:T(8,128)(2,1)}), bf16[2048,4096]{1,0:T(8,128)(2,1)}) %all-gather.9.cloned.1.call-update) | async-done | bytes 16777232 | tf_op jit(solution)/shard_map/all_gather | solution.py:251
  322.3 12.8 %fusion.41 = f32[512,4096]{1,0:T(8,128)S(1)} fusion(bf16[2048,4096]{1,0:T(8,128)(2,1)} %all-gather.9.cloned.1.call-done, bf16[512,2048]{1,0:T(8,128)(2,1)} %all-reduce.8.cloned.1.call-done, bf16[1,512,2048]{2,1,0:T(8,128)(2,1)S(1)} %copy-done.9, f32[2048]{0:T(1024)S(1)} %bitcast.120, f32[512]{0:T(512)S(1)} %get-tuple-element.107), kind=kOutput, calls=%fused_computation.117 | convolution fusion | flops 8596226048 | bytes 29370368 | tf_op jit(solution)/shard_map/dot_general | solution.py:317
  335.1 3.2 copy-done.6
  339.6 38.7 %all-gather.11.cloned.1.call-done = bf16[2048,2048]{1,0:T(8,128)(2,1)} async-done(((bf16[256,2048]{1,0:T(8,128)(2,1)}), bf16[2048,2048]{1,0:T(8,128)(2,1)}) %all-gather.11.cloned.1.call-update) | async-done | bytes 8388624 | tf_op jit(solution)/shard_map/all_gather | solution.py:251
  378.3 9.1 convolution_convert_fusion.5
  387.5 86.2 %all-reduce.10.cloned.1.call-done = bf16[512,2048]{1,0:T(8,128)(2,1)} async-done(((bf16[512,2048]{1,0:T(8,128)(2,1)}), bf16[512,2048]{1,0:T(8,128)(2,1)}) %all-reduce.10.cloned.1.call-update) | async-done | bytes 2097168 | tf_op jit(solution)/shard_map/psum | solution.py:246
  473.7 2.2 fusion.15
  476.0 3.2 fusion.22
  479.2 10.9 %multiply_convert_fusion.1 = (bf16[512,2048]{1,0:T(8,128)(2,1)S(1)}, bf16[512,2048]{1,0:T(8,128)(2,1)S(1)}) fusion(f32[512,4096]{1,0:T(8,128)} %copy-done.6, bf16[2048,2048]{1,0:T(8,128)(2,1)} %all-gather.11.cloned.1.call-done, bf16[512,2048]{1,0:T(8,128)(2,1)S(1)} %copy-done.2, bf16[1,512,2048]{2,1,0:T(8,128)(2,1)S(1)} %copy-done, ...), kind=kOutput, calls=%fused_computation.42 | convolution fusion | flops 4316987392 | bytes 25180160 | tf_op jit(solution)/shard_map/dot_general | solution.py:336
  492.1 13.4 %convolution_convert_fusion.7 = bf16[512,2048]{1,0:T(8,128)(2,1)} fusion(bf16[2048,4096]{1,0:T(8,128)(2,1)} %all-gather.9.cloned.1.call-done, bf16[512,2048]{1,0:T(8,128)(2,1)S(1)} %get-tuple-element.64, bf16[512,2048]{1,0:T(8,128)(2,1)S(1)} %get-tuple-element.63), kind=kOutput, calls=%fused_computation.51 | convolution fusion | flops 8599371776 | bytes 23068672 | tf_op jit(solution)/shard_map/dot_general | solution.py:54
  505.5 85.3 %all-reduce.12.cloned.1.call-done = bf16[512,2048]{1,0:T(8,128)(2,1)} async-done(((bf16[512,2048]{1,0:T(8,128)(2,1)}), bf16[512,2048]{1,0:T(8,128)(2,1)}) %all-reduce.12.cloned.1.call-update) | async-done | bytes 2097168 | tf_op jit(solution)/shard_map/psum | solution.py:246
  590.9 4.0 fusion.14
  595.0 5.0 fusion.11
  601.6 12.3 %all_to_all.21 = bf16[4,1,1,512,128]{4,3,2,1,0:T(8,128)(2,1)} all-to-all(bf16[4,1,1,512,128]{4,3,2,1,0:T(8,128)(2,1)S(1)} %bitcast.111), channel_id=1, replica_groups=mesh['fsdp'=2,'ctx'=4,'tp'=4] {'ctx'}, dimensions={0} | all-to-all | bytes 1048576 | tf_op jit(solution)/shard_map/all_to_all | solution.py:232
  613.9 11.9 %attn_bwd.1 = bf16[1,2048,384]{2,1,0:T(8,128)(2,1)} custom-call(bf16[1,2048,384]{2,1,0:T(8,128)(2,1)} %bitcast.104, bf16[1,2048,384]{2,1,0:T(8,128)(2,1)} %bitcast.105, bf16[1,2048,384]{2,1,0:T(8,128)(2,1)} %bitcast.106, bf16[1,2048,128]{2,1,0:T(8,128)(2,1)} %get-tuple-element.12.att_ref, bf16[1,2048,128]{2,1,0:T(8,128)(2,1)} %bitcast.118, ...), custom_call_target="tpu_custom_call" | custom-call | flops 2684354560 | bytes 4718592 | tf_op jit(solution)/shard_map/attn_bwd/pallas_call | solution.py:196
  625.8 4.3 all-to-all-start.3
  630.2 4.2 convolution_convert_fusion.3
  634.5 15.7 %all-to-all-done.3 = bf16[4,1,1,512,384]{4,3,2,1,0:T(8,128)(2,1)} async-done(((bf16[4,1,1,512,384]{4,3,2,1,0:T(8,128)(2,1)}), bf16[4,1,1,512,384]{4,3,2,1,0:T(8,128)(2,1)}, u32[]{:S(2)}, u32[]{:S(2)}) %all-to-all-start.3) | async-done | bytes 1572896 | tf_op jit(solution)/shard_map/all_to_all | solution.py:240
  650.3 2.7 slice_convert_fusion.2
  652.9 2.0 copy.57
  655.0 3.7 multiply_subtract_fusion.1
  660.0 1.6 copy.55
  661.6 2.9 pad_maximum_fusion.6
  664.4 2.5 copy.56
  667.0 2.5 fusion.30
  669.5 17.6 %all-reduce.1 = (f32[512]{0:T(512)S(1)}, f32[512]{0:T(512)S(1)}, f32[4,2048]{1,0:T(4,128)S(1)}) all-reduce(f32[512]{0:T(512)S(1)} %get-tuple-element.52, f32[512]{0:T(512)S(1)} %get-tuple-element.47, f32[4,2048]{1,0:T(4,128)S(1)} %pad_maximum_fusion.10), channel_id=1, replica_groups=mesh['fsdp'=2,'ctx'=4,'tp'=4] {'tp'}, use_global_device_ids=true, to_apply=%region_14.15 | all-reduce | flops 9216 | bytes 73728 | tf_op jit(solution)/shard_map/psum | solution.py:373
  687.1 2.4 subtract_convert_fusion.1
  690.5 7.5 convolution_convert_fusion.4
  698.2 10.6 %convolution_convert_fusion.1 = bf16[2048,2048]{1,0:T(8,128)(2,1)} fusion(bf16[512,2048]{1,0:T(8,128)(2,1)} %copy-done.8, bf16[512,2048]{1,0:T(8,128)(2,1)} %all-reduce.10.cloned.1.call-done, bf16[1,512,2048]{2,1,0:T(8,128)(2,1)S(1)} %copy-done, f32[512]{0:T(512)S(1)} %get-tuple-element.51, f32[512]{0:T(512)S(1)} %get-tuple-element.108, ...), kind=kOutput, calls=%fused_computation.13 | convolution fusion | flops 4307550208 | bytes 14694400 | tf_op jit(solution)/shard_map/dot_general | solution.py:54
  710.0 5.2 fusion.2
  715.2 3.7 fusion.1
  719.2 15.7 %convolution_convert_fusion = bf16[2048,4096]{1,0:T(8,128)(2,1)} fusion(bf16[512,2048]{1,0:T(8,128)(2,1)} %copy-done.21, bf16[512,2048]{1,0:T(8,128)(2,1)} %copy-done.20, bf16[512,2048]{1,0:T(8,128)(2,1)} %all-reduce.8.cloned.1.call-done, bf16[1,512,2048]{2,1,0:T(8,128)(2,1)} %param.10, f32[2048]{0:T(1024)S(1)} %bitcast.123, f32[512]{0:T(512)S(1)} %get-tuple-element.107), kind=kOutput, calls=%fused_computation | convolution fusion | flops 8613003264 | bytes 25176064 | tf_op jit(solution)/shard_map/dot_general | solution.py:54
  734.9 1.8 convert_element_type.168
  736.7 44.9 %all-reduce.14.cloned.1.call-done = bf16[512,2048]{1,0:T(8,128)(2,1)} async-done(((bf16[512,2048]{1,0:T(8,128)(2,1)}), bf16[512,2048]{1,0:T(8,128)(2,1)}) %all-reduce.14.cloned.1.call-update) | async-done | bytes 2097168 | tf_op jit(solution)/shard_map/psum | solution.py:246
  781.6 5.4 add_bitcast_fusion
  786.9 68.5 %reduce-scatter.11.cloned.1.call-done = bf16[256,2048]{1,0:T(8,128)(2,1)} async-done(((bf16[2048,2048]{1,0:T(8,128)(2,1)}), bf16[256,2048]{1,0:T(8,128)(2,1)}) %reduce-scatter.11.cloned.1.call-update) | async-done | bytes 1048592 | tf_op jit(solution)/shard_map/reduce_scatter | solution.py:256
  855.4 2.8 convert_element_type.172
  858.2 64.8 %reduce-scatter.5.cloned.1.call-done = bf16[256,1664]{0,1:T(8,128)(2,1)} async-done(((bf16[2048,1664]{0,1:T(8,128)(2,1)}), bf16[256,1664]{0,1:T(8,128)(2,1)}) %reduce-scatter.5.cloned.1.call-update) | async-done | bytes 851984 | tf_op jit(solution)/shard_map/reduce_scatter | solution.py:256
  923.0 1.3 fusion.49
  928.0 114.6 %reduce-scatter.9.cloned.1.call-done = bf16[256,4096]{1,0:T(8,128)(2,1)} async-done(((bf16[2048,4096]{1,0:T(8,128)(2,1)}), bf16[256,4096]{1,0:T(8,128)(2,1)}) %reduce-scatter.9.cloned.1.call-update) | async-done | bytes 2097168 | tf_op jit(solution)/shard_map/reduce_scatter | solution.py:256
  1042.6 4.1 fusion.46
  (95 shorter events, 18.2 us)
Async XLA Ops:
  7.2 51.4 %all-gather.5.cloned.1.call-start = ((), (), s32[]{:S(2)}) async-start(), calls=%async_computation.8 | async-start | bytes 7077888 | tf_op jit(solution)/shard_map/all_gather | solution.py:251
  9.3 125.4 %all-gather.7.cloned.1.call-start = ((), (), s32[]{:S(2)}) async-start(), calls=%async_computation.9 | async-start | bytes 2359296 | tf_op jit(solution)/shard_map/all_gather | solution.py:251
  64.8 15.1 %copy-start.1 = (f32[512,1536]{0,1:T(8,128)}, f32[512,1536]{0,1:T(8,128)S(1)}, u32[]{:S(2)}) copy-start(f32[512,1536]{0,1:T(8,128)S(1)} %convolution_bitcast_fusion) | copy-start | bytes 9437188
  131.1 12.3 %all-to-all-start.1 = ((bf16[4,1,1,512,128]{3,4,2,1,0:T(8,128)(2,1)}), bf16[4,1,1,512,128]{3,4,2,1,0:T(8,128)(2,1)S(1)}, u32[]{:S(2)}, u32[]{:S(2)}) async-start(bf16[4,1,1,512,128]{3,4,2,1,0:T(8,128)(2,1)} %copy.50), calls=%async_computation.1 | async-start | bytes 1048576 | tf_op jit(solution)/shard_map/all_to_all | solution.py:240
  134.6 96.6 %all-reduce.8.cloned.1.call-start = ((), (), s32[]{:S(2)}) async-start(), calls=%async_computation.10 | async-start | bytes 4194304 | tf_op jit(solution)/shard_map/psum | solution.py:246
  143.4 4.5 copy-start.16
  143.4 4.5 copy-start.11
  147.9 174.4 %copy-start.9 = (bf16[1,512,2048]{2,1,0:T(8,128)(2,1)S(1)}, bf16[1,512,2048]{2,1,0:T(8,128)(2,1)}, u32[]{:S(2)}) copy-start(bf16[1,512,2048]{2,1,0:T(8,128)(2,1)} %param.10) | copy-start | bytes 6291460
  147.9 174.4 %all-gather.9.cloned.1.call-start = ((), (), s32[]{:S(2)}) async-start(), calls=%async_computation.11 | async-start | bytes 18874368 | tf_op jit(solution)/shard_map/all_gather | solution.py:251
  150.8 227.5 %all-gather.11.cloned.1.call-start = ((), (), s32[]{:S(2)}) async-start(), calls=%async_computation.12 | async-start | bytes 9437184 | tf_op jit(solution)/shard_map/all_gather | solution.py:251
  151.4 322.3 %all-reduce.10.cloned.1.call-start = ((), (), s32[]{:S(2)}) async-start(), calls=%async_computation.13 | async-start | bytes 4194304 | tf_op jit(solution)/shard_map/psum | solution.py:246
  335.1 3.2 copy-start.6
  339.6 38.7 %copy-start.8 = (bf16[512,2048]{1,0:T(8,128)(2,1)}, bf16[512,2048]{1,0:T(8,128)(2,1)S(1)}, u32[]{:S(2)}) copy-start(bf16[512,2048]{1,0:T(8,128)(2,1)S(1)} %multiply_convert_fusion.2) | copy-start | bytes 6291460
  387.4 88.6 %copy-start = (bf16[1,512,2048]{2,1,0:T(8,128)(2,1)S(1)}, bf16[1,512,2048]{2,1,0:T(8,128)(2,1)}, u32[]{:S(2)}) copy-start(bf16[1,512,2048]{2,1,0:T(8,128)(2,1)} %param.19) | copy-start | bytes 6291460
  387.4 203.4 %all-reduce.12.cloned.1.call-start = ((), (), s32[]{:S(2)}) async-start(), calls=%async_computation.14 | async-start | bytes 4194304 | tf_op jit(solution)/shard_map/psum | solution.py:246
  473.7 5.4 copy-start.2
  490.1 1.3 copy-start.20
  490.1 2.0 copy-start.21
  590.9 4.0 copy-start.3
  590.9 4.0 copy-start.4
  590.9 4.1 copy-start.5
  595.0 5.0 copy-start.19
  600.0 1.3 copy-start.10
  613.9 16.3 %copy-start.17 = (bf16[4,1,1,512,128]{3,4,2,1,0:T(8,128)(2,1)S(1)}, bf16[4,1,1,512,128]{3,4,2,1,0:T(8,128)(2,1)}, u32[]{:S(2)}) copy-start(bf16[4,1,1,512,128]{3,4,2,1,0:T(8,128)(2,1)} %copy-done.16) | copy-start | bytes 1572868
  625.8 24.5 %all-to-all-start.3 = ((bf16[4,1,1,512,384]{4,3,2,1,0:T(8,128)(2,1)}), bf16[4,1,1,512,384]{4,3,2,1,0:T(8,128)(2,1)}, u32[]{:S(2)}, u32[]{:S(2)}) async-start(bf16[4,1,1,512,384]{4,3,2,1,0:T(8,128)(2,1)} %bitcast.112), calls=%async_computation.3 | async-start | bytes 3145728 | tf_op jit(solution)/shard_map/all_to_all | solution.py:240
  630.1 104.7 %reduce-scatter.7.cloned.1.call-start = ((), (), s32[]{:S(2)}) async-start(), calls=%async_computation.17 | async-start | bytes 2359296 | tf_op jit(solution)/shard_map/reduce_scatter | solution.py:256
  634.5 147.1 %all-reduce.14.cloned.1.call-start = ((), (), s32[]{:S(2)}) async-start(), calls=%async_computation.15 | async-start | bytes 4194304 | tf_op jit(solution)/shard_map/psum | solution.py:246
  687.1 3.4 copy-start.18
  689.5 0.8 copy-start.12
  689.5 1.0 copy-start.14
  698.0 157.4 %reduce-scatter.11.cloned.1.call-start = ((), (), s32[]{:S(2)}) async-start(), calls=%async_computation.19 | async-start | bytes 9437184 | tf_op jit(solution)/shard_map/reduce_scatter | solution.py:256
  708.8 1.0 copy-start.13
  708.8 1.2 copy-start.15
  708.8 214.2 %reduce-scatter.5.cloned.1.call-start = ((), (), s32[]{:S(2)}) async-start(), calls=%async_computation.16 | async-start | bytes 7667712 | tf_op jit(solution)/shard_map/reduce_scatter | solution.py:256
  718.9 323.7 %reduce-scatter.9.cloned.1.call-start = ((), (), s32[]{:S(2)}) async-start(), calls=%async_computation.18 | async-start | bytes 18874368 | tf_op jit(solution)/shard_map/reduce_scatter | solution.py:256
  923.0 4.3 copy-start.7
Sparse Core Ops, SparseCore 0:
  10.4 48.1 all-gather.4
  60.5 27.7 all-gather.6
  148.0 83.1 all-reduce.7
  233.5 88.7 all-gather.8
  324.0 54.2 all-gather.10
  387.6 86.1 all-reduce.9
  505.7 85.1 all-reduce.11
  634.8 40.6 reduce-scatter.6
  698.1 83.4 all-reduce.13
  784.9 70.5 reduce-scatter.10
  858.9 64.0 reduce-scatter.4
  926.4 116.1 reduce-scatter.8

commit v3 on v2

--- a/solution.py
+++ b/solution.py
@@ -239,6 +239,40 @@
     parts = values_in.reshape(seqs, each, ctx_size, span, width).transpose(2, 0, 1, 3, 4)
     parts = lax.all_to_all(parts, "ctx", 0, 0, tiled=True)
     return parts.transpose(1, 3, 0, 2, 4).reshape(seqs, span, ctx_size * each, width)
+
+
+def heads_to_own(values_in, seqs, ctx_size, tensor):
+    count, length, width = values_in.shape
+    each, span = count // seqs, length // ctx_size
+    parts = values_in.reshape(seqs, each, ctx_size, span, width).transpose(2, 0, 3, 1, 4)
+    parts = parts.reshape(ctx_size * tensor, seqs * span // tensor, each * width)
+    parts = lax.all_to_all(parts, ("ctx", "tp"), 0, 0, tiled=True)
+    parts = parts.reshape(ctx_size, tensor, -1, each * width).transpose(2, 1, 0, 3)
+    return parts.reshape(seqs * span // tensor, tensor * ctx_size * each * width)
+
+
+def own_to_heads(values_in, seqs, ctx_size, tensor, width):
+    own = values_in.shape[0]
+    each = values_in.shape[1] // (tensor * ctx_size * width)
+    span = own * tensor // seqs
+    parts = values_in.reshape(own, tensor, ctx_size, each * width).transpose(2, 1, 0, 3)
+    parts = parts.reshape(ctx_size * tensor, own, each * width)
+    parts = lax.all_to_all(parts, ("ctx", "tp"), 0, 0, tiled=True)
+    parts = parts.reshape(ctx_size, seqs, span, each, width).transpose(1, 3, 0, 2, 4)
+    return parts.reshape(seqs * each, ctx_size * span, width)
+
+
+def tensor_scatter(values_in):
+    tensor = lax.axis_size("tp")
+    parts = values_in.astype(jnp.bfloat16).reshape(tensor, -1, values_in.shape[1])
+    parts = lax.all_to_all(parts, "tp", 0, 0, tiled=True)
+    return jnp.sum(parts.astype(jnp.float32), axis=0)
+
+
+def tensor_gather(values_in):
+    tensor = lax.axis_size("tp")
+    parts = jnp.broadcast_to(values_in[None], (tensor,) + values_in.shape)
+    return lax.all_to_all(parts, "tp", 0, 0, tiled=True)
 
 
 def tensor_sum(values_in):
@@ -280,7 +314,8 @@
     q_shape = (seq_count, seq_span, heads_here, HEAD_DIM)
 
     w_qkv = gather_rows(jnp.concatenate([q_weight, k_weight, v_weight], axis=1))
-    w_out = gather_rows(o_weight)
+    out_rows = tensor_gather(o_weight).transpose(1, 0, 2).reshape(-1, model_width)
+    w_out = gather_rows(out_rows)
     w_gate_up = gather_rows(jnp.concatenate([gate_weight, up_weight], axis=1))
     w_down = gather_rows(down_weight)
     gain_table = gather_rows(norm_gains).astype(jnp.float32)
@@ -289,6 +324,9 @@
     gain_attn = gain_table[:, 2]
     gain_ffn = gain_table[:, 3]
     inputs = tokens.reshape(row_count, model_width)
+    own_count = row_count // tensor
+    own_start = lax.axis_index("tp") * own_count
+    own_inputs = lax.dynamic_slice_in_dim(inputs, own_start, own_count).astype(jnp.float32)
     cosine_table, sine_table = rope_tables(seq_span, position)
 
     qkv_proj = jnp.dot(inputs, w_qkv, preferred_element_type=jnp.float32)
@@ -309,11 +347,12 @@
         ctx_size,
     )
     attended, log_total = attn_fwd(packed)
+    att_own = heads_to_own(attended, seq_count, ctx_size, tensor)
+    branch_a = contract_cols(att_own, w_out)
+    a_rs = rms_scale(branch_a)
+    middle_own = own_inputs + branch_a * a_rs * gain_attn
+    middle_low = tensor_gather(middle_own.astype(jnp.bfloat16)).reshape(row_count, model_width)
     att_low = to_positions(attended, seq_count, ctx_size).reshape(row_count, local_width)
-    branch_a = tensor_sum(contract_cols(att_low, w_out))
-    a_rs = rms_scale(branch_a)
-    middle = inputs.astype(jnp.float32) + branch_a * a_rs * gain_attn
-    middle_low = middle.astype(jnp.bfloat16)
     gate_up = jnp.dot(middle_low, w_gate_up, preferred_element_type=jnp.float32)
     gate_proj = gate_up[:, :hidden]
     up_proj = gate_up[:, hidden:]
@@ -321,7 +360,7 @@
     branch_f = tensor_sum(contract_cols(activated, w_down))
     f_rs = rms_scale(branch_f)
     block_out = (
-        (middle + branch_f * f_rs * gain_ffn)
+        (middle_low.astype(jnp.float32) + branch_f * f_rs * gain_ffn)
         .astype(jnp.bfloat16)
         .reshape(seq_count, seq_span, model_width)
     )
@@ -340,19 +379,25 @@
     )
     d_up = (d_act * gate_proj * sigmoid_gate).astype(jnp.bfloat16)
     d_gate_up = jnp.concatenate([d_gate, d_up], axis=1)
-    d_middle = grad_out + tensor_sum(contract_cols(d_gate_up, w_gate_up))
+    own_grad_out = lax.dynamic_slice_in_dim(
+        cotangent.reshape(row_count, model_width), own_start, own_count
+    ).astype(jnp.float32)
+    d_middle = own_grad_out + tensor_scatter(contract_cols(d_gate_up, w_gate_up))
     gate_up_part = contract_rows(middle_low, d_gate_up)
     gate_up_grad = scatter_rows(gate_up_part).astype(jnp.float32)
     attn_gain_part = jnp.sum(d_middle * branch_a * a_rs, axis=0)
     attn_dot = jnp.sum(d_middle * gain_attn * branch_a, axis=1, keepdims=True)
-    d_branch_a = norm_backward(d_middle, branch_a, a_rs, gain_attn, attn_dot, model_width).astype(
+    d_branch_own = norm_backward(d_middle, branch_a, a_rs, gain_attn, attn_dot, model_width).astype(
         jnp.bfloat16
     )
-    d_att = jnp.dot(d_branch_a, w_out, preferred_element_type=jnp.float32).astype(jnp.bfloat16)
+    d_att_own = jnp.dot(d_branch_own, w_out, preferred_element_type=jnp.float32).astype(jnp.bfloat16)
+    d_att = own_to_heads(d_att_own, seq_count, ctx_size, tensor, HEAD_DIM)
+    d_branch_own, d_att = lax.optimization_barrier((d_branch_own, d_att))
+    d_branch_a = tensor_gather(d_branch_own).reshape(row_count, model_width)
     out_part = contract_rows(d_branch_a, att_low)
     out_grad = scatter_rows(out_part).astype(jnp.float32)
     d_packed = to_positions(
-        attn_bwd(packed, attended, to_heads(d_att.reshape(q_shape), ctx_size), log_total),
+        attn_bwd(packed, attended, d_att, log_total),
         seq_count,
         ctx_size,
     )
@@ -369,27 +414,30 @@
         (0, feature_start),
     )
     is_first = lax.axis_index("tp") == 0
-    post_gains = jnp.where(is_first, jnp.stack([attn_gain_part, ffn_gain_part]), 0.0)
-    query_dot, key_dot, gain_sum = lax.psum(
-        (
-            jnp.sum(d_q_norm * gain_q * q_proj, axis=1),
-            jnp.sum(d_k_norm * gain_k * k_proj, axis=1),
-            jnp.concatenate([pre_gains, post_gains], axis=0),
-        ),
+    post_gains = jnp.stack([attn_gain_part, jnp.where(is_first, ffn_gain_part, 0.0)])
+    query_dot, key_dot = lax.psum(
+        (jnp.sum(d_q_norm * gain_q * q_proj, axis=1), jnp.sum(d_k_norm * gain_k * k_proj, axis=1)),
         "tp",
     )
+    d_query = norm_backward(d_q_norm, q_proj, q_rs, gain_q, query_dot[:, None], model_width)
+    d_key = norm_backward(d_k_norm, k_proj, k_rs, gain_k, key_dot[:, None], model_width)
+    d_qkv = jnp.concatenate(
+        [d_query.astype(jnp.bfloat16), d_key.astype(jnp.bfloat16), d_value], axis=1
+    )
+    token_own = d_middle + tensor_scatter(contract_cols(d_qkv, w_qkv))
+    token_grad = (
+        tensor_gather(token_own.astype(jnp.bfloat16))
+        .astype(jnp.float32)
+        .reshape(seq_count, seq_span, model_width)
+    )
+    gain_part, d_qkv = lax.optimization_barrier(
+        (jnp.concatenate([pre_gains, post_gains], axis=0), d_qkv)
+    )
+    gain_sum = lax.psum(gain_part, "tp")
     gain_high = gain_sum.astype(jnp.bfloat16)
     gain_rest = (gain_sum - gain_high.astype(jnp.float32)).astype(jnp.bfloat16)
     gain_terms = jnp.concatenate([gain_high, gain_rest], axis=0).T
     gain_terms = jnp.pad(gain_terms, ((0, 0), (0, HEAD_DIM - gain_terms.shape[1])))
-    d_query = norm_backward(d_q_norm, q_proj, q_rs, gain_q, query_dot[:, None], model_width)
-    d_key = norm_backward(d_k_norm, k_proj, k_rs, gain_k, key_dot[:, None], model_width)
-    d_qkv = jnp.concatenate(
-        [d_query.astype(jnp.bfloat16), d_key.astype(jnp.bfloat16), d_value], axis=1
-    )
-    token_grad = (d_middle + tensor_sum(contract_cols(d_qkv, w_qkv))).reshape(
-        seq_count, seq_span, model_width
-    )
     qkv_part = contract_rows(inputs, d_qkv).astype(jnp.bfloat16)
     last_grad = scatter_rows(jnp.concatenate([qkv_part, gain_terms], axis=1)).astype(jnp.float32)
     qkv_grad = last_grad[:, : 3 * local_width]

time: 1060 us -> 883 us (0.83)
  waiting for transfers between devices: 734 us -> 290 us
  blocking collectives: 75.4 us -> 304 us
  local copies, waits for them, and re-layouts: 40.1 us -> 58.3 us
  starting transfers between devices: 8.87 us -> 21.9 us
    all_to_all x0 -> x5, blocking collectives: none -> 229 us  [the longest x3 134 us: tensor_gather(): return lax.all_to_all(parts, 'tp', 0, 0, tiled=True)]
    psum x4 -> x1, waiting for transfers between devices: 296 us -> 86.3 us  [tensor_sum(): total = lax.psum(values_in, 'tp')]
    reduce_scatter x4, waiting for transfers between devices: 248 us -> 60.8 us  [scatter_rows(): lax.psum_scatter(values_in, weight_axes, scatter_dimension=0, tiled=True)]
    all_gather x4, waiting for transfers between devices: 164 us -> 38.4 us  [gather_rows(): return lax.all_gather(values_in, weight_axes, axis=0, tiled=True)]
    all_to_all x0 -> x3, waiting for transfers between devices: none -> 72.4 us  [the longest x1 43.3 us: tensor_gather(): return lax.all_to_all(parts, 'tp', 0, 0, tiled=True)]
    psum x0 -> x1, blocking collectives: none -> 16.7 us  [per_device(): gain_sum = lax.psum(gain_part, 'tp')]
    all_to_all x0 -> x3, starting transfers between devices: none -> 12.6 us  [the longest x1 4.76 us: heads_to_own(): parts = lax.all_to_all(parts, ('ctx', 'tp'), 0, 0, tiled=True)]
    all_to_all x2 -> x1, blocking collectives: 35.6 us -> 27.9 us  [to_heads(): parts = lax.all_to_all(parts, 'ctx', 0, 0, tiled=True)]
  transfers between devices with their start and end apart: 14 -> 14, of which waited for: 12 -> 9; matrix products, arithmetic and copies ran while one was open for 13% -> 17% of each run, Pallas kernels for 1% -> 2%
where the time goes in v3:
time: 883 us; the launch traced here: 874 us
  blocking collectives  304 us (34%)
  waiting for transfers between devices  290 us (33%)
  matrix products  108 us (12%)
  local copies, waits for them, and re-layouts  58.3 us (7%)
  other arithmetic  55.3 us (6%)
  starting transfers between devices  21.9 us (2%)
  Pallas kernels  20.9 us (2%)
  between operations  14.5 us (2%)
    all_to_all x3, blocking collectives, tensor_gather(): return lax.all_to_all(parts, 'tp', 0, 0, tiled=True)  134 us
    all_to_all x2, blocking collectives, tensor_scatter(): parts = lax.all_to_all(parts, 'tp', 0, 0, tiled=True)  94.9 us
    psum x1, waiting for transfers between devices, tensor_sum(): total = lax.psum(values_in, 'tp')  86.3 us
    dot_general x8, matrix products, dot_f32(): lax.dot_general(left, right, (((left_dim,), (right_dim,)), ((), ())), pre...  71.7 us
    reduce_scatter x4, waiting for transfers between devices, scatter_rows(): lax.psum_scatter(values_in, weight_axes, scatter_dimension=0, tiled=True)  60.8 us
    all_to_all x1, waiting for transfers between devices, tensor_gather(): return lax.all_to_all(parts, 'tp', 0, 0, tiled=True)  43.3 us
    all_gather x4, waiting for transfers between devices, gather_rows(): return lax.all_gather(values_in, weight_axes, axis=0, tiled=True)  38.4 us
    all_to_all x2, waiting for transfers between devices, to_positions(): parts = lax.all_to_all(parts, 'ctx', 0, 0, tiled=True)  31.7 us
  transfers between devices with their start and end apart: 14, of which 9 were waited for; matrix products, arithmetic and copies ran while one was open for 17% of the time, Pallas kernels for 2%

profile of v3, /device:TPU:0, one launch (start us, length us, event | category | flops | bytes accessed | tf_op | source)
XLA Modules:
  0.0 873.8 jit_solution(975836184421709491)
XLA Ops:
  7.2 2.1 pad_maximum_fusion.7
  10.6 32.0 %all_to_all.55 = bf16[4,256,512]{1,2,0:T(8,128)(2,1)} all-to-all(bf16[4,256,512]{1,2,0:T(8,128)(2,1)S(1)} %broadcast_in_dim.15), channel_id=1, replica_groups=mesh['fsdp'=2,'ctx'=4,'tp'=4] {'tp'}, dimensions={0} | all-to-all | bytes 2097152 | tf_op jit(solution)/shard_map/all_to_all | solution.py:275
  42.7 2.8 pad_maximum_fusion.3
  46.1 9.2 %all_gather.16 = bf16[2048,4]{0,1:T(4,128)(2,1)S(1)} all-gather(bf16[256,4]{0,1:T(4,128)(2,1)S(1)} %copy-done.18), channel_id=1, replica_groups=mesh['fsdp'=2,'ctx'=4,'tp'=4] {'fsdp','ctx'}, dimensions={0}, use_global_device_ids=true | all-gather | bytes 18432 | tf_op jit(solution)/shard_map/all_gather | solution.py:285
  58.7 6.2 convolution_bitcast_fusion
  66.0 11.7 %all-reduce.2 = (f32[512]{0:T(512)S(1)}, f32[512]{0:T(512)S(1)}) all-reduce(f32[512]{0:T(512)S(1)} %get-tuple-element.73, f32[512]{0:T(512)S(1)} %get-tuple-element.72), channel_id=1, replica_groups=mesh['fsdp'=2,'ctx'=4,'tp'=4] {'tp'}, use_global_device_ids=true, to_apply=%region_1.0 | all-reduce | flops 1024 | bytes 8192 | tf_op jit(solution)/shard_map/psum | solution.py:336
  79.9 2.4 copy.81
  82.3 2.4 copy.82
  84.6 2.2 fusion.38
  86.9 2.4 copy.80
  89.2 2.4 copy.79
  91.6 2.1 copy.65
  93.7 4.0 add_convert_fusion
  97.6 4.2 concatenate.52
  101.8 27.9 %all_to_all.56 = bf16[4,1,1,512,384]{4,3,2,1,0:T(8,128)(2,1)} all-to-all(bf16[4,1,1,512,384]{4,3,2,1,0:T(8,128)(2,1)} %bitcast.143), channel_id=1, replica_groups=mesh['fsdp'=2,'ctx'=4,'tp'=4] {'ctx'}, dimensions={0} | all-to-all | bytes 3145728 | tf_op jit(solution)/shard_map/all_to_all | solution.py:232
  129.7 9.0 %attn_fwd.1 = (bf16[1,2048,128]{2,1,0:T(8,128)(2,1)}, f32[1,1,2048]{2,1,0:T(1,128)}) custom-call(bf16[1,2048,384]{2,1,0:T(8,128)(2,1)} %bitcast.134, bf16[1,2048,384]{2,1,0:T(8,128)(2,1)} %bitcast.135, bf16[1,2048,384]{2,1,0:T(8,128)(2,1)} %bitcast.136), custom_call_target="tpu_custom_call" | custom-call | flops 1073741824 | bytes 2621440 | tf_op jit(solution)/shard_map/attn_fwd/pallas_call | solution.py:118
  138.8 4.8 all-to-all-start.1
  143.6 15.6 %all-to-all-done.1 = bf16[16,128,128]{2,1,0:T(8,128)(2,1)} async-done(((bf16[16,128,128]{2,1,0:T(8,128)(2,1)}), bf16[16,128,128]{2,1,0:T(8,128)(2,1)}, u32[]{:S(2)}, u32[]{:S(2)}) %all-to-all-start.1) | async-done | bytes 524320 | tf_op jit(solution)/shard_map/all_to_all | solution.py:249
  161.2 4.9 multiply_reduce_fusion.4
  168.7 51.9 %all_to_all.57 = bf16[4,128,2048]{2,1,0:T(8,128)(2,1)} all-to-all(bf16[4,128,2048]{2,1,0:T(8,128)(2,1)S(1)} %broadcast_in_dim.16), channel_id=1, replica_groups=mesh['fsdp'=2,'ctx'=4,'tp'=4] {'tp'}, dimensions={0} | all-to-all | bytes 4194304 | tf_op jit(solution)/shard_map/all_to_all | solution.py:275
  220.5 12.6 %fusion.41 = f32[512,4096]{1,0:T(8,128)S(1)} fusion(bf16[512,2048]{1,0:T(8,128)(2,1)} %bitcast.141, bf16[2048,4096]{1,0:T(8,128)(2,1)} %all-gather.9.cloned.1.call-done), kind=kOutput, calls=%fused_computation.118 | convolution fusion | flops 8589934592 | bytes 27262976 | tf_op jit(solution)/shard_map/dot_general | solution.py:356
  233.1 3.2 copy-done.4
  236.3 2.5 multiply_convert_fusion.2
  238.9 36.9 %all-gather.11.cloned.1.call-done = bf16[2048,2048]{1,0:T(8,128)(2,1)} async-done(((bf16[256,2048]{1,0:T(8,128)(2,1)}), bf16[2048,2048]{1,0:T(8,128)(2,1)}) %all-gather.11.cloned.1.call-update) | async-done | bytes 8388624 | tf_op jit(solution)/shard_map/all_gather | solution.py:285
  275.8 9.9 %convolution_convert_fusion.5 = bf16[512,2048]{1,0:T(8,128)(2,1)} fusion(bf16[512,2048]{1,0:T(8,128)(2,1)} %multiply_convert_fusion.2, bf16[2048,2048]{1,0:T(8,128)(2,1)} %all-gather.11.cloned.1.call-done), kind=kOutput, calls=%fused_computation.34 | convolution fusion | flops 4296015872 | bytes 12582912 | tf_op jit(solution)/shard_map/dot_general | solution.py:54
  285.7 86.3 %all-reduce.5.cloned.1.call-done = bf16[512,2048]{1,0:T(8,128)(2,1)} async-done(((bf16[512,2048]{1,0:T(8,128)(2,1)}), bf16[512,2048]{1,0:T(8,128)(2,1)}) %all-reduce.5.cloned.1.call-update) | async-done | bytes 2097168 | tf_op jit(solution)/shard_map/psum | solution.py:280
  372.0 2.2 fusion.6
  374.2 5.4 fusion.13
  380.2 10.8 %multiply_convert_fusion.1 = (bf16[512,2048]{1,0:T(8,128)(2,1)S(1)}, bf16[512,2048]{1,0:T(8,128)(2,1)}) fusion(f32[512,4096]{1,0:T(8,128)S(1)} %copy-done.5, bf16[2048,2048]{1,0:T(8,128)(2,1)} %all-gather.11.cloned.1.call-done, bf16[512,2048]{1,0:T(8,128)(2,1)S(1)} %copy-done.7, bf16[1,512,2048]{2,1,0:T(8,128)(2,1)} %param.19, ...), kind=kOutput, calls=%fused_computation.28 | convolution fusion | flops 4316987392 | bytes 25180160 | tf_op jit(solution)/shard_map/dot_general | solution.py:375
  391.0 13.8 %convolution_convert_fusion.6 = bf16[512,2048]{1,0:T(8,128)(2,1)S(1)} fusion(bf16[2048,4096]{1,0:T(8,128)(2,1)} %all-gather.9.cloned.1.call-done, bf16[512,2048]{1,0:T(8,128)(2,1)} %get-tuple-element.81, bf16[512,2048]{1,0:T(8,128)(2,1)S(1)} %get-tuple-element.80), kind=kOutput, calls=%fused_computation.35 | convolution fusion | flops 8599371776 | bytes 23068672 | tf_op jit(solution)/shard_map/dot_general | solution.py:54
  404.8 51.3 %all_to_all.58 = bf16[4,128,2048]{2,1,0:T(8,128)(2,1)S(1)} all-to-all(bf16[4,128,2048]{2,1,0:T(8,128)(2,1)S(1)} %bitcast.150), channel_id=1, replica_groups=mesh['fsdp'=2,'ctx'=4,'tp'=4] {'tp'}, dimensions={0} | all-to-all | bytes 4194304 | tf_op jit(solution)/shard_map/all_to_all | solution.py:268
  458.7 7.1 convolution_convert_fusion.7
  465.8 2.2 reshape.326
  469.9 4.2 all-to-all-start.5
  476.2 13.5 %all-to-all-done.5 = bf16[16,128,128]{2,1,0:T(8,128)(2,1)} async-done(((bf16[16,128,128]{2,1,0:T(8,128)(2,1)}), bf16[16,128,128]{2,1,0:T(8,128)(2,1)}, u32[]{:S(2)}, u32[]{:S(2)}) %all-to-all-start.5) | async-done | bytes 524320 | tf_op jit(solution)/shard_map/all_to_all | solution.py:260
  489.8 4.2 all-to-all-start.10
  494.0 8.8 %all-to-all-done.10 = bf16[4,1,1,512,128]{3,4,2,1,0:T(8,128)(2,1)} async-done(((bf16[4,1,1,512,128]{3,4,2,1,0:T(8,128)(2,1)}), bf16[4,1,1,512,128]{3,4,2,1,0:T(8,128)(2,1)}, u32[]{:S(2)}, u32[]{:S(2)}) %all-to-all-start.10) | async-done | bytes 524320 | tf_op jit(solution)/shard_map/all_to_all | solution.py:240
  504.1 50.6 %all_to_all.59 = bf16[4,128,2048]{2,1,0:T(8,128)(2,1)S(1)} all-to-all(bf16[4,128,2048]{2,1,0:T(8,128)(2,1)S(1)} %broadcast_in_dim.21), channel_id=1, replica_groups=mesh['fsdp'=2,'ctx'=4,'tp'=4] {'tp'}, dimensions={0} | all-to-all | bytes 4194304 | tf_op jit(solution)/shard_map/all_to_all | solution.py:275
  554.8 3.7 convolution_convert_fusion.3
  558.9 11.2 %convolution_convert_fusion.1 = bf16[2048,2048]{1,0:T(8,128)(2,1)} fusion(bf16[512,2048]{1,0:T(8,128)(2,1)} %multiply_convert_fusion.2, bf16[512,2048]{1,0:T(8,128)(2,1)} %all-reduce.5.cloned.1.call-done, bf16[1,512,2048]{2,1,0:T(8,128)(2,1)} %param.19, f32[512]{0:T(512)S(1)} %get-tuple-element.69, f32[512]{0:T(512)S(1)} %get-tuple-element.122, ...), kind=kOutput, calls=%fused_computation.8 | convolution fusion | flops 4307550208 | bytes 14694400 | tf_op jit(solution)/shard_map/dot_general | solution.py:54
  570.1 11.9 %attn_bwd.1 = bf16[1,2048,384]{2,1,0:T(8,128)(2,1)} custom-call(bf16[1,2048,384]{2,1,0:T(8,128)(2,1)} %bitcast.137, bf16[1,2048,384]{2,1,0:T(8,128)(2,1)} %bitcast.138, bf16[1,2048,384]{2,1,0:T(8,128)(2,1)} %bitcast.139, bf16[1,2048,128]{2,1,0:T(8,128)(2,1)} %get-tuple-element.16.att_ref, bf16[1,2048,128]{2,1,0:T(8,128)(2,1)} %bitcast.27.grad_ref, ...), custom_call_target="tpu_custom_call" | custom-call | flops 2684354560 | bytes 4718592 | tf_op jit(solution)/shard_map/attn_bwd/pallas_call | solution.py:196
  582.0 4.4 all-to-all-start.6
  586.4 22.9 %all-to-all-done.6 = bf16[4,1,1,512,384]{4,3,2,1,0:T(8,128)(2,1)} async-done(((bf16[4,1,1,512,384]{4,3,2,1,0:T(8,128)(2,1)}), bf16[4,1,1,512,384]{4,3,2,1,0:T(8,128)(2,1)}, u32[]{:S(2)}, u32[]{:S(2)}) %all-to-all-start.6) | async-done | bytes 1572896 | tf_op jit(solution)/shard_map/all_to_all | solution.py:240
  609.3 3.0 slice_convert_fusion.2
  612.3 2.1 copy.73
  614.4 5.1 multiply_subtract_fusion.1
  620.8 2.6 copy.71
  623.4 2.9 pad_maximum_fusion.6
  626.2 2.5 copy.72
  628.8 2.7 fusion.24
  631.5 9.5 %all-reduce.1 = (f32[512]{0:T(512)S(1)}, f32[512]{0:T(512)S(1)}) all-reduce(f32[512]{0:T(512)S(1)} %get-tuple-element.70, f32[512]{0:T(512)S(1)} %get-tuple-element.63), channel_id=1, replica_groups=mesh['fsdp'=2,'ctx'=4,'tp'=4] {'tp'}, use_global_device_ids=true, to_apply=%region_13.14 | all-reduce | flops 1024 | bytes 8192 | tf_op jit(solution)/shard_map/psum | solution.py:418
  641.0 2.3 subtract_convert_fusion.1
  644.4 16.7 %psum.47 = f32[4,2048]{1,0:T(4,128)S(1)} all-reduce(f32[4,2048]{1,0:T(4,128)S(1)} %pad_maximum_fusion.8), channel_id=1, replica_groups=mesh['fsdp'=2,'ctx'=4,'tp'=4] {'tp'}, use_global_device_ids=true, to_apply=%region_19.20 | all-reduce | flops 8192 | bytes 65536 | tf_op jit(solution)/shard_map/psum | solution.py:436
  661.2 5.3 fusion.2
  666.4 3.7 fusion.1
  671.7 15.4 %convolution_convert_fusion = bf16[2048,4096]{1,0:T(8,128)(2,1)} fusion(bf16[512,2048]{1,0:T(8,128)(2,1)S(1)} %bitcast.142, bf16[512,2048]{1,0:T(8,128)(2,1)} %get-tuple-element.81, bf16[512,2048]{1,0:T(8,128)(2,1)} %copy-done.19), kind=kOutput, calls=%fused_computation | convolution fusion | flops 8606711808 | bytes 23068672 | tf_op jit(solution)/shard_map/dot_general | solution.py:54
  688.7 7.5 convolution_convert_fusion.4
  696.3 43.6 %all_to_all.60 = bf16[4,128,2048]{2,1,0:T(8,128)(2,1)S(1)} all-to-all(bf16[4,128,2048]{2,1,0:T(8,128)(2,1)S(1)} %bitcast.148), channel_id=1, replica_groups=mesh['fsdp'=2,'ctx'=4,'tp'=4] {'tp'}, dimensions={0} | all-to-all | bytes 4194304 | tf_op jit(solution)/shard_map/all_to_all | solution.py:268
  743.1 3.6 all-to-all-start.8
  748.5 43.3 %all-to-all-done.8 = bf16[4,128,2048]{2,1,0:T(8,128)(2,1)S(1)} async-done(((bf16[4,128,2048]{2,1,0:T(8,128)(2,1)}), bf16[4,128,2048]{2,1,0:T(8,128)(2,1)S(1)}, u32[]{:S(2)}, u32[]{:S(2)}) %all-to-all-start.8) | async-done | bytes 2097184 | tf_op jit(solution)/shard_map/all_to_all | solution.py:275
  791.8 2.5 bitcast_convert_fusion
  794.3 2.8 convert_element_type.190
  802.2 60.8 %reduce-scatter.9.cloned.1.call-done = bf16[256,4096]{1,0:T(8,128)(2,1)} async-done(((bf16[2048,4096]{1,0:T(8,128)(2,1)}), bf16[256,4096]{1,0:T(8,128)(2,1)}) %reduce-scatter.9.cloned.1.call-update) | async-done | bytes 2097168 | tf_op jit(solution)/shard_map/reduce_scatter | solution.py:290
  863.0 4.1 fusion.36
  (104 shorter events, 37.8 us)
Async XLA Ops:
  7.2 35.5 %copy-start.17 = (bf16[256,2048]{1,0:T(8,128)(2,1)S(1)}, bf16[256,2048]{1,0:T(8,128)(2,1)}, u32[]{:S(2)}) copy-start(bf16[256,2048]{1,0:T(8,128)(2,1)} %param.16) | copy-start | bytes 3145732
  7.2 51.5 %all-gather.5.cloned.1.call-start = ((), (), s32[]{:S(2)}) async-start(), calls=%async_computation.15 | async-start | bytes 7077888 | tf_op jit(solution)/shard_map/all_gather | solution.py:285
  9.4 151.8 %all-gather.7.cloned.1.call-start = ((), (), s32[]{:S(2)}) async-start(), calls=%async_computation.16 | async-start | bytes 9437184 | tf_op jit(solution)/shard_map/all_gather | solution.py:285
  42.6 3.5 copy-start.18
  42.6 177.9 %all-gather.9.cloned.1.call-start = ((), (), s32[]{:S(2)}) async-start(), calls=%async_computation.17 | async-start | bytes 18874368 | tf_op jit(solution)/shard_map/all_gather | solution.py:285
  45.5 230.3 %all-gather.11.cloned.1.call-start = ((), (), s32[]{:S(2)}) async-start(), calls=%async_computation.18 | async-start | bytes 9437184 | tf_op jit(solution)/shard_map/all_gather | solution.py:285
  138.8 20.4 %all-to-all-start.1 = ((bf16[16,128,128]{2,1,0:T(8,128)(2,1)}), bf16[16,128,128]{2,1,0:T(8,128)(2,1)}, u32[]{:S(2)}, u32[]{:S(2)}) async-start(bf16[16,128,128]{2,1,0:T(8,128)(2,1)} %bitcast.151), calls=%async_computation.1 | async-start | bytes 1048576 | tf_op jit(solution)/shard_map/all_to_all | solution.py:249
  143.6 228.4 %all-reduce.5.cloned.1.call-start = ((), (), s32[]{:S(2)}) async-start(), calls=%async_computation.19 | async-start | bytes 4194304 | tf_op jit(solution)/shard_map/psum | solution.py:280
  166.1 1.0 copy-start.2
  233.1 3.2 copy-start.4
  372.0 7.7 copy-start.7
  374.2 6.0 copy-start.5
  391.0 13.8 %copy-start.19 = (bf16[512,2048]{1,0:T(8,128)(2,1)}, bf16[512,2048]{1,0:T(8,128)(2,1)S(1)}, u32[]{:S(2)}) copy-start(bf16[512,2048]{1,0:T(8,128)(2,1)S(1)} %get-tuple-element.80) | copy-start | bytes 6291460
  404.8 51.7 %copy-start.3 = (f32[128,2048]{1,0:T(8,128)S(1)}, f32[128,2048]{1,0:T(8,128)}, u32[]{:S(2)}) copy-start(f32[128,2048]{1,0:T(8,128)} %copy-done.2) | copy-start | bytes 3145732
  404.8 51.7 %copy-start.9 = (bf16[1,512,2048]{2,1,0:T(8,128)(2,1)S(1)}, bf16[1,512,2048]{2,1,0:T(8,128)(2,1)}, u32[]{:S(2)}) copy-start(bf16[1,512,2048]{2,1,0:T(8,128)(2,1)} %param.19) | copy-start | bytes 6291460
  456.6 1.0 copy-start
  457.9 0.8 copy-start.10
  469.9 19.8 %all-to-all-start.5 = ((bf16[16,128,128]{2,1,0:T(8,128)(2,1)}), bf16[16,128,128]{2,1,0:T(8,128)(2,1)}, u32[]{:S(2)}, u32[]{:S(2)}) async-start(bf16[16,128,128]{2,1,0:T(8,128)(2,1)} %bitcast.154), calls=%async_computation.5 | async-start | bytes 1048576 | tf_op jit(solution)/shard_map/all_to_all | solution.py:260
  489.8 13.0 %all-to-all-start.10 = ((bf16[4,1,1,512,128]{3,4,2,1,0:T(8,128)(2,1)}), bf16[4,1,1,512,128]{3,4,2,1,0:T(8,128)(2,1)}, u32[]{:S(2)}, u32[]{:S(2)}) async-start(bf16[4,1,1,512,128]{3,4,2,1,0:T(8,128)(2,1)} %copy.74), calls=%async_computation.11 | async-start | bytes 1048576 | tf_op jit(solution)/shard_map/all_to_all | solution.py:240
  493.9 252.8 %reduce-scatter.7.cloned.1.call-start = ((), (), s32[]{:S(2)}) async-start(), calls=%async_computation.21 | async-start | bytes 2359296 | tf_op jit(solution)/shard_map/reduce_scatter | solution.py:290
  558.5 235.9 %reduce-scatter.11.cloned.1.call-start = ((), (), s32[]{:S(2)}) async-start(), calls=%async_computation.23 | async-start | bytes 9437184 | tf_op jit(solution)/shard_map/reduce_scatter | solution.py:290
  582.0 27.3 %all-to-all-start.6 = ((bf16[4,1,1,512,384]{4,3,2,1,0:T(8,128)(2,1)}), bf16[4,1,1,512,384]{4,3,2,1,0:T(8,128)(2,1)}, u32[]{:S(2)}, u32[]{:S(2)}) async-start(bf16[4,1,1,512,384]{4,3,2,1,0:T(8,128)(2,1)} %bitcast.158), calls=%async_computation.6 | async-start | bytes 3145728 | tf_op jit(solution)/shard_map/all_to_all | solution.py:240
  586.4 210.8 %reduce-scatter.5.cloned.1.call-start = ((), (), s32[]{:S(2)}) async-start(), calls=%async_computation.20 | async-start | bytes 7667712 | tf_op jit(solution)/shard_map/reduce_scatter | solution.py:290
  641.0 3.3 copy-start.15
  643.3 0.8 copy-start.11
  643.3 1.0 copy-start.13
  670.1 1.6 copy-start.6
  670.1 192.9 %reduce-scatter.9.cloned.1.call-start = ((), (), s32[]{:S(2)}) async-start(), calls=%async_computation.22 | async-start | bytes 18874368 | tf_op jit(solution)/shard_map/reduce_scatter | solution.py:290
  687.1 1.1 copy-start.12
  687.1 1.4 copy-start.14
  687.1 1.6 copy-start.16
  696.2 44.0 %copy-start.1 = (f32[128,2048]{1,0:T(8,128)S(1)}, f32[128,2048]{1,0:T(8,128)}, u32[]{:S(2)}) copy-start(f32[128,2048]{1,0:T(8,128)} %copy-done) | copy-start | bytes 3145732
  743.1 48.7 %all-to-all-start.8 = ((bf16[4,128,2048]{2,1,0:T(8,128)(2,1)}), bf16[4,128,2048]{2,1,0:T(8,128)(2,1)S(1)}, u32[]{:S(2)}, u32[]{:S(2)}) async-start(bf16[4,128,2048]{2,1,0:T(8,128)(2,1)} %broadcast_in_dim.18), calls=%async_computation.8 | async-start | bytes 4194304 | tf_op jit(solution)/shard_map/all_to_all | solution.py:275
  797.1 4.3 copy-start.8
Sparse Core Ops, SparseCore 0:
  10.5 48.1 all-gather.4
  60.5 57.8 all-gather.6
  121.0 98.7 all-gather.8
  221.5 54.2 all-gather.10
  285.8 86.1 all-reduce.4
  558.6 42.0 reduce-scatter.6
  604.1 71.5 reduce-scatter.10
  679.1 64.0 reduce-scatter.4
  746.8 116.1 reduce-scatter.8

commit v4 on v3

--- a/solution.py
+++ b/solution.py
@@ -315,8 +315,9 @@
 
     w_qkv = gather_rows(jnp.concatenate([q_weight, k_weight, v_weight], axis=1))
     out_rows = tensor_gather(o_weight).transpose(1, 0, 2).reshape(-1, model_width)
-    w_out = gather_rows(out_rows)
-    w_gate_up = gather_rows(jnp.concatenate([gate_weight, up_weight], axis=1))
+    w_middle = gather_rows(jnp.concatenate([out_rows, gate_weight, up_weight], axis=1))
+    w_out = w_middle[:, :model_width]
+    w_gate_up = w_middle[:, model_width:]
     w_down = gather_rows(down_weight)
     gain_table = gather_rows(norm_gains).astype(jnp.float32)
     gain_q = lax.dynamic_slice_in_dim(gain_table[:, 0], feature_start, local_width)
@@ -394,8 +395,6 @@
     d_att = own_to_heads(d_att_own, seq_count, ctx_size, tensor, HEAD_DIM)
     d_branch_own, d_att = lax.optimization_barrier((d_branch_own, d_att))
     d_branch_a = tensor_gather(d_branch_own).reshape(row_count, model_width)
-    out_part = contract_rows(d_branch_a, att_low)
-    out_grad = scatter_rows(out_part).astype(jnp.float32)
     d_packed = to_positions(
         attn_bwd(packed, attended, d_att, log_total),
         seq_count,
@@ -424,27 +423,26 @@
     d_qkv = jnp.concatenate(
         [d_query.astype(jnp.bfloat16), d_key.astype(jnp.bfloat16), d_value], axis=1
     )
-    token_own = d_middle + tensor_scatter(contract_cols(d_qkv, w_qkv))
-    token_grad = (
-        tensor_gather(token_own.astype(jnp.bfloat16))
-        .astype(jnp.float32)
-        .reshape(seq_count, seq_span, model_width)
-    )
-    gain_part, d_qkv = lax.optimization_barrier(
-        (jnp.concatenate([pre_gains, post_gains], axis=0), d_qkv)
-    )
-    gain_sum = lax.psum(gain_part, "tp")
-    gain_high = gain_sum.astype(jnp.bfloat16)
-    gain_rest = (gain_sum - gain_high.astype(jnp.float32)).astype(jnp.bfloat16)
+    gain_part = jnp.concatenate([pre_gains, post_gains], axis=0)
+    gain_high = gain_part.astype(jnp.bfloat16)
+    gain_rest = (gain_part - gain_high.astype(jnp.float32)).astype(jnp.bfloat16)
     gain_terms = jnp.concatenate([gain_high, gain_rest], axis=0).T
     gain_terms = jnp.pad(gain_terms, ((0, 0), (0, HEAD_DIM - gain_terms.shape[1])))
-    qkv_part = contract_rows(inputs, d_qkv).astype(jnp.bfloat16)
-    last_grad = scatter_rows(jnp.concatenate([qkv_part, gain_terms], axis=1)).astype(jnp.float32)
-    qkv_grad = last_grad[:, : 3 * local_width]
-    gain_grad = (
-        last_grad[:, 3 * local_width : 3 * local_width + 4]
-        + last_grad[:, 3 * local_width + 4 : 3 * local_width + 8]
-    )
+    out_part = contract_rows(d_branch_a, att_low).astype(jnp.bfloat16)
+    out_and_gains = scatter_rows(
+        jnp.concatenate([out_part, gain_terms], axis=1)
+    ).astype(jnp.float32)
+    out_grad = out_and_gains[:, :local_width]
+    token_own = d_middle + tensor_scatter(contract_cols(d_qkv, w_qkv))
+    qkv_part = contract_rows(inputs, d_qkv)
+    qkv_grad = scatter_rows(qkv_part).astype(jnp.float32)
+    gain_rows = out_and_gains[:, local_width : local_width + 4] + (
+        out_and_gains[:, local_width + 4 : local_width + 8]
+    )
+    token_low = tensor_gather(token_own.astype(jnp.bfloat16))
+    token_grad = token_low.astype(jnp.float32).reshape(seq_count, seq_span, model_width)
+    gain_rows, _ = lax.optimization_barrier((gain_rows, token_low))
+    gain_grad = lax.psum(gain_rows, "tp")
     return (
         block_out,
         token_grad,

time: 883 us -> 917 us (1.039)
  waiting for transfers between devices: 290 us -> 373 us
  blocking collectives: 304 us -> 248 us
    all_to_all x3 -> x1, blocking collectives: 134 us -> 51.7 us  [tensor_gather(): return lax.all_to_all(parts, 'tp', 0, 0, tiled=True)]
    reduce_scatter x4, waiting for transfers between devices: 60.8 us -> 122 us  [scatter_rows(): lax.psum_scatter(values_in, weight_axes, scatter_dimension=0, tiled=True)]
    all_to_all x1 -> x3, waiting for transfers between devices: 43.3 us -> 99.2 us  [tensor_gather(): return lax.all_to_all(parts, 'tp', 0, 0, tiled=True)]
    all_to_all x2 -> x1, waiting for transfers between devices: 31.7 us -> 0.01 us  [to_positions(): parts = lax.all_to_all(parts, 'ctx', 0, 0, tiled=True)]
    all_to_all x0 -> x1, blocking collectives: none -> 24.5 us  [to_positions(): parts = lax.all_to_all(parts, 'ctx', 0, 0, tiled=True)]
    all_to_all x1 -> x3, starting transfers between devices: 3.61 us -> 14.4 us  [tensor_gather(): return lax.all_to_all(parts, 'tp', 0, 0, tiled=True)]
    unnamed x48 -> x54, local copies, waits for them, and re-layouts: 23.7 us -> 21.5 us
    all_gather x4 -> x3, waiting for transfers between devices: 38.4 us -> 37 us  [gather_rows(): return lax.all_gather(values_in, weight_axes, axis=0, tiled=True)]
where the time goes in v4:
time: 917 us; the launch traced here: 908 us
  waiting for transfers between devices  373 us (41%)
  blocking collectives  248 us (27%)
  matrix products  111 us (12%)
  local copies, waits for them, and re-layouts  61.5 us (7%)
  other arithmetic  51.3 us (6%)
  starting transfers between devices  27.7 us (3%)
  Pallas kernels  20.9 us (2%)
  between operations  14.8 us (2%)
    reduce_scatter x4, waiting for transfers between devices, scatter_rows(): lax.psum_scatter(values_in, weight_axes, scatter_dimension=0, tiled=True)  122 us
    all_to_all x3, waiting for transfers between devices, tensor_gather(): return lax.all_to_all(parts, 'tp', 0, 0, tiled=True)  99.2 us
    all_to_all x2, blocking collectives, tensor_scatter(): parts = lax.all_to_all(parts, 'tp', 0, 0, tiled=True)  98.3 us
    psum x1, waiting for transfers between devices, tensor_sum(): total = lax.psum(values_in, 'tp')  84.4 us
    dot_general x8, matrix products, dot_f32(): lax.dot_general(left, right, (((left_dim,), (right_dim,)), ((), ())), pre...  72.4 us
    all_to_all x1, blocking collectives, tensor_gather(): return lax.all_to_all(parts, 'tp', 0, 0, tiled=True)  51.7 us
    all_gather x3, waiting for transfers between devices, gather_rows(): return lax.all_gather(values_in, weight_axes, axis=0, tiled=True)  37 us
    all_to_all x1, blocking collectives, to_heads(): parts = lax.all_to_all(parts, 'ctx', 0, 0, tiled=True)  33.1 us
  transfers between devices with their start and end apart: 14, of which 9 were waited for; matrix products, arithmetic and copies ran while one was open for 17% of the time, Pallas kernels for 2%

profile of v4, /device:TPU:0, one launch (start us, length us, event | category | flops | bytes accessed | tf_op | source)
XLA Modules:
  0.0 907.8 jit_solution(16988167143750550479)
XLA Ops:
  7.2 2.1 pad_maximum_fusion.7
  11.4 6.3 all-to-all-start.2
  19.7 23.7 %all-to-all-done.2 = bf16[4,256,512]{2,1,0:T(8,128)(2,1)S(1)} async-done(((bf16[4,256,512]{2,1,0:T(8,128)(2,1)}), bf16[4,256,512]{2,1,0:T(8,128)(2,1)S(1)}, u32[]{:S(2)}, u32[]{:S(2)}) %all-to-all-start.2) | async-done | bytes 1048608 | tf_op jit(solution)/shard_map/all_to_all | solution.py:275
  44.8 2.9 pad_maximum_fusion.1
  48.4 9.2 %all_gather.13 = bf16[2048,4]{0,1:T(4,128)(2,1)S(1)} all-gather(bf16[256,4]{0,1:T(4,128)(2,1)S(1)} %copy-done.19), channel_id=1, replica_groups=mesh['fsdp'=2,'ctx'=4,'tp'=4] {'fsdp','ctx'}, dimensions={0}, use_global_device_ids=true | all-gather | bytes 18432 | tf_op jit(solution)/shard_map/all_gather | solution.py:285
  59.5 6.2 convolution_bitcast_fusion
  66.8 10.9 %all-reduce.2 = (f32[512]{0:T(512)S(1)}, f32[512]{0:T(512)S(1)}) all-reduce(f32[512]{0:T(512)S(1)} %get-tuple-element.81, f32[512]{0:T(512)S(1)} %get-tuple-element.80), channel_id=1, replica_groups=mesh['fsdp'=2,'ctx'=4,'tp'=4] {'tp'}, use_global_device_ids=true, to_apply=%region_1.0 | all-reduce | flops 1024 | bytes 8192 | tf_op jit(solution)/shard_map/psum | solution.py:337
  79.9 2.4 copy.101
  82.3 2.4 copy.102
  84.7 2.2 fusion.54
  86.9 2.4 copy.103
  89.2 2.4 copy.104
  93.6 4.0 add_convert_fusion
  97.6 4.2 concatenate.52
  101.8 33.1 %all_to_all.55 = bf16[4,1,1,512,384]{4,3,2,1,0:T(8,128)(2,1)} all-to-all(bf16[4,1,1,512,384]{4,3,2,1,0:T(8,128)(2,1)} %bitcast.139), channel_id=1, replica_groups=mesh['fsdp'=2,'ctx'=4,'tp'=4] {'ctx'}, dimensions={0} | all-to-all | bytes 3145728 | tf_op jit(solution)/shard_map/all_to_all | solution.py:232
  134.9 9.0 attn_fwd.1
  143.9 4.2 all-to-all-start.1
  148.2 15.5 %all-to-all-done.1 = bf16[16,128,128]{2,1,0:T(8,128)(2,1)} async-done(((bf16[16,128,128]{2,1,0:T(8,128)(2,1)}), bf16[16,128,128]{2,1,0:T(8,128)(2,1)}, u32[]{:S(2)}, u32[]{:S(2)}) %all-to-all-start.1) | async-done | bytes 524320 | tf_op jit(solution)/shard_map/all_to_all | solution.py:249
  163.8 2.0 copy.85
  165.8 37.0 %all-gather.6.cloned.1.call-done = bf16[2048,6144]{0,1:T(8,128)(2,1)} async-done(((bf16[256,6144]{0,1:T(8,128)(2,1)}), bf16[2048,6144]{0,1:T(8,128)(2,1)}) %all-gather.6.cloned.1.call-update) | async-done | bytes 25165840 | tf_op jit(solution)/shard_map/all_gather | solution.py:285
  202.8 4.9 multiply_reduce_fusion.4
  209.7 51.7 %all_to_all.56 = bf16[4,128,2048]{2,1,0:T(8,128)(2,1)S(1)} all-to-all(bf16[4,128,2048]{2,1,0:T(8,128)(2,1)S(1)} %broadcast_in_dim.16), channel_id=1, replica_groups=mesh['fsdp'=2,'ctx'=4,'tp'=4] {'tp'}, dimensions={0} | all-to-all | bytes 4194304 | tf_op jit(solution)/shard_map/all_to_all | solution.py:275
  261.4 15.2 %fusion.2 = f32[512,4096]{1,0:T(8,128)} fusion(bf16[512,2048]{1,0:T(8,128)(2,1)S(1)} %bitcast.136, bf16[2048,6144]{0,1:T(8,128)(2,1)} %all-gather.6.cloned.1.call-done), kind=kOutput, calls=%fused_computation.3 | convolution fusion | flops 8589934592 | bytes 27262976 | tf_op jit(solution)/shard_map/dot_general | solution.py:357
  276.6 6.0 multiply_convert_fusion.2
  282.6 9.9 %convolution_convert_fusion.5 = bf16[512,2048]{1,0:T(8,128)(2,1)} fusion(bf16[512,2048]{1,0:T(8,128)(2,1)} %multiply_convert_fusion.2, bf16[2048,2048]{1,0:T(8,128)(2,1)} %all-gather.8.cloned.1.call-done), kind=kOutput, calls=%fused_computation.43 | convolution fusion | flops 4296015872 | bytes 12582912 | tf_op jit(solution)/shard_map/dot_general | solution.py:54
  292.5 84.4 %all-reduce.5.cloned.1.call-done = bf16[512,2048]{1,0:T(8,128)(2,1)} async-done(((bf16[512,2048]{1,0:T(8,128)(2,1)}), bf16[512,2048]{1,0:T(8,128)(2,1)}) %all-reduce.5.cloned.1.call-update) | async-done | bytes 2097168 | tf_op jit(solution)/shard_map/psum | solution.py:280
  376.9 2.2 fusion.13
  379.1 5.4 fusion.20
  385.1 10.0 %multiply_convert_fusion.1 = (bf16[512,2048]{1,0:T(8,128)(2,1)S(1)}, bf16[512,2048]{1,0:T(8,128)(2,1)S(1)}) fusion(f32[512,4096]{1,0:T(8,128)S(1)} %copy-done.4, bf16[2048,2048]{1,0:T(8,128)(2,1)} %all-gather.8.cloned.1.call-done, bf16[512,2048]{1,0:T(8,128)(2,1)S(1)} %copy-done.7, bf16[1,512,2048]{2,1,0:T(8,128)(2,1)} %param.19, ...), kind=kOutput, calls=%fused_computation.35 | convolution fusion | flops 4316987392 | bytes 25180160 | tf_op jit(solution)/shard_map/dot_general | solution.py:376
  395.2 14.1 %fusion.21 = bf16[512,2048]{1,0:T(8,128)(2,1)S(1)} fusion(bf16[2048,6144]{0,1:T(8,128)(2,1)} %all-gather.6.cloned.1.call-done, bf16[512,2048]{1,0:T(8,128)(2,1)S(1)} %get-tuple-element.87, bf16[512,2048]{1,0:T(8,128)(2,1)S(1)} %get-tuple-element.86), kind=kOutput, calls=%fused_computation.40 | convolution fusion | flops 8599371776 | bytes 23068672 | tf_op jit(solution)/shard_map/dot_general | solution.py:54
  409.3 51.3 %all_to_all.57 = bf16[4,128,2048]{2,1,0:T(8,128)(2,1)S(1)} all-to-all(bf16[4,128,2048]{2,1,0:T(8,128)(2,1)S(1)} %bitcast.144), channel_id=1, replica_groups=mesh['fsdp'=2,'ctx'=4,'tp'=4] {'tp'}, dimensions={0} | all-to-all | bytes 4194304 | tf_op jit(solution)/shard_map/all_to_all | solution.py:268
  463.2 7.1 fusion.25
  470.3 2.2 reshape.326
  474.4 4.2 all-to-all-start.5
  478.7 2.0 copy.95
  480.7 13.5 %all-to-all-done.5 = bf16[16,128,128]{2,1,0:T(8,128)(2,1)} async-done(((bf16[16,128,128]{2,1,0:T(8,128)(2,1)}), bf16[16,128,128]{2,1,0:T(8,128)(2,1)}, u32[]{:S(2)}, u32[]{:S(2)}) %all-to-all-start.5) | async-done | bytes 524320 | tf_op jit(solution)/shard_map/all_to_all | solution.py:260
  494.3 4.5 all-to-all-start.10
  498.8 11.9 %attn_bwd.1 = bf16[1,2048,384]{2,1,0:T(8,128)(2,1)} custom-call(bf16[1,2048,384]{2,1,0:T(8,128)(2,1)} %bitcast.132, bf16[1,2048,384]{2,1,0:T(8,128)(2,1)} %bitcast.133, bf16[1,2048,384]{2,1,0:T(8,128)(2,1)} %bitcast.134, bf16[1,2048,128]{2,1,0:T(8,128)(2,1)} %get-tuple-element.15.att_ref, bf16[1,2048,128]{2,1,0:T(8,128)(2,1)} %bitcast.27.grad_ref, ...), custom_call_target="tpu_custom_call" | custom-call | flops 2684354560 | bytes 4718592 | tf_op jit(solution)/shard_map/attn_bwd/pallas_call | solution.py:196
  510.7 24.5 %all_to_all.58 = bf16[4,1,1,512,384]{4,3,2,1,0:T(8,128)(2,1)} all-to-all(bf16[4,1,1,512,384]{4,3,2,1,0:T(8,128)(2,1)} %bitcast.150), channel_id=1, replica_groups=mesh['fsdp'=2,'ctx'=4,'tp'=4] {'ctx'}, dimensions={0} | all-to-all | bytes 3145728 | tf_op jit(solution)/shard_map/all_to_all | solution.py:240
  535.2 2.6 broadcast_in_dim.19
  537.8 4.5 all-to-all-start.9
  542.3 2.4 slice_convert_fusion.2
  548.0 2.5 copy.93
  550.5 2.9 pad_maximum_fusion.5
  553.4 2.6 copy.92
  556.0 2.1 fusion.38
  558.3 32.1 %all-to-all-done.9 = bf16[4,128,2048]{2,1,0:T(8,128)(2,1)} async-done(((bf16[4,128,2048]{2,1,0:T(8,128)(2,1)}), bf16[4,128,2048]{2,1,0:T(8,128)(2,1)}, u32[]{:S(2)}, u32[]{:S(2)}) %all-to-all-start.9) | async-done | bytes 2097184 | tf_op jit(solution)/shard_map/all_to_all | solution.py:275
  590.4 3.0 convolution_convert_fusion.3
  595.3 11.2 %convolution_convert_fusion.1 = bf16[2048,2048]{1,0:T(8,128)(2,1)} fusion(bf16[512,2048]{1,0:T(8,128)(2,1)} %multiply_convert_fusion.2, bf16[512,2048]{1,0:T(8,128)(2,1)} %all-reduce.5.cloned.1.call-done, bf16[1,512,2048]{2,1,0:T(8,128)(2,1)} %param.19, f32[512]{0:T(512)S(1)} %get-tuple-element.77, f32[512]{0:T(512)S(1)} %get-tuple-element.128, ...), kind=kOutput, calls=%fused_computation.10 | convolution fusion | flops 4307550208 | bytes 14694400 | tf_op jit(solution)/shard_map/dot_general | solution.py:54
  606.6 2.1 copy.94
  608.6 10.1 %all-reduce.1 = (f32[512]{0:T(512)S(1)}, f32[512]{0:T(512)S(1)}) all-reduce(f32[512]{0:T(512)S(1)} %get-tuple-element.78, f32[512]{0:T(512)S(1)} %get-tuple-element.71), channel_id=1, replica_groups=mesh['fsdp'=2,'ctx'=4,'tp'=4] {'tp'}, use_global_device_ids=true, to_apply=%region_13.14 | all-reduce | flops 1024 | bytes 8192 | tf_op jit(solution)/shard_map/psum | solution.py:417
  618.7 2.1 subtract_convert_fusion.1
  621.8 7.2 fusion.8
  630.7 14.6 %convolution_convert_fusion = bf16[2048,4096]{1,0:T(8,128)(2,1)} fusion(bf16[512,2048]{1,0:T(8,128)(2,1)S(1)} %bitcast.137, bf16[512,2048]{1,0:T(8,128)(2,1)} %copy-done.21, bf16[512,2048]{1,0:T(8,128)(2,1)} %copy-done.20), kind=kOutput, calls=%fused_computation | convolution fusion | flops 8606711808 | bytes 23068672 | tf_op jit(solution)/shard_map/dot_general | solution.py:54
  646.9 7.5 convolution_convert_fusion.4
  654.5 47.0 %all_to_all.59 = bf16[4,128,2048]{2,1,0:T(8,128)(2,1)S(1)} all-to-all(bf16[4,128,2048]{2,1,0:T(8,128)(2,1)S(1)} %bitcast.143), channel_id=1, replica_groups=mesh['fsdp'=2,'ctx'=4,'tp'=4] {'tp'}, dimensions={0} | all-to-all | bytes 4194304 | tf_op jit(solution)/shard_map/all_to_all | solution.py:268
  704.7 3.6 all-to-all-start.8
  711.3 43.4 %all-to-all-done.8 = bf16[4,128,2048]{2,1,0:T(8,128)(2,1)S(1)} async-done(((bf16[4,128,2048]{2,1,0:T(8,128)(2,1)}), bf16[4,128,2048]{2,1,0:T(8,128)(2,1)S(1)}, u32[]{:S(2)}, u32[]{:S(2)}) %all-to-all-start.8) | async-done | bytes 2097184 | tf_op jit(solution)/shard_map/all_to_all | solution.py:275
  754.7 10.4 %psum.47 = f32[256,4]{0,1:T(4,128)} all-reduce(f32[256,4]{0,1:T(4,128)S(1)} %slice_add_fusion), channel_id=1, replica_groups=mesh['fsdp'=2,'ctx'=4,'tp'=4] {'tp'}, use_global_device_ids=true, to_apply=%region_23.24 | all-reduce | flops 1024 | bytes 8192 | tf_op jit(solution)/shard_map/psum | solution.py:445
  765.1 2.5 bitcast_convert_fusion
  767.6 2.8 convert_element_type.190
  770.4 6.5 reduce-scatter.5.cloned.1.call-done
  781.1 115.6 %reduce-scatter.9.cloned.1.call-done = bf16[256,4096]{1,0:T(8,128)(2,1)} async-done(((bf16[2048,4096]{1,0:T(8,128)(2,1)}), bf16[256,4096]{1,0:T(8,128)(2,1)}) %reduce-scatter.9.cloned.1.call-update) | async-done | bytes 2097168 | tf_op jit(solution)/shard_map/reduce_scatter | solution.py:290
  896.7 4.1 fusion.53
  (108 shorter events, 40.4 us)
Async XLA Ops:
  7.2 10.6 %copy-start.10 = (bf16[256,2048]{1,0:T(8,128)(2,1)S(1)}, bf16[256,2048]{1,0:T(8,128)(2,1)}, u32[]{:S(2)}) copy-start(bf16[256,2048]{1,0:T(8,128)(2,1)} %param.15) | copy-start | bytes 3145732
  7.2 52.3 %all-gather.4.cloned.1.call-start = ((), (), s32[]{:S(2)}) async-start(), calls=%async_computation.15 | async-start | bytes 7077888 | tf_op jit(solution)/shard_map/all_gather | solution.py:285
  11.4 32.1 %all-to-all-start.2 = ((bf16[4,256,512]{2,1,0:T(8,128)(2,1)}), bf16[4,256,512]{2,1,0:T(8,128)(2,1)S(1)}, u32[]{:S(2)}, u32[]{:S(2)}) async-start(bf16[4,256,512]{2,1,0:T(8,128)(2,1)} %broadcast_in_dim.15), calls=%async_computation.2 | async-start | bytes 2097152 | tf_op jit(solution)/shard_map/all_to_all | solution.py:275
  17.7 185.1 %all-gather.6.cloned.1.call-start = ((), (), s32[]{:S(2)}) async-start(), calls=%async_computation.16 | async-start | bytes 28311552 | tf_op jit(solution)/shard_map/all_gather | solution.py:285
  44.8 3.7 copy-start.19
  47.7 234.9 %all-gather.8.cloned.1.call-start = ((), (), s32[]{:S(2)}) async-start(), calls=%async_computation.17 | async-start | bytes 9437184 | tf_op jit(solution)/shard_map/all_gather | solution.py:285
  143.9 19.8 %all-to-all-start.1 = ((bf16[16,128,128]{2,1,0:T(8,128)(2,1)}), bf16[16,128,128]{2,1,0:T(8,128)(2,1)}, u32[]{:S(2)}, u32[]{:S(2)}) async-start(bf16[16,128,128]{2,1,0:T(8,128)(2,1)} %bitcast.145), calls=%async_computation.1 | async-start | bytes 1048576 | tf_op jit(solution)/shard_map/all_to_all | solution.py:249
  148.2 228.7 %all-reduce.5.cloned.1.call-start = ((), (), s32[]{:S(2)}) async-start(), calls=%async_computation.18 | async-start | bytes 4194304 | tf_op jit(solution)/shard_map/psum | solution.py:280
  207.7 53.6 %copy-start.2 = (f32[128,2048]{1,0:T(8,128)}, f32[128,2048]{1,0:T(8,128)S(1)}, u32[]{:S(2)}) copy-start(f32[128,2048]{1,0:T(8,128)S(1)} %get-tuple-element.133) | copy-start | bytes 3145732
  261.4 15.2 %copy-start.5 = (bf16[4,128,2048]{2,1,0:T(8,128)(2,1)}, bf16[4,128,2048]{2,1,0:T(8,128)(2,1)S(1)}, u32[]{:S(2)}) copy-start(bf16[4,128,2048]{2,1,0:T(8,128)(2,1)S(1)} %all_to_all.56) | copy-start | bytes 6291460
  376.9 7.7 copy-start.7
  379.1 6.0 copy-start.4
  395.1 14.1 %copy-start.20 = (bf16[512,2048]{1,0:T(8,128)(2,1)}, bf16[512,2048]{1,0:T(8,128)(2,1)S(1)}, u32[]{:S(2)}) copy-start(bf16[512,2048]{1,0:T(8,128)(2,1)S(1)} %get-tuple-element.86) | copy-start | bytes 6291460
  395.2 14.1 %copy-start.21 = (bf16[512,2048]{1,0:T(8,128)(2,1)}, bf16[512,2048]{1,0:T(8,128)(2,1)S(1)}, u32[]{:S(2)}) copy-start(bf16[512,2048]{1,0:T(8,128)(2,1)S(1)} %get-tuple-element.87) | copy-start | bytes 6291460
  409.3 51.7 %copy-start.3 = (f32[128,2048]{1,0:T(8,128)S(1)}, f32[128,2048]{1,0:T(8,128)}, u32[]{:S(2)}) copy-start(f32[128,2048]{1,0:T(8,128)} %copy-done.2) | copy-start | bytes 3145732
  409.3 51.7 %copy-start.8 = (bf16[1,512,2048]{2,1,0:T(8,128)(2,1)S(1)}, bf16[1,512,2048]{2,1,0:T(8,128)(2,1)}, u32[]{:S(2)}) copy-start(bf16[1,512,2048]{2,1,0:T(8,128)(2,1)} %param.19) | copy-start | bytes 6291460
  461.0 1.0 copy-start
  462.4 0.8 copy-start.9
  474.4 19.8 %all-to-all-start.5 = ((bf16[16,128,128]{2,1,0:T(8,128)(2,1)}), bf16[16,128,128]{2,1,0:T(8,128)(2,1)}, u32[]{:S(2)}, u32[]{:S(2)}) async-start(bf16[16,128,128]{2,1,0:T(8,128)(2,1)} %bitcast.148), calls=%async_computation.5 | async-start | bytes 1048576 | tf_op jit(solution)/shard_map/all_to_all | solution.py:260
  494.3 16.4 %all-to-all-start.10 = ((bf16[4,1,1,512,128]{3,4,2,1,0:T(8,128)(2,1)}), bf16[4,1,1,512,128]{3,4,2,1,0:T(8,128)(2,1)}, u32[]{:S(2)}, u32[]{:S(2)}) async-start(bf16[4,1,1,512,128]{3,4,2,1,0:T(8,128)(2,1)} %copy.95), calls=%async_computation.11 | async-start | bytes 1048576 | tf_op jit(solution)/shard_map/all_to_all | solution.py:240
  537.8 52.6 %all-to-all-start.9 = ((bf16[4,128,2048]{2,1,0:T(8,128)(2,1)}), bf16[4,128,2048]{2,1,0:T(8,128)(2,1)}, u32[]{:S(2)}, u32[]{:S(2)}) async-start(bf16[4,128,2048]{2,1,0:T(8,128)(2,1)} %broadcast_in_dim.19), calls=%async_computation.10 | async-start | bytes 4194304 | tf_op jit(solution)/shard_map/all_to_all | solution.py:275
  542.3 166.0 %reduce-scatter.7.cloned.1.call-start = ((), (), s32[]{:S(2)}) async-start(), calls=%async_computation.20 | async-start | bytes 2949120 | tf_op jit(solution)/shard_map/reduce_scatter | solution.py:290
  542.3 2.4 copy-start.11
  595.3 172.3 %reduce-scatter.11.cloned.1.call-start = ((), (), s32[]{:S(2)}) async-start(), calls=%async_computation.22 | async-start | bytes 9437184 | tf_op jit(solution)/shard_map/reduce_scatter | solution.py:290
  606.5 170.4 %reduce-scatter.5.cloned.1.call-start = ((), (), s32[]{:S(2)}) async-start(), calls=%async_computation.19 | async-start | bytes 7077888 | tf_op jit(solution)/shard_map/reduce_scatter | solution.py:290
  618.7 3.1 copy-start.16
  618.7 3.1 copy-start.18
  620.9 0.8 copy-start.12
  620.9 1.0 copy-start.14
  629.0 1.7 copy-start.6
  629.1 267.6 %reduce-scatter.9.cloned.1.call-start = ((), (), s32[]{:S(2)}) async-start(), calls=%async_computation.21 | async-start | bytes 18874368 | tf_op jit(solution)/shard_map/reduce_scatter | solution.py:290
  645.4 1.2 copy-start.13
  645.4 1.4 copy-start.15
  645.4 1.6 copy-start.17
  654.5 47.3 %copy-start.1 = (f32[128,2048]{1,0:T(8,128)S(1)}, f32[128,2048]{1,0:T(8,128)}, u32[]{:S(2)}) copy-start(f32[128,2048]{1,0:T(8,128)} %copy-done) | copy-start | bytes 3145732
  704.7 50.0 %all-to-all-start.8 = ((bf16[4,128,2048]{2,1,0:T(8,128)(2,1)}), bf16[4,128,2048]{2,1,0:T(8,128)(2,1)S(1)}, u32[]{:S(2)}, u32[]{:S(2)}) async-start(bf16[4,128,2048]{2,1,0:T(8,128)(2,1)} %broadcast_in_dim.18), calls=%async_computation.8 | async-start | bytes 4194304 | tf_op jit(solution)/shard_map/all_to_all | solution.py:275
Sparse Core Ops, SparseCore 0:
  10.5 48.1 all-gather.3
  61.1 141.6 all-gather.5
  204.7 52.7 all-gather.7
  292.6 84.2 all-reduce.4
  595.4 41.6 reduce-scatter.6
  640.4 71.4 reduce-scatter.10
  715.3 61.5 reduce-scatter.4
  780.5 116.1 reduce-scatter.8

commit v5 on v4

--- a/solution.py
+++ b/solution.py
@@ -241,16 +241,6 @@
     return parts.transpose(1, 3, 0, 2, 4).reshape(seqs, span, ctx_size * each, width)
 
 
-def heads_to_own(values_in, seqs, ctx_size, tensor):
-    count, length, width = values_in.shape
-    each, span = count // seqs, length // ctx_size
-    parts = values_in.reshape(seqs, each, ctx_size, span, width).transpose(2, 0, 3, 1, 4)
-    parts = parts.reshape(ctx_size * tensor, seqs * span // tensor, each * width)
-    parts = lax.all_to_all(parts, ("ctx", "tp"), 0, 0, tiled=True)
-    parts = parts.reshape(ctx_size, tensor, -1, each * width).transpose(2, 1, 0, 3)
-    return parts.reshape(seqs * span // tensor, tensor * ctx_size * each * width)
-
-
 def own_to_heads(values_in, seqs, ctx_size, tensor, width):
     own = values_in.shape[0]
     each = values_in.shape[1] // (tensor * ctx_size * width)
@@ -273,12 +263,6 @@
     tensor = lax.axis_size("tp")
     parts = jnp.broadcast_to(values_in[None], (tensor,) + values_in.shape)
     return lax.all_to_all(parts, "tp", 0, 0, tiled=True)
-
-
-def tensor_sum(values_in):
-    values_in = values_in.astype(jnp.bfloat16)
-    total = lax.psum(values_in, "tp")
-    return total.astype(jnp.float32)
 
 
 def gather_rows(values_in):
@@ -314,11 +298,12 @@
     q_shape = (seq_count, seq_span, heads_here, HEAD_DIM)
 
     w_qkv = gather_rows(jnp.concatenate([q_weight, k_weight, v_weight], axis=1))
+    w_out_here = gather_rows(o_weight)
+    w_ffn = gather_rows(jnp.concatenate([gate_weight, up_weight, down_weight], axis=1))
+    w_gate_up = w_ffn[:, : 2 * hidden]
+    w_down = w_ffn[:, 2 * hidden :]
     out_rows = tensor_gather(o_weight).transpose(1, 0, 2).reshape(-1, model_width)
-    w_middle = gather_rows(jnp.concatenate([out_rows, gate_weight, up_weight], axis=1))
-    w_out = w_middle[:, :model_width]
-    w_gate_up = w_middle[:, model_width:]
-    w_down = gather_rows(down_weight)
+    w_out = gather_rows(out_rows)
     gain_table = gather_rows(norm_gains).astype(jnp.float32)
     gain_q = lax.dynamic_slice_in_dim(gain_table[:, 0], feature_start, local_width)
     gain_k = lax.dynamic_slice_in_dim(gain_table[:, 1], feature_start, local_width)
@@ -348,44 +333,74 @@
         ctx_size,
     )
     attended, log_total = attn_fwd(packed)
-    att_own = heads_to_own(attended, seq_count, ctx_size, tensor)
-    branch_a = contract_cols(att_own, w_out)
-    a_rs = rms_scale(branch_a)
-    middle_own = own_inputs + branch_a * a_rs * gain_attn
-    middle_low = tensor_gather(middle_own.astype(jnp.bfloat16)).reshape(row_count, model_width)
     att_low = to_positions(attended, seq_count, ctx_size).reshape(row_count, local_width)
-    gate_up = jnp.dot(middle_low, w_gate_up, preferred_element_type=jnp.float32)
-    gate_proj = gate_up[:, :hidden]
-    up_proj = gate_up[:, hidden:]
-    activated = (jax.nn.silu(gate_proj) * up_proj).astype(jnp.bfloat16)
-    branch_f = tensor_sum(contract_cols(activated, w_down))
-    f_rs = rms_scale(branch_f)
-    block_out = (
-        (middle_low.astype(jnp.float32) + branch_f * f_rs * gain_ffn)
-        .astype(jnp.bfloat16)
-        .reshape(seq_count, seq_span, model_width)
-    )
-    grad_out = cotangent.reshape(row_count, model_width).astype(jnp.float32)
-    ffn_gain_part = jnp.sum(grad_out * branch_f * f_rs, axis=0)
-    ffn_dot = jnp.sum(grad_out * gain_ffn * branch_f, axis=1, keepdims=True)
-    d_branch_f = norm_backward(grad_out, branch_f, f_rs, gain_ffn, ffn_dot, model_width).astype(
-        jnp.bfloat16
-    )
-    down_part = contract_rows(d_branch_f, activated)
+
+    half_count = own_count // 2
+    half_rows = half_count * tensor
+    part = contract_cols(att_low, w_out_here).astype(jnp.bfloat16)
+    part = part.reshape(tensor, 2, half_count, model_width)
+    branch_a = [tensor_scatter(part[:, half].reshape(half_rows, model_width)) for half in range(2)]
+    grad_out_rows = cotangent.reshape(tensor, 2, half_count, model_width)
+    middle_low, gate_proj, up_proj, activated, branch_f = [], [], [], [], []
+    for half in range(2):
+        middle = own_inputs[half * half_count : (half + 1) * half_count] + (
+            branch_a[half] * rms_scale(branch_a[half]) * gain_attn
+        )
+        middle_low.append(
+            tensor_gather(middle.astype(jnp.bfloat16)).reshape(half_rows, model_width)
+        )
+        gate_up = jnp.dot(middle_low[half], w_gate_up, preferred_element_type=jnp.float32)
+        gate_proj.append(gate_up[:, :hidden])
+        up_proj.append(gate_up[:, hidden:])
+        activated.append((jax.nn.silu(gate_proj[half]) * up_proj[half]).astype(jnp.bfloat16))
+        part = contract_cols(activated[half], w_down)
+        branch_f.append(tensor_scatter(part).astype(jnp.bfloat16))
+    branch_f = [
+        tensor_gather(branch_f[half])
+        .reshape(half_rows, model_width)
+        .astype(jnp.float32)
+        for half in range(2)
+    ]
+    block_halves, gain_halves, d_branch_f, d_gate_up, d_middle = [], [], [], [], []
+    for half in range(2):
+        if half:
+            branch_f[half], part = lax.optimization_barrier((branch_f[half], part))
+        f_rs = rms_scale(branch_f[half])
+        block_halves.append(
+            (middle_low[half].astype(jnp.float32) + branch_f[half] * f_rs * gain_ffn)
+            .astype(jnp.bfloat16)
+            .reshape(tensor, 1, half_count, model_width)
+        )
+        grad_out = grad_out_rows[:, half].reshape(half_rows, model_width).astype(jnp.float32)
+        gain_halves.append(jnp.sum(grad_out * branch_f[half] * f_rs, axis=0))
+        ffn_dot = jnp.sum(grad_out * gain_ffn * branch_f[half], axis=1, keepdims=True)
+        d_branch_f.append(
+            norm_backward(grad_out, branch_f[half], f_rs, gain_ffn, ffn_dot, model_width).astype(
+                jnp.bfloat16
+            )
+        )
+        d_act = jnp.dot(d_branch_f[half], w_down, preferred_element_type=jnp.float32)
+        gate, up = gate_proj[half], up_proj[half]
+        sigmoid_gate = jax.nn.sigmoid(gate)
+        d_gate = d_act * up * sigmoid_gate * (1.0 + gate * (1.0 - sigmoid_gate))
+        d_up = d_act * gate * sigmoid_gate
+        d_gate_up.append(
+            jnp.concatenate([d_gate.astype(jnp.bfloat16), d_up.astype(jnp.bfloat16)], axis=1)
+        )
+        part = contract_cols(d_gate_up[half], w_gate_up)
+        d_middle.append(tensor_scatter(part))
+    block_out = jnp.concatenate(block_halves, axis=1).reshape(seq_count, seq_span, model_width)
+    ffn_gain_part = gain_halves[0] + gain_halves[1]
+    down_part = contract_rows(jnp.concatenate(d_branch_f), jnp.concatenate(activated))
     down_grad = scatter_rows(down_part).astype(jnp.float32)
-    d_act = jnp.dot(d_branch_f, w_down, preferred_element_type=jnp.float32)
-    sigmoid_gate = jax.nn.sigmoid(gate_proj)
-    d_gate = (d_act * up_proj * sigmoid_gate * (1.0 + gate_proj * (1.0 - sigmoid_gate))).astype(
-        jnp.bfloat16
-    )
-    d_up = (d_act * gate_proj * sigmoid_gate).astype(jnp.bfloat16)
-    d_gate_up = jnp.concatenate([d_gate, d_up], axis=1)
+    gate_up_part = contract_rows(jnp.concatenate(middle_low), jnp.concatenate(d_gate_up))
+    gate_up_grad = scatter_rows(gate_up_part).astype(jnp.float32)
     own_grad_out = lax.dynamic_slice_in_dim(
         cotangent.reshape(row_count, model_width), own_start, own_count
     ).astype(jnp.float32)
-    d_middle = own_grad_out + tensor_scatter(contract_cols(d_gate_up, w_gate_up))
-    gate_up_part = contract_rows(middle_low, d_gate_up)
-    gate_up_grad = scatter_rows(gate_up_part).astype(jnp.float32)
+    d_middle = own_grad_out + jnp.concatenate(d_middle)
+    branch_a = jnp.concatenate(branch_a)
+    a_rs = rms_scale(branch_a)
     attn_gain_part = jnp.sum(d_middle * branch_a * a_rs, axis=0)
     attn_dot = jnp.sum(d_middle * gain_attn * branch_a, axis=1, keepdims=True)
     d_branch_own = norm_backward(d_middle, branch_a, a_rs, gain_attn, attn_dot, model_width).astype(
@@ -423,22 +438,19 @@
     d_qkv = jnp.concatenate(
         [d_query.astype(jnp.bfloat16), d_key.astype(jnp.bfloat16), d_value], axis=1
     )
+    out_part = contract_rows(d_branch_a, att_low)
+    out_grad = scatter_rows(out_part).astype(jnp.float32)
     gain_part = jnp.concatenate([pre_gains, post_gains], axis=0)
     gain_high = gain_part.astype(jnp.bfloat16)
     gain_rest = (gain_part - gain_high.astype(jnp.float32)).astype(jnp.bfloat16)
     gain_terms = jnp.concatenate([gain_high, gain_rest], axis=0).T
     gain_terms = jnp.pad(gain_terms, ((0, 0), (0, HEAD_DIM - gain_terms.shape[1])))
-    out_part = contract_rows(d_branch_a, att_low).astype(jnp.bfloat16)
-    out_and_gains = scatter_rows(
-        jnp.concatenate([out_part, gain_terms], axis=1)
-    ).astype(jnp.float32)
-    out_grad = out_and_gains[:, :local_width]
     token_own = d_middle + tensor_scatter(contract_cols(d_qkv, w_qkv))
-    qkv_part = contract_rows(inputs, d_qkv)
-    qkv_grad = scatter_rows(qkv_part).astype(jnp.float32)
-    gain_rows = out_and_gains[:, local_width : local_width + 4] + (
-        out_and_gains[:, local_width + 4 : local_width + 8]
-    )
+    qkv_part = contract_rows(inputs, d_qkv).astype(jnp.bfloat16)
+    last_grad = scatter_rows(jnp.concatenate([qkv_part, gain_terms], axis=1)).astype(jnp.float32)
+    qkv_width = 3 * local_width
+    qkv_grad = last_grad[:, :qkv_width]
+    gain_rows = last_grad[:, qkv_width : qkv_width + 4] + last_grad[:, qkv_width + 4 : qkv_width + 8]
     token_low = tensor_gather(token_own.astype(jnp.bfloat16))
     token_grad = token_low.astype(jnp.float32).reshape(seq_count, seq_span, model_width)
     gain_rows, _ = lax.optimization_barrier((gain_rows, token_low))

time: 917 us -> 942 us (1.027)
  waiting for transfers between devices: 373 us -> 335 us
  blocking collectives: 248 us -> 285 us
  starting transfers between devices: 27.7 us -> 41.2 us
  matrix products: 111 us -> 124 us
  local copies, waits for them, and re-layouts: 61.5 us -> 49.1 us
  other arithmetic: 51.3 us -> 61.3 us
    psum x1 -> x0, waiting for transfers between devices: 84.4 us -> none  [tensor_sum(): total = lax.psum(values_in, 'tp')]
    all_to_all x2 -> x4, waiting for transfers between devices: 29.1 us -> 81.2 us  [tensor_scatter(): parts = lax.all_to_all(parts, 'tp', 0, 0, tiled=True)]
    reduce_scatter x4, waiting for transfers between devices: 122 us -> 70.2 us  [scatter_rows(): lax.psum_scatter(values_in, weight_axes, scatter_dimension=0, tiled=True)]
    all_to_all x1 -> x2, waiting for transfers between devices: 0.01 us -> 33.1 us  [to_positions(): parts = lax.all_to_all(parts, 'ctx', 0, 0, tiled=True)]
    all_to_all x1 -> x2, blocking collectives: 51.7 us -> 78.7 us  [tensor_gather(): return lax.all_to_all(parts, 'tp', 0, 0, tiled=True)]
    all_to_all x3 -> x5, waiting for transfers between devices: 99.2 us -> 116 us  [tensor_gather(): return lax.all_to_all(parts, 'tp', 0, 0, tiled=True)]
    all_to_all x2 -> x3, blocking collectives: 98.3 us -> 107 us  [tensor_scatter(): parts = lax.all_to_all(parts, 'tp', 0, 0, tiled=True)]
    dot_general x8 -> x10, matrix products: 72.4 us -> 79.3 us  [dot_f32(): lax.dot_general(left, right, (((left_dim,), (right_dim,)), ((), ())), pre...]
  transfers between devices with their start and end apart: 14 -> 19, of which waited for: 9 -> 13; matrix products, arithmetic and copies ran while one was open for 17% -> 22% of each run, Pallas kernels for 2% -> 2%
where the time goes in v5:
time: 942 us; the launch traced here: 931 us
  waiting for transfers between devices  335 us (36%)
  blocking collectives  285 us (30%)
  matrix products  124 us (13%)
  other arithmetic  61.3 us (7%)
  local copies, waits for them, and re-layouts  49.1 us (5%)
  starting transfers between devices  41.2 us (4%)
  Pallas kernels  21 us (2%)
  between operations  15.4 us (2%)
    all_to_all x5, waiting for transfers between devices, tensor_gather(): return lax.all_to_all(parts, 'tp', 0, 0, tiled=True)  116 us
    all_to_all x3, blocking collectives, tensor_scatter(): parts = lax.all_to_all(parts, 'tp', 0, 0, tiled=True)  107 us
    all_to_all x4, waiting for transfers between devices, tensor_scatter(): parts = lax.all_to_all(parts, 'tp', 0, 0, tiled=True)  81.2 us
    dot_general x10, matrix products, dot_f32(): lax.dot_general(left, right, (((left_dim,), (right_dim,)), ((), ())), pre...  79.3 us
    all_to_all x2, blocking collectives, tensor_gather(): return lax.all_to_all(parts, 'tp', 0, 0, tiled=True)  78.7 us
    reduce_scatter x4, waiting for transfers between devices, scatter_rows(): lax.psum_scatter(values_in, weight_axes, scatter_dimension=0, tiled=True)  70.2 us
    all_to_all x1, blocking collectives, to_heads(): parts = lax.all_to_all(parts, 'ctx', 0, 0, tiled=True)  37.5 us
    all_to_all x2, waiting for transfers between devices, to_positions(): parts = lax.all_to_all(parts, 'ctx', 0, 0, tiled=True)  33.1 us
  transfers between devices with their start and end apart: 19, of which 13 were waited for; matrix products, arithmetic and copies ran while one was open for 22% of the time, Pallas kernels for 2%

profile of v5, /device:TPU:0, one launch (start us, length us, event | category | flops | bytes accessed | tf_op | source)
XLA Modules:
  0.0 931.2 jit_solution(5545440654590535441)
XLA Ops:
  10.3 2.9 pad_maximum_fusion
  13.8 10.4 %all_gather.16 = bf16[2048,4]{0,1:T(4,128)(2,1)S(1)} all-gather(bf16[256,4]{0,1:T(4,128)(2,1)S(1)} %copy-done.44), channel_id=1, replica_groups=mesh['fsdp'=2,'ctx'=4,'tp'=4] {'fsdp','ctx'}, dimensions={0}, use_global_device_ids=true | all-gather | bytes 18432 | tf_op jit(solution)/shard_map/all_gather | solution.py:269
  26.1 32.5 %all-gather.5.cloned.1.call-done = bf16[2048,1536]{1,0:T(8,128)(2,1)} async-done(((bf16[256,1536]{1,0:T(8,128)(2,1)}), bf16[2048,1536]{1,0:T(8,128)(2,1)}) %all-gather.5.cloned.1.call-update) | async-done | bytes 6291472 | tf_op jit(solution)/shard_map/all_gather | solution.py:269
  58.6 6.2 convolution_bitcast_fusion
  66.0 11.7 %all-reduce.2 = (f32[512]{0:T(512)S(1)}, f32[512]{0:T(512)S(1)}) all-reduce(f32[512]{0:T(512)S(1)} %get-tuple-element.65, f32[512]{0:T(512)S(1)} %get-tuple-element.64), channel_id=1, replica_groups=mesh['fsdp'=2,'ctx'=4,'tp'=4] {'tp'}, use_global_device_ids=true, to_apply=%region_1.0 | all-reduce | flops 1024 | bytes 8192 | tf_op jit(solution)/shard_map/psum | solution.py:322
  84.0 2.4 copy.69
  88.4 3.0 add_convert_fusion.2
  91.3 3.0 concatenate.83
  94.4 37.5 %all_to_all.90 = bf16[4,1,1,512,384]{4,3,2,1,0:T(8,128)(2,1)} all-to-all(bf16[4,1,1,512,384]{4,3,2,1,0:T(8,128)(2,1)S(1)} %bitcast.187), channel_id=1, replica_groups=mesh['fsdp'=2,'ctx'=4,'tp'=4] {'ctx'}, dimensions={0} | all-to-all | bytes 3145728 | tf_op jit(solution)/shard_map/all_to_all | solution.py:232
  131.9 9.0 attn_fwd.1
  143.0 3.5 all-to-all-start.1
  146.5 10.3 %all-to-all-done.1 = bf16[4,1,1,512,128]{3,4,2,1,0:T(8,128)(2,1)S(1)} async-done(((bf16[4,1,1,512,128]{3,4,2,1,0:T(8,128)(2,1)}), bf16[4,1,1,512,128]{3,4,2,1,0:T(8,128)(2,1)S(1)}, u32[]{:S(2)}, u32[]{:S(2)}) %all-to-all-start.1) | async-done | bytes 524320 | tf_op jit(solution)/shard_map/all_to_all | solution.py:240
  156.8 3.4 convolution_convert_fusion.5
  161.4 28.4 %all_to_all.91 = bf16[4,64,2048]{2,1,0:T(8,128)(2,1)S(1)} all-to-all(bf16[4,64,2048]{2,1,0:T(8,128)(2,1)S(1)} %get-tuple-element.89), channel_id=1, replica_groups=mesh['fsdp'=2,'ctx'=4,'tp'=4] {'tp'}, dimensions={0} | all-to-all | bytes 2097152 | tf_op jit(solution)/shard_map/all_to_all | solution.py:258
  189.8 3.5 all-to-all-start.2
  193.5 25.1 %all-to-all-done.2 = bf16[4,64,2048]{2,1,0:T(8,128)(2,1)S(1)} async-done(((bf16[4,64,2048]{2,1,0:T(8,128)(2,1)}), bf16[4,64,2048]{2,1,0:T(8,128)(2,1)S(1)}, u32[]{:S(2)}, u32[]{:S(2)}) %all-to-all-start.2) | async-done | bytes 1048608 | tf_op jit(solution)/shard_map/all_to_all | solution.py:258
  219.6 3.5 all-to-all-start.12
  225.7 22.6 %all-to-all-done.12 = bf16[4,256,512]{1,2,0:T(8,128)(2,1)S(1)} async-done(((bf16[4,256,512]{1,2,0:T(8,128)(2,1)}), bf16[4,256,512]{1,2,0:T(8,128)(2,1)S(1)}, u32[]{:S(2)}, u32[]{:S(2)}) %all-to-all-start.12) | async-done | bytes 1048608 | tf_op jit(solution)/shard_map/all_to_all | solution.py:265
  248.5 27.7 %all_to_all.92 = bf16[4,64,2048]{2,1,0:T(8,128)(2,1)S(1)} all-to-all(bf16[4,64,2048]{2,1,0:T(8,128)(2,1)S(1)} %broadcast_in_dim.21), channel_id=1, replica_groups=mesh['fsdp'=2,'ctx'=4,'tp'=4] {'tp'}, dimensions={0} | all-to-all | bytes 2097152 | tf_op jit(solution)/shard_map/all_to_all | solution.py:265
  277.4 3.7 all-to-all-start.7
  281.2 8.1 fusion.7
  291.3 7.1 fusion.29
  298.4 7.4 all-to-all-done.7
  305.8 3.5 all-to-all-start.4
  309.4 8.1 fusion.5
  319.5 7.1 fusion.32
  326.6 8.0 all-to-all-done.4
  334.6 3.5 all-to-all-start.8
  338.3 25.0 %all-to-all-done.8 = bf16[4,64,2048]{2,1,0:T(8,128)(2,1)S(1)} async-done(((bf16[4,64,2048]{2,1,0:T(8,128)(2,1)}), bf16[4,64,2048]{2,1,0:T(8,128)(2,1)S(1)}, u32[]{:S(2)}, u32[]{:S(2)}) %all-to-all-start.8) | async-done | bytes 1048608 | tf_op jit(solution)/shard_map/all_to_all | solution.py:258
  364.7 3.5 all-to-all-start.5
  368.8 2.3 reduce_sum.232
  371.1 22.3 %all-to-all-done.5 = bf16[4,64,2048]{2,1,0:T(8,128)(2,1)S(1)} async-done(((bf16[4,64,2048]{2,1,0:T(8,128)(2,1)}), bf16[4,64,2048]{2,1,0:T(8,128)(2,1)S(1)}, u32[]{:S(2)}, u32[]{:S(2)}) %all-to-all-start.5) | async-done | bytes 1048608 | tf_op jit(solution)/shard_map/all_to_all | solution.py:265
  395.5 4.7 all-to-all-start.9
  403.3 21.8 %all-to-all-done.9 = bf16[4,64,2048]{2,1,0:T(8,128)(2,1)} async-done(((bf16[4,64,2048]{2,1,0:T(8,128)(2,1)}), bf16[4,64,2048]{2,1,0:T(8,128)(2,1)}, u32[]{:S(2)}, u32[]{:S(2)}) %all-to-all-start.9) | async-done | bytes 1048608 | tf_op jit(solution)/shard_map/all_to_all | solution.py:265
  429.4 8.1 multiply_convert_fusion.3
  437.5 11.9 %fusion.3 = bf16[256,2048]{1,0:T(8,128)(2,1)} fusion(bf16[2048,6144]{1,0:T(8,128)(2,1)} %all-gather.9.cloned.1.call-done, bf16[256,2048]{1,0:T(8,128)(2,1)} %get-tuple-element.73, bf16[256,2048]{1,0:T(8,128)(2,1)} %get-tuple-element.72), kind=kOutput, calls=%fused_computation.5 | convolution fusion | flops 4299161600 | bytes 19922944 | tf_op jit(solution)/shard_map/dot_general | solution.py:54
  453.8 7.5 multiply_convert_fusion.1
  461.4 11.0 %fusion.26 = bf16[256,2048]{1,0:T(8,128)(2,1)S(1)} fusion(bf16[2048,6144]{1,0:T(8,128)(2,1)} %all-gather.9.cloned.1.call-done, bf16[256,2048]{1,0:T(8,128)(2,1)} %get-tuple-element.71, bf16[256,2048]{1,0:T(8,128)(2,1)S(1)} %get-tuple-element.70), kind=kOutput, calls=%fused_computation.38 | convolution fusion | flops 4299685888 | bytes 19922944 | tf_op jit(solution)/shard_map/dot_general | solution.py:54
  472.4 28.6 %all_to_all.93 = bf16[4,64,2048]{2,1,0:T(8,128)(2,1)} all-to-all(bf16[4,64,2048]{2,1,0:T(8,128)(2,1)S(1)} %bitcast.205), channel_id=1, replica_groups=mesh['fsdp'=2,'ctx'=4,'tp'=4] {'tp'}, dimensions={0} | all-to-all | bytes 2097152 | tf_op jit(solution)/shard_map/all_to_all | solution.py:258
  500.9 4.3 all-to-all-start.10
  506.9 23.1 %all-to-all-done.10 = bf16[4,64,2048]{2,1,0:T(8,128)(2,1)} async-done(((bf16[4,64,2048]{2,1,0:T(8,128)(2,1)}), bf16[4,64,2048]{2,1,0:T(8,128)(2,1)}, u32[]{:S(2)}, u32[]{:S(2)}) %all-to-all-start.10) | async-done | bytes 1048608 | tf_op jit(solution)/shard_map/all_to_all | solution.py:258
  534.5 6.3 convolution_convert_fusion.6
  541.3 18.9 %all_to_all.94 = bf16[16,128,128]{2,1,0:T(8,128)(2,1)} all-to-all(bf16[16,128,128]{2,1,0:T(8,128)(2,1)S(1)} %bitcast.202), channel_id=1, replica_groups=mesh['fsdp'=2,'ctx'=4,'tp'=4] {'ctx','tp'}, dimensions={0} | all-to-all | bytes 1048576 | tf_op jit(solution)/shard_map/all_to_all | solution.py:250
  560.4 51.0 %all_to_all.95 = bf16[4,128,2048]{2,1,0:T(8,128)(2,1)S(1)} all-to-all(bf16[4,128,2048]{2,1,0:T(8,128)(2,1)S(1)} %broadcast_in_dim.30), channel_id=1, replica_groups=mesh['fsdp'=2,'ctx'=4,'tp'=4] {'tp'}, dimensions={0} | all-to-all | bytes 4194304 | tf_op jit(solution)/shard_map/all_to_all | solution.py:265
  611.3 2.6 convolution_convert_fusion.3
  615.5 8.6 convolution_convert_fusion.1
  624.2 11.9 %attn_bwd.1 = bf16[1,2048,384]{2,1,0:T(8,128)(2,1)} custom-call(bf16[1,2048,384]{2,1,0:T(8,128)(2,1)} %bitcast.178, bf16[1,2048,384]{2,1,0:T(8,128)(2,1)} %bitcast.179, bf16[1,2048,384]{2,1,0:T(8,128)(2,1)} %bitcast.180, bf16[1,2048,128]{2,1,0:T(8,128)(2,1)} %get-tuple-element.16.att_ref, bf16[1,2048,128]{2,1,0:T(8,128)(2,1)} %bitcast.211, ...), custom_call_target="tpu_custom_call" | custom-call | flops 2684354560 | bytes 4718592 | tf_op jit(solution)/shard_map/attn_bwd/pallas_call | solution.py:196
  636.1 3.6 all-to-all-start.14
  639.8 22.8 %all-to-all-done.14 = bf16[4,1,1,512,384]{4,3,2,1,0:T(8,128)(2,1)S(1)} async-done(((bf16[4,1,1,512,384]{4,3,2,1,0:T(8,128)(2,1)}), bf16[4,1,1,512,384]{4,3,2,1,0:T(8,128)(2,1)S(1)}, u32[]{:S(2)}, u32[]{:S(2)}) %all-to-all-start.14) | async-done | bytes 1572896 | tf_op jit(solution)/shard_map/all_to_all | solution.py:240
  668.1 2.8 pad_maximum_fusion.4
  674.7 2.7 fusion.74
  677.4 10.1 %all-reduce.1 = (f32[512]{0:T(512)S(1)}, f32[512]{0:T(512)S(1)}) all-reduce(f32[512]{0:T(512)S(1)} %get-tuple-element.58, f32[512]{0:T(512)S(1)} %get-tuple-element.53), channel_id=1, replica_groups=mesh['fsdp'=2,'ctx'=4,'tp'=4] {'tp'}, use_global_device_ids=true, to_apply=%region_21.22 | all-reduce | flops 1024 | bytes 8192 | tf_op jit(solution)/shard_map/psum | solution.py:432
  690.0 5.5 fusion.10
  695.5 3.7 fusion.9
  700.7 15.0 %convolution_convert_fusion = bf16[2048,4096]{1,0:T(8,128)(2,1)} fusion(bf16[256,2048]{1,0:T(8,128)(2,1)} %get-tuple-element.71, bf16[256,2048]{1,0:T(8,128)(2,1)} %copy-done.45, bf16[256,2048]{1,0:T(8,128)(2,1)} %get-tuple-element.73, bf16[256,2048]{1,0:T(8,128)(2,1)} %get-tuple-element.72, bf16[256,2048]{1,0:T(8,128)(2,1)S(1)} %bitcast.189, ...), kind=kOutput, calls=%fused_computation | convolution fusion | flops 8619294720 | bytes 23068672 | tf_op jit(solution)/shard_map/dot_general | solution.py:54
  717.1 7.1 convolution_convert_fusion.4
  724.2 50.0 %all_to_all.96 = bf16[4,128,2048]{2,1,0:T(8,128)(2,1)S(1)} all-to-all(bf16[4,128,2048]{2,1,0:T(8,128)(2,1)S(1)} %bitcast.197), channel_id=1, replica_groups=mesh['fsdp'=2,'ctx'=4,'tp'=4] {'tp'}, dimensions={0} | all-to-all | bytes 4194304 | tf_op jit(solution)/shard_map/all_to_all | solution.py:258
  778.2 3.6 all-to-all-start.16
  787.1 42.0 %all-to-all-done.16 = bf16[4,128,2048]{2,1,0:T(8,128)(2,1)S(1)} async-done(((bf16[4,128,2048]{2,1,0:T(8,128)(2,1)}), bf16[4,128,2048]{2,1,0:T(8,128)(2,1)S(1)}, u32[]{:S(2)}, u32[]{:S(2)}) %all-to-all-start.16) | async-done | bytes 2097184 | tf_op jit(solution)/shard_map/all_to_all | solution.py:265
  829.1 2.5 bitcast_convert_fusion
  831.6 2.8 convert_element_type.286
  839.0 10.6 %psum.39 = f32[256,4]{0,1:T(4,128)} all-reduce(f32[256,4]{0,1:T(4,128)S(1)} %slice_add_fusion), channel_id=1, replica_groups=mesh['fsdp'=2,'ctx'=4,'tp'=4] {'tp'}, use_global_device_ids=true, to_apply=%region_32.33 | all-reduce | flops 1024 | bytes 8192 | tf_op jit(solution)/shard_map/psum | solution.py:457
  849.6 70.2 %reduce-scatter.9.cloned.1.call-done = bf16[256,4096]{1,0:T(8,128)(2,1)} async-done(((bf16[2048,4096]{1,0:T(8,128)(2,1)}), bf16[256,4096]{1,0:T(8,128)(2,1)}) %reduce-scatter.9.cloned.1.call-update) | async-done | bytes 2097168 | tf_op jit(solution)/shard_map/reduce_scatter | solution.py:274
  919.9 4.1 fusion.93
  (196 shorter events, 80.1 us)
Async XLA Ops:
  7.2 3.1 copy-start.33
  7.2 3.1 copy-start.32
  7.2 51.4 %all-gather.5.cloned.1.call-start = ((), (), s32[]{:S(2)}) async-start(), calls=%async_computation.22 | async-start | bytes 7077888 | tf_op jit(solution)/shard_map/all_gather | solution.py:269
  9.4 137.1 %all-gather.7.cloned.1.call-start = ((), (), s32[]{:S(2)}) async-start(), calls=%async_computation.23 | async-start | bytes 2359296 | tf_op jit(solution)/shard_map/all_gather | solution.py:269
  10.2 271.0 %all-gather.9.cloned.1.call-start = ((), (), s32[]{:S(2)}) async-start(), calls=%async_computation.24 | async-start | bytes 28311552 | tf_op jit(solution)/shard_map/all_gather | solution.py:269
  64.9 14.0 %copy-start = (f32[512,1536]{0,1:T(8,128)}, f32[512,1536]{0,1:T(8,128)S(1)}, u32[]{:S(2)}) copy-start(f32[512,1536]{0,1:T(8,128)S(1)} %convolution_bitcast_fusion) | copy-start | bytes 9437188
  79.8 1.7 copy-start.24
  143.0 13.8 %all-to-all-start.1 = ((bf16[4,1,1,512,128]{3,4,2,1,0:T(8,128)(2,1)}), bf16[4,1,1,512,128]{3,4,2,1,0:T(8,128)(2,1)S(1)}, u32[]{:S(2)}, u32[]{:S(2)}) async-start(bf16[4,1,1,512,128]{3,4,2,1,0:T(8,128)(2,1)} %copy.53), calls=%async_computation.1 | async-start | bytes 1048576 | tf_op jit(solution)/shard_map/all_to_all | solution.py:240
  156.8 3.4 copy-start.39
  161.4 31.9 %copy-start.30 = (bf16[256,512]{1,0:T(8,128)(2,1)S(1)}, bf16[256,512]{1,0:T(8,128)(2,1)}, u32[]{:S(2)}) copy-start(bf16[256,512]{1,0:T(8,128)(2,1)} %param.14) | copy-start | bytes 786436
  189.8 28.8 %all-to-all-start.2 = ((bf16[4,64,2048]{2,1,0:T(8,128)(2,1)}), bf16[4,64,2048]{2,1,0:T(8,128)(2,1)S(1)}, u32[]{:S(2)}, u32[]{:S(2)}) async-start(bf16[4,64,2048]{2,1,0:T(8,128)(2,1)} %get-tuple-element.88), calls=%async_computation.2 | async-start | bytes 2097152 | tf_op jit(solution)/shard_map/all_to_all | solution.py:258
  219.6 28.8 %all-to-all-start.12 = ((bf16[4,256,512]{1,2,0:T(8,128)(2,1)}), bf16[4,256,512]{1,2,0:T(8,128)(2,1)S(1)}, u32[]{:S(2)}, u32[]{:S(2)}) async-start(bf16[4,256,512]{1,2,0:T(8,128)(2,1)} %broadcast_in_dim.25), calls=%async_computation.12 | async-start | bytes 2097152 | tf_op jit(solution)/shard_map/all_to_all | solution.py:265
  224.4 0.8 copy-start.1
  224.7 0.8 copy-start.3
  248.4 29.0 %copy-start.20 = (bf16[4,256,512]{1,2,0:T(8,128)(2,1)}, bf16[4,256,512]{1,2,0:T(8,128)(2,1)S(1)}, u32[]{:S(2)}) copy-start(bf16[4,256,512]{1,2,0:T(8,128)(2,1)S(1)} %all-to-all-done.12) | copy-start | bytes 3145732
  276.2 13.1 %copy-start.22 = (bf16[4,64,2048]{2,1,0:T(8,128)(2,1)}, bf16[4,64,2048]{2,1,0:T(8,128)(2,1)S(1)}, u32[]{:S(2)}) copy-start(bf16[4,64,2048]{2,1,0:T(8,128)(2,1)S(1)} %all_to_all.92) | copy-start | bytes 3145732
  277.4 28.4 %all-to-all-start.7 = ((bf16[4,64,2048]{2,1,0:T(8,128)(2,1)}), bf16[4,64,2048]{2,1,0:T(8,128)(2,1)S(1)}, u32[]{:S(2)}, u32[]{:S(2)}) async-start(bf16[4,64,2048]{2,1,0:T(8,128)(2,1)} %broadcast_in_dim.23), calls=%async_computation.7 | async-start | bytes 2097152 | tf_op jit(solution)/shard_map/all_to_all | solution.py:265
  289.3 2.0 copy-start.14
  291.3 7.1 copy-start.25
  305.8 11.7 %copy-start.16 = (bf16[4,64,2048]{2,1,0:T(8,128)(2,1)}, bf16[4,64,2048]{2,1,0:T(8,128)(2,1)S(1)}, u32[]{:S(2)}) copy-start(bf16[4,64,2048]{2,1,0:T(8,128)(2,1)S(1)} %all-to-all-done.7) | copy-start | bytes 3145732
  305.8 28.8 %all-to-all-start.4 = ((bf16[4,64,2048]{2,1,0:T(8,128)(2,1)}), bf16[4,64,2048]{2,1,0:T(8,128)(2,1)S(1)}, u32[]{:S(2)}, u32[]{:S(2)}) async-start(bf16[4,64,2048]{2,1,0:T(8,128)(2,1)} %bitcast.19), calls=%async_computation.4 | async-start | bytes 2097152 | tf_op jit(solution)/shard_map/all_to_all | solution.py:258
  317.5 2.0 copy-start.12
  319.5 7.1 copy-start.27
  334.6 28.8 %all-to-all-start.8 = ((bf16[4,64,2048]{2,1,0:T(8,128)(2,1)}), bf16[4,64,2048]{2,1,0:T(8,128)(2,1)S(1)}, u32[]{:S(2)}, u32[]{:S(2)}) async-start(bf16[4,64,2048]{2,1,0:T(8,128)(2,1)} %bitcast.204), calls=%async_computation.8 | async-start | bytes 2097152 | tf_op jit(solution)/shard_map/all_to_all | solution.py:258
  363.4 1.3 copy-start.21
  364.7 28.8 %all-to-all-start.5 = ((bf16[4,64,2048]{2,1,0:T(8,128)(2,1)}), bf16[4,64,2048]{2,1,0:T(8,128)(2,1)S(1)}, u32[]{:S(2)}, u32[]{:S(2)}) async-start(bf16[4,64,2048]{2,1,0:T(8,128)(2,1)} %broadcast_in_dim.22), calls=%async_computation.5 | async-start | bytes 2097152 | tf_op jit(solution)/shard_map/all_to_all | solution.py:265
  368.2 166.2 %all-gather.11.cloned.1.call-start = ((), (), s32[]{:S(2)}) async-start(), calls=%async_computation.25 | async-start | bytes 9437184 | tf_op jit(solution)/shard_map/all_gather | solution.py:269
  368.8 31.4 %copy-start.5 = (bf16[1,512,2048]{2,1,0:T(8,128)(2,1)S(1)}, bf16[1,512,2048]{2,1,0:T(8,128)(2,1)}, u32[]{:S(2)}) copy-start(bf16[1,512,2048]{2,1,0:T(8,128)(2,1)} %param.19) | copy-start | bytes 6291460
  395.5 29.6 %all-to-all-start.9 = ((bf16[4,64,2048]{2,1,0:T(8,128)(2,1)}), bf16[4,64,2048]{2,1,0:T(8,128)(2,1)}, u32[]{:S(2)}, u32[]{:S(2)}) async-start(bf16[4,64,2048]{2,1,0:T(8,128)(2,1)} %broadcast_in_dim.24), calls=%async_computation.9 | async-start | bytes 2097152 | tf_op jit(solution)/shard_map/all_to_all | solution.py:265
  426.6 2.8 copy-start.15
  429.4 8.1 copy-start.34
  449.4 1.2 copy-start.6
  449.6 1.6 copy-start.17
  451.3 2.6 copy-start.13
  453.1 8.3 copy-start.29
  461.4 11.0 %copy-start.45 = (bf16[256,2048]{1,0:T(8,128)(2,1)}, bf16[256,2048]{1,0:T(8,128)(2,1)S(1)}, u32[]{:S(2)}) copy-start(bf16[256,2048]{1,0:T(8,128)(2,1)S(1)} %get-tuple-element.70) | copy-start | bytes 3145732
  472.4 32.9 %copy-start.2 = (f32[64,2048]{1,0:T(8,128)S(1)}, f32[64,2048]{1,0:T(8,128)}, u32[]{:S(2)}) copy-start(f32[64,2048]{1,0:T(8,128)} %copy-done.1) | copy-start | bytes 1572868
  472.4 32.9 %copy-start.4 = (f32[64,2048]{1,0:T(8,128)S(1)}, f32[64,2048]{1,0:T(8,128)}, u32[]{:S(2)}) copy-start(f32[64,2048]{1,0:T(8,128)} %copy-done.3) | copy-start | bytes 1572868
  500.9 29.1 %all-to-all-start.10 = ((bf16[4,64,2048]{2,1,0:T(8,128)(2,1)}), bf16[4,64,2048]{2,1,0:T(8,128)(2,1)}, u32[]{:S(2)}, u32[]{:S(2)}) async-start(bf16[4,64,2048]{2,1,0:T(8,128)(2,1)} %bitcast.33), calls=%async_computation.10 | async-start | bytes 2097152 | tf_op jit(solution)/shard_map/all_to_all | solution.py:258
  505.2 280.1 %reduce-scatter.7.cloned.1.call-start = ((), (), s32[]{:S(2)}) async-start(), calls=%async_computation.27 | async-start | bytes 2359296 | tf_op jit(solution)/shard_map/reduce_scatter | solution.py:274
  506.9 26.2 %copy-start.7 = (f32[64,2048]{1,0:T(8,128)}, f32[64,2048]{1,0:T(8,128)S(1)}, u32[]{:S(2)}) copy-start(f32[64,2048]{1,0:T(8,128)S(1)} %convert_reduce_fusion.1) | copy-start | bytes 1572868
  531.4 1.6 copy-start.9
  560.4 51.0 %copy-start.40 = (bf16[4,1,1,512,128]{3,4,2,1,0:T(8,128)(2,1)S(1)}, bf16[4,1,1,512,128]{3,4,2,1,0:T(8,128)(2,1)}, u32[]{:S(2)}) copy-start(bf16[4,1,1,512,128]{3,4,2,1,0:T(8,128)(2,1)} %copy-done.39) | copy-start | bytes 1572868
  614.0 1.2 copy-start.26
  614.0 1.5 copy-start.28
  614.0 217.6 %reduce-scatter.11.cloned.1.call-start = ((), (), s32[]{:S(2)}) async-start(), calls=%async_computation.29 | async-start | bytes 9437184 | tf_op jit(solution)/shard_map/reduce_scatter | solution.py:274
  636.1 26.4 %all-to-all-start.14 = ((bf16[4,1,1,512,384]{4,3,2,1,0:T(8,128)(2,1)}), bf16[4,1,1,512,384]{4,3,2,1,0:T(8,128)(2,1)S(1)}, u32[]{:S(2)}, u32[]{:S(2)}) async-start(bf16[4,1,1,512,384]{4,3,2,1,0:T(8,128)(2,1)} %bitcast.203), calls=%async_computation.14 | async-start | bytes 3145728 | tf_op jit(solution)/shard_map/all_to_all | solution.py:240
  639.7 194.8 %reduce-scatter.5.cloned.1.call-start = ((), (), s32[]{:S(2)}) async-start(), calls=%async_computation.26 | async-start | bytes 7667712 | tf_op jit(solution)/shard_map/reduce_scatter | solution.py:274
  662.5 1.0 copy-start.31
  687.6 2.3 copy-start.41
  687.6 2.4 copy-start.43
  689.9 5.6 copy-start.35
  689.9 5.6 copy-start.37
  699.2 1.2 copy-start.18
  699.2 1.5 copy-start.23
  699.2 220.6 %reduce-scatter.9.cloned.1.call-start = ((), (), s32[]{:S(2)}) async-start(), calls=%async_computation.28 | async-start | bytes 18874368 | tf_op jit(solution)/shard_map/reduce_scatter | solution.py:274
  715.7 1.0 copy-start.36
  715.7 1.2 copy-start.38
  715.7 1.4 copy-start.42
  774.2 1.0 copy-start.8
  774.2 1.2 copy-start.10
  778.2 50.8 %all-to-all-start.16 = ((bf16[4,128,2048]{2,1,0:T(8,128)(2,1)}), bf16[4,128,2048]{2,1,0:T(8,128)(2,1)S(1)}, u32[]{:S(2)}, u32[]{:S(2)}) async-start(bf16[4,128,2048]{2,1,0:T(8,128)(2,1)} %broadcast_in_dim.27), calls=%async_computation.16 | async-start | bytes 4194304 | tf_op jit(solution)/shard_map/all_to_all | solution.py:265
  781.9 1.9 copy-start.19
  834.5 1.4 copy-start.11
  (1 other events, 0.7 us)
Sparse Core Ops, SparseCore 0:
  10.5 48.1 all-gather.4
  60.5 27.7 all-gather.6
  90.8 139.8 all-gather.8
  370.6 56.1 all-gather.10
  614.1 43.5 reduce-scatter.6
  661.0 71.5 reduce-scatter.10
  736.0 64.0 reduce-scatter.4
  803.6 116.1 reduce-scatter.8
